TPU v7x, 32 devices: a whole 2x2x4 slice. The times are simulated.
32 devices in a mesh: dp: 4 (over x, core), expert: 8 (over z, y).
Axes of the slice: x: 2, y: 2, z: 4, core: 2. Of those that a mesh axis runs over, the one named last changes fastest.
Arguments:
- hidden_in: bfloat16 [32, 512, 1024], P(('dp', 'expert')), may hold values from -6 to 6
- segment_ids: int32 [32, 512], P(('dp', 'expert')), may hold values from 0 to 15, never falling along the last dimension, each value on 1 to 256 neighbouring positions
- head_experts: int32 [32, 512, 4, 2], P(('dp', 'expert')), may hold values from 0 to 4, all different within a row
- token_experts: int32 [32, 512, 16], P(('dp', 'expert')), may hold values from 0 to 95, all different within a row; in each aligned block of 512 rows (0 to 511, 512 to 1023, ..., all dimensions but the last counted through in order) at most 96 rows name the same one
- attention_gain: float32 [1024], replicated, may hold values from 0.5 to 1.5
- query_weight: bfloat16 [1024, 512], replicated, may hold values from -0.1875 to 0.1875
- key_weight: bfloat16 [1024, 512], replicated, may hold values from -0.1875 to 0.1875
- value_weight: bfloat16 [1024, 2560], replicated, may hold values from -0.1875 to 0.1875
- value_selector: bfloat16 [1024, 20], replicated, may hold values from -0.09375 to 0.09375
- output_selector: bfloat16 [1024, 20], replicated, may hold values from -0.09375 to 0.09375
- output_weight: bfloat16 [2560, 1024], replicated, may hold values from -1.5 to 1.5
- mixture_gain: float32 [1024], replicated, may hold values from 0.5 to 1.5
- router_weight: bfloat16 [1024, 96], replicated, may hold values from -0.09375 to 0.09375
- up_weight: bfloat16 [96, 1024, 128], P(('dp', 'expert')), may hold values from -0.1875 to 0.1875
- down_weight: bfloat16 [96, 128, 1024], P(('dp', 'expert')), may hold values from -0.375 to 0.375
- expert_counts: int32 [96], replicated, may hold values from 0 to 999
- output_cotangent: bfloat16 [32, 512, 1024], P(('dp', 'expert')), may hold values from -6 to 6
Outputs:
- hidden_out: bfloat16 [32, 512, 1024], P(('dp', 'expert'))
- grad_input: float32 [32, 512, 1024], P(('dp', 'expert'))
- grad_attention_gain: float32 [1024], replicated
- grad_query_weight: float32 [1024, 512], replicated
- grad_key_weight: float32 [1024, 512], replicated
- grad_value_weight: float32 [1024, 2560], replicated
- grad_value_selector: float32 [1024, 20], replicated
- grad_output_selector: float32 [1024, 20], replicated
- grad_output_weight: float32 [2560, 1024], replicated
- grad_mixture_gain: float32 [1024], replicated
- grad_router_weight: float32 [1024, 96], replicated
- grad_up_weight: float32 [96, 1024, 128], P(('dp', 'expert'))
- grad_down_weight: float32 [96, 128, 1024], P(('dp', 'expert'))
- new_counts: int32 [96], replicated
Inputs may be any that keep to these rules, and one draw needn't show every extreme that they name: `token_experts`: each token names 16 different experts; the 512 tokens of one row (one device) name no expert more than 96 times, a bound that some block reaches. `segment_ids`: within a row the numbers never fall; each of the 16 documents covers 1 to 256 tokens, one exactly 256. `head_experts`: the 2 experts of a token's head differ.
All inputs are finite; a program needn't handle non-finite values.
Results may differ from a plain program's by a relative error of at most 0.012.
Values may be sent and summed in bfloat16 or wider, within the bound.
No kernel may reach another device: no remote copies, remote signals or barrier semaphores. Data moves between devices by JAX's collectives and lax.ppermute only.
A program may use at most 320 MiB of HBM per device.

v0:
```python
import jax
import jax.numpy as jnp
from jax import lax
from jax.sharding import PartitionSpec as P

D = 1024
H = 4
DH = 128
NE = 5
TOPK = 16


epsilon = 1e-06
masked_value = -1e30


def inverse_rms(values):
    return lax.rsqrt(jnp.mean(values * values, axis=-1, keepdims=True) + epsilon)


def norm_back(values, scaling, gain, upstream):
    weighted = upstream * gain
    middle = jnp.mean(values * weighted, axis=-1, keepdims=True)
    return scaling * weighted - values * scaling * scaling * scaling * middle


def masked_scores(query_low, key_low, allowed):
    raw = jnp.einsum(
        "qhd,khd->hqk", query_low, key_low, preferred_element_type=jnp.float32
    ) * DH ** (-0.5)
    return jnp.where(allowed[None], raw, masked_value)


def weight_grad(left, right):
    return jnp.einsum("td,tc->dc", left, right, preferred_element_type=jnp.float32)


def input_term(delta, weight):
    return jnp.einsum("tc,dc->td", delta, weight, preferred_element_type=jnp.float32)


def smooth_gate(values):
    return jax.nn.gelu(values, approximate=True)


def on_device(
    hidden_in,
    segment_ids,
    head_experts,
    token_experts,
    attention_gain,
    query_weight,
    key_weight,
    value_weight,
    value_selector,
    output_selector,
    output_weight,
    mixture_gain,
    router_weight,
    up_weight,
    down_weight,
    expert_counts,
    output_cotangent,
):
    length = hidden_in.shape[1]
    devices = lax.axis_size(("dp", "expert"))
    experts = router_weight.shape[1]
    local_experts = up_weight.shape[0]
    slot_depth = max(4, 9 * length * TOPK // (8 * experts))
    inputs = hidden_in[0].astype(jnp.float32)
    att_rms = inverse_rms(inputs)
    normed_low = (inputs * att_rms * attention_gain).astype(jnp.bfloat16)
    query_low = (
        jnp.dot(normed_low, query_weight, preferred_element_type=jnp.float32)
        .astype(jnp.bfloat16)
        .reshape(length, H, DH)
    )
    key_low = (
        jnp.dot(normed_low, key_weight, preferred_element_type=jnp.float32)
        .astype(jnp.bfloat16)
        .reshape(length, H, DH)
    )
    values_all = jnp.dot(normed_low, value_weight, preferred_element_type=jnp.float32).reshape(
        length, H, NE, DH
    )
    value_sigmoid = jax.nn.sigmoid(
        jnp.dot(normed_low, value_selector, preferred_element_type=jnp.float32)
    ).reshape(length, H, NE)
    output_sigmoid = jax.nn.sigmoid(
        jnp.dot(normed_low, output_selector, preferred_element_type=jnp.float32)
    ).reshape(length, H, NE)
    chosen_mask = jnp.sum(
        (head_experts[0][:, :, :, None] == jnp.arange(NE, dtype=jnp.int32)).astype(jnp.float32),
        axis=2,
    )
    value_gate = value_sigmoid * chosen_mask
    output_gate = output_sigmoid * chosen_mask
    value_low = jnp.sum(value_gate[..., None] * values_all, axis=2).astype(jnp.bfloat16)
    positions = jnp.arange(length, dtype=jnp.int32)
    segments = segment_ids[0]
    allowed = (positions[None, :] <= positions[:, None]) & (segments[None, :] == segments[:, None])
    scores = masked_scores(query_low, key_low, allowed)
    log_total = jax.nn.logsumexp(scores, axis=-1, keepdims=True)
    probs_low = jnp.exp(scores - log_total).astype(jnp.bfloat16)
    mixed_heads = jnp.einsum(
        "hqk,khd->qhd", probs_low, value_low, preferred_element_type=jnp.float32
    )
    spread_low = (
        (output_gate[..., None] * mixed_heads[:, :, None, :])
        .astype(jnp.bfloat16)
        .reshape(length, H * NE * DH)
    )
    middle_rows = inputs + jnp.dot(spread_low, output_weight, preferred_element_type=jnp.float32)
    moe_rms = inverse_rms(middle_rows)
    moe_low = (middle_rows * moe_rms * mixture_gain).astype(jnp.bfloat16)
    logits = jnp.dot(moe_low, router_weight, preferred_element_type=jnp.float32)
    chosen = token_experts[0]
    gate_values = jax.nn.sigmoid(jnp.take_along_axis(logits, chosen, axis=1))
    pair_ids = chosen.reshape(-1)
    expert_range = jnp.arange(experts, dtype=jnp.int32)
    one_hot = (pair_ids[:, None] == expert_range[None, :]).astype(jnp.int32)
    rank_in = jnp.sum(
        (jnp.cumsum(one_hot, axis=0, dtype=jnp.int32) - one_hot) * one_hot, axis=1, dtype=jnp.int32
    )
    local_counts = jnp.sum(one_hot, axis=0, dtype=jnp.int32)
    send_slot = (
        pair_ids % local_experts * (devices * slot_depth)
        + pair_ids // local_experts * slot_depth
        + rank_in
    )
    pair_count = length * TOPK
    slot_pair = (
        jnp.full((local_experts * devices * slot_depth,), pair_count, jnp.int32)
        .at[send_slot]
        .set(jnp.arange(pair_count, dtype=jnp.int32))
    )
    slot_token = slot_pair // TOPK
    padded_rows = jnp.concatenate([moe_low, jnp.zeros((1, D), jnp.bfloat16)], axis=0)
    outgoing = padded_rows[slot_token].reshape(local_experts, devices, slot_depth, D)
    arriving = lax.all_to_all(outgoing, ("dp", "expert"), split_axis=1, concat_axis=1, tiled=True)
    arriving = arriving.reshape(local_experts, devices * slot_depth, D)
    pre_act = jnp.einsum("emd,edf->emf", arriving, up_weight, preferred_element_type=jnp.float32)
    hidden_low = smooth_gate(pre_act).astype(jnp.bfloat16)
    produced = jnp.einsum(
        "emf,efd->emd", hidden_low, down_weight, preferred_element_type=jnp.float32
    ).astype(jnp.bfloat16)
    returned = lax.all_to_all(
        produced.reshape(local_experts, devices, slot_depth, D),
        ("dp", "expert"),
        split_axis=1,
        concat_axis=1,
        tiled=True,
    )
    picked = (
        returned.reshape(local_experts * devices * slot_depth, D)[send_slot]
        .reshape(length, TOPK, D)
        .astype(jnp.float32)
    )
    output_rows = middle_rows + jnp.sum(gate_values[:, :, None] * picked, axis=1)
    upstream = output_cotangent[0].astype(jnp.float32)
    gate_delta = jnp.sum(upstream[:, None, :] * picked, axis=2) * gate_values * (1.0 - gate_values)
    logit_delta = jnp.sum(
        (chosen[:, :, None] == expert_range[None, None, :]).astype(jnp.float32)
        * gate_delta[:, :, None],
        axis=1,
    ).astype(jnp.bfloat16)
    grad_router = jnp.einsum("td,te->de", moe_low, logit_delta, preferred_element_type=jnp.float32)
    slot_gate = jnp.concatenate([gate_values.reshape(-1), jnp.zeros((1,), jnp.float32)])[slot_pair]
    upstream_padded = jnp.concatenate([upstream, jnp.zeros((1, D), jnp.float32)], axis=0)
    grad_send = (
        (upstream_padded[slot_token] * slot_gate[:, None])
        .astype(jnp.bfloat16)
        .reshape(local_experts, devices, slot_depth, D)
    )
    grad_rows = lax.all_to_all(grad_send, ("dp", "expert"), split_axis=1, concat_axis=1, tiled=True)
    grad_rows = grad_rows.reshape(local_experts, devices * slot_depth, D)
    hidden_grad = jnp.einsum(
        "emd,efd->emf", grad_rows, down_weight, preferred_element_type=jnp.float32
    )
    gate_pullback = jax.vjp(smooth_gate, pre_act)[1]
    hidden_delta = gate_pullback(hidden_grad)[0].astype(jnp.bfloat16)
    grad_down = jnp.einsum(
        "emf,emd->efd", hidden_low, grad_rows, preferred_element_type=jnp.float32
    )
    grad_up = jnp.einsum("emd,emf->edf", arriving, hidden_delta, preferred_element_type=jnp.float32)
    rows_delta = jnp.einsum(
        "emf,edf->emd", hidden_delta, up_weight, preferred_element_type=jnp.float32
    ).astype(jnp.bfloat16)
    came_back = lax.all_to_all(
        rows_delta.reshape(local_experts, devices, slot_depth, D),
        ("dp", "expert"),
        split_axis=1,
        concat_axis=1,
        tiled=True,
    )
    expert_delta = jnp.sum(
        came_back.reshape(local_experts * devices * slot_depth, D)[send_slot]
        .reshape(length, TOPK, D)
        .astype(jnp.float32),
        axis=1,
    )
    expert_delta = expert_delta + jnp.einsum(
        "te,de->td", logit_delta, router_weight, preferred_element_type=jnp.float32
    )
    middle_delta = upstream + norm_back(middle_rows, moe_rms, mixture_gain, expert_delta)
    grad_mixture = jnp.sum(expert_delta * middle_rows * moe_rms, axis=0)
    middle_low = middle_delta.astype(jnp.bfloat16)
    grad_output = jnp.einsum(
        "tc,td->cd", spread_low, middle_low, preferred_element_type=jnp.float32
    )
    spread_delta = jnp.einsum(
        "td,cd->tc", middle_low, output_weight, preferred_element_type=jnp.float32
    ).reshape(length, H, NE, DH)
    mixed_delta = jnp.sum(output_gate[..., None] * spread_delta, axis=2).astype(jnp.bfloat16)
    oselect_delta = (
        (
            jnp.sum(spread_delta * mixed_heads[:, :, None, :], axis=3)
            * chosen_mask
            * output_sigmoid
            * (1.0 - output_sigmoid)
        )
        .astype(jnp.bfloat16)
        .reshape(length, H * NE)
    )
    scores = masked_scores(query_low, key_low, allowed)
    probs_full = jnp.exp(scores - log_total)
    probs_again = probs_full.astype(jnp.bfloat16)
    weight_delta = jnp.einsum(
        "qhd,khd->hqk", mixed_delta, value_low, preferred_element_type=jnp.float32
    )
    score_delta = (
        probs_full * (weight_delta - jnp.sum(probs_full * weight_delta, axis=-1, keepdims=True))
    ).astype(jnp.bfloat16)
    query_delta = (
        (
            jnp.einsum("hqk,khd->qhd", score_delta, key_low, preferred_element_type=jnp.float32)
            * DH ** (-0.5)
        )
        .astype(jnp.bfloat16)
        .reshape(length, H * DH)
    )
    key_delta = (
        (
            jnp.einsum("hqk,qhd->khd", score_delta, query_low, preferred_element_type=jnp.float32)
            * DH ** (-0.5)
        )
        .astype(jnp.bfloat16)
        .reshape(length, H * DH)
    )
    value_delta = jnp.einsum(
        "hqk,qhd->khd", probs_again, mixed_delta, preferred_element_type=jnp.float32
    )
    values_delta = (
        (value_gate[..., None] * value_delta[:, :, None, :])
        .astype(jnp.bfloat16)
        .reshape(length, H * NE * DH)
    )
    vselect_delta = (
        (
            jnp.sum(value_delta[:, :, None, :] * values_all, axis=3)
            * chosen_mask
            * value_sigmoid
            * (1.0 - value_sigmoid)
        )
        .astype(jnp.bfloat16)
        .reshape(length, H * NE)
    )
    grad_query = weight_grad(normed_low, query_delta)
    grad_key = weight_grad(normed_low, key_delta)
    grad_value = weight_grad(normed_low, values_delta)
    grad_vselect = weight_grad(normed_low, vselect_delta)
    grad_oselect = weight_grad(normed_low, oselect_delta)
    normed_delta = (
        input_term(query_delta, query_weight)
        + input_term(key_delta, key_weight)
        + input_term(values_delta, value_weight)
    )
    normed_delta = (
        normed_delta
        + input_term(vselect_delta, value_selector)
        + input_term(oselect_delta, output_selector)
    )
    input_delta = middle_delta + norm_back(inputs, att_rms, attention_gain, normed_delta)
    grad_attention = jnp.sum(normed_delta * inputs * att_rms, axis=0)
    summed = lax.psum(
        (
            grad_attention,
            grad_query,
            grad_key,
            grad_value,
            grad_vselect,
            grad_oselect,
            grad_output,
            grad_mixture,
            grad_router,
            local_counts.astype(jnp.float32),
        ),
        ("dp", "expert"),
    )
    new_counts = expert_counts + summed[9].astype(jnp.int32)
    return (
        output_rows.astype(jnp.bfloat16)[None],
        input_delta[None],
        summed[0],
        summed[1],
        summed[2],
        summed[3],
        summed[4],
        summed[5],
        summed[6],
        summed[7],
        summed[8],
        grad_up,
        grad_down,
        new_counts,
    )


def solution(mesh):
    placed = (
        P(("dp", "expert"), None, None),
        P(("dp", "expert"), None),
        P(("dp", "expert"), None, None, None),
        P(("dp", "expert"), None, None),
        P(),
        P(),
        P(),
        P(),
        P(),
        P(),
        P(),
        P(),
        P(),
        P(("dp", "expert"), None, None),
        P(("dp", "expert"), None, None),
        P(),
        P(("dp", "expert"), None, None),
    )
    return jax.shard_map(
        on_device,
        mesh=mesh,
        in_specs=placed,
        out_specs=(
            P(("dp", "expert"), None, None),
            P(("dp", "expert"), None, None),
            P(),
            P(),
            P(),
            P(),
            P(),
            P(),
            P(),
            P(),
            P(),
            P(("dp", "expert"), None, None),
            P(("dp", "expert"), None, None),
            P(),
        ),
        check_vma=False,
    )
```

profile of v0, /device:TPU:0, one launch (start us, length us, event | category | flops | bytes accessed | tf_op | source)
XLA Modules:
  0.0 2664.6 jit_solution(8840407814624057356)
XLA Ops:
  32.0 54.4 %reduce-window.6 = s32[96,64,128]{2,1,0:T(8,128)} reduce-window(s32[96,64,128]{2,1,0:T(8,128)} %fusion.13, s32[]{:T(128)} %constant.47.clone.1), window={size=1x1x128 pad=0_0x0_0x127_0}, to_apply=%region_6.7 | reduce-window | flops 99876864 | bytes 6291460 | tf_op jit(solution)/shard_map/reduce-window
  102.4 31.4 %scatter_custom_fusion = s32[9216]{0:T(1024)} fusion(s32[8192]{0:T(1024)S(1)} %bitcast.216, s32[8192]{0:T(1024)} %iota.32, s32[]{:T(128)} %constant.90.clone.1), kind=kCustom, calls=%fused_computation.156 | custom fusion | bytes 37376 | tf_op jit(solution)/shard_map/scatter | solution.py:135
  139.2 8.0 copy.256
  166.0 65.5 %gather_fusion.5 = f32[8192]{0:T(1024)S(1)} fusion(f32[512,96]{0,1:T(8,128)S(1)} %fusion.83, s32[8192]{0:T(1024)S(1)} %reshape.525), kind=kCustom, calls=%fused_computation.5 | custom fusion | bytes 131072 | tf_op jit(solution)/shard_map/jit(take_along_axis)/gather | solution.py:118
  231.7 51.2 %gather_fusion.3 = f32[9216]{0:T(1024)S(1)} fusion(f32[8193]{0:T(1024)S(1)} %pad_maximum_fusion, s32[9216]{0:T(1024)S(1)} %copy-done.59), kind=kCustom, calls=%fused_computation.3 | custom fusion | bytes 110592 | tf_op jit(solution)/shard_map/gather | solution.py:168
  284.7 40.4 %gather_fusion.2 = f32[9216,1024]{1,0:T(8,128)} fusion(f32[513,1024]{1,0:T(8,128)S(1)} %concatenate.10, s32[9216]{0:T(1024)S(1)} %get-tuple-element.43), kind=kCustom, calls=%fused_computation.2 | custom fusion | bytes 75534336 | tf_op jit(solution)/shard_map/gather | solution.py:171
  325.1 20.6 fusion
  353.3 39.8 %gather_fusion = bf16[9216,1024]{1,0:T(8,128)(2,1)} fusion(bf16[513,1024]{1,0:T(8,128)(2,1)S(1)} %concatenate.9, s32[9216]{0:T(1024)S(1)} %get-tuple-element.43), kind=kCustom, calls=%fused_computation | custom fusion | bytes 37785600 | tf_op jit(solution)/shard_map/gather | solution.py:139
  393.0 17.1 copy.270
  410.1 364.4 %all-to-all-done.2 = bf16[3,32,96,1024]{3,2,0,1:T(8,128)(2,1)} async-done(((bf16[3,32,96,1024]{3,2,0,1:T(8,128)(2,1)}), bf16[3,32,96,1024]{3,2,0,1:T(8,128)(2,1)}, u32[]{:S(2)}, u32[]{:S(2)}) %all-to-all-start.2) | async-done | bytes 18874400 | tf_op jit(solution)/shard_map/all_to_all | solution.py:175
  778.9 9.6 copy.276
  801.8 398.0 %all-to-all-done = bf16[3,32,96,1024]{3,2,0,1:T(8,128)(2,1)} async-done(((bf16[3,32,96,1024]{3,2,0,1:T(8,128)(2,1)}), bf16[3,32,96,1024]{3,2,0,1:T(8,128)(2,1)}, u32[]{:S(2)}, u32[]{:S(2)}) %all-to-all-start) | async-done | bytes 18874400 | tf_op jit(solution)/shard_map/all_to_all | solution.py:140
  1199.8 9.4 copy.271
  1209.3 13.1 fusion.9
  1222.4 10.8 convolution_convert_fusion
  1233.3 17.1 copy.277
  1254.4 11.6 convolution_convert_fusion.1
  1266.0 17.1 copy.272
  1283.1 392.7 %all-to-all-done.3 = bf16[3,32,96,1024]{3,2,0,1:T(8,128)(2,1)} async-done(((bf16[3,32,96,1024]{3,2,0,1:T(8,128)(2,1)}), bf16[3,32,96,1024]{3,2,0,1:T(8,128)(2,1)}, u32[]{:S(2)}, u32[]{:S(2)}) %all-to-all-start.3) | async-done | bytes 18874400 | tf_op jit(solution)/shard_map/all_to_all | solution.py:189
  1680.2 17.1 copy.278
  1697.3 49.4 %gather_fusion.4 = bf16[8192,1024]{1,0:T(8,128)(2,1)} fusion(bf16[9216,1024]{1,0:T(8,128)(2,1)} %bitcast.181, s32[8192]{0:T(1024)S(1)} %broadcast_clamp_fusion), kind=kCustom, calls=%fused_computation.4 | custom fusion | bytes 33587200 | tf_op jit(solution)/shard_map/gather | solution.py:197
  1746.7 12.5 convert_reduce_fusion
  1759.2 341.9 %all-to-all-done.1 = bf16[3,32,96,1024]{3,2,0,1:T(8,128)(2,1)} async-done(((bf16[3,32,96,1024]{3,2,0,1:T(8,128)(2,1)}), bf16[3,32,96,1024]{3,2,0,1:T(8,128)(2,1)}, u32[]{:S(2)}, u32[]{:S(2)}) %all-to-all-start.1) | async-done | bytes 18874400 | tf_op jit(solution)/shard_map/all_to_all | solution.py:147
  2101.1 17.0 copy.273
  2118.2 49.6 %gather_fusion.1 = bf16[8192,1024]{1,0:T(8,128)(2,1)} fusion(bf16[9216,1024]{1,0:T(8,128)(2,1)} %bitcast.180, s32[8192]{0:T(1024)S(1)} %broadcast_clamp_fusion), kind=kCustom, calls=%fused_computation.1 | custom fusion | bytes 33587200 | tf_op jit(solution)/shard_map/gather | solution.py:155
  2167.8 9.4 fusion.2
  2183.2 11.6 fusion.1
  2234.8 13.3 fusion.91
  2248.0 13.5 fusion.82
  2269.3 38.6 %all-reduce.2 = (f32[1024]{0:T(1024)}, f32[1024]{0:T(1024)}, f32[96]{0:T(128)S(1)}) all-reduce(f32[1024]{0:T(1024)S(1)} %get-tuple-element.18, f32[1024]{0:T(1024)S(1)} %get-tuple-element.16, f32[96]{0:T(128)S(1)} %convert_element_type.194), channel_id=1, replica_groups=mesh['dp'=4,'expert'=8] {'dp','expert'}, use_global_device_ids=true, to_apply=%region_21.22 | all-reduce | flops 2144 | bytes 17152 | tf_op jit(solution)/shard_map/psum | solution.py:285
  2312.7 324.6 %all-reduce.6.cloned.1.call-done = (f32[1024,512]{1,0:T(8,128)}, f32[1024,512]{1,0:T(8,128)}, f32[1024,2560]{1,0:T(8,128)}, f32[1024,20]{0,1:T(8,128)}, f32[1024...) async-done(((f32[1024,512]{1,0:T(8,128)}, f32[1024,512]{1,0:T(8,128)}, f32[1024,2560]{1,0:T(8,128)}, f32[1024,20]{0,1:T(8,128)}, f32[1024,20]{0,1:T(8,128)}, ...) | async-done | bytes 25722896 | tf_op jit(solution)/shard_map/psum | solution.py:285
  2641.8 9.6 copy.323
  (289 shorter events, 168.8 us)
Async XLA Ops:
  7.2 16.9 copy-start
  7.2 11.8 copy-start.6
  7.2 12.1 copy-start.57
  13.6 12.0 copy-start.72
  18.1 136.9 %copy-start.19 = (pred[512,512]{0,1:T(8,128)(4,1)}, pred[512,512]{0,1:T(8,128)(4,1)S(1)}, u32[]{:S(2)}) copy-start(pred[512,512]{0,1:T(8,128)(4,1)S(1)} %fusion.51) | copy-start | bytes 786436
  23.4 132.9 %copy-start.42 = (f32[512,4,5]{0,2,1:T(8,128)}, f32[512,4,5]{0,2,1:T(8,128)S(1)}, u32[]{:S(2)}) copy-start(f32[512,4,5]{0,2,1:T(8,128)S(1)} %copy.253) | copy-start | bytes 122884
  94.1 41.2 %copy-start.35 = (bf16[512,512]{0,1:T(8,128)(2,1)S(1)}, bf16[512,512]{0,1:T(8,128)(2,1)}, u32[]{:S(2)}) copy-start(bf16[512,512]{0,1:T(8,128)(2,1)} %convolution_convert_fusion.2) | copy-start | bytes 1572868
  94.1 41.1 %copy-start.37 = (bf16[512,512]{0,1:T(8,128)(2,1)S(1)}, bf16[512,512]{0,1:T(8,128)(2,1)}, u32[]{:S(2)}) copy-start(bf16[512,512]{0,1:T(8,128)(2,1)} %convolution_convert_fusion.3) | copy-start | bytes 1572868
  139.2 15.7 copy-start.70
  163.0 68.6 %copy-start.77 = (f32[512]{0:T(512)}, f32[512]{0:T(512)S(1)}, u32[]{:S(2)}) copy-start(f32[512]{0:T(512)S(1)} %add_rsqrt_fusion) | copy-start | bytes 6148
  166.0 65.6 %copy-start.53 = (s32[8192]{0:T(1024)S(1)}, s32[8192]{0:T(1024)}, u32[]{:S(2)}) copy-start(s32[8192]{0:T(1024)} %eq.79) | copy-start | bytes 98308
  166.0 65.6 %copy-start.59 = (s32[9216]{0:T(1024)S(1)}, s32[9216]{0:T(1024)}, u32[]{:S(2)}) copy-start(s32[9216]{0:T(1024)} %get-tuple-element.42) | copy-start | bytes 110596
  231.6 51.2 %copy-start.28 = (f32[8192]{0:T(1024)}, f32[8192]{0:T(1024)S(1)}, u32[]{:S(2)}) copy-start(f32[8192]{0:T(1024)S(1)} %gather_fusion.5) | copy-start | bytes 98308
  345.7 428.8 %all-to-all-start.2 = ((bf16[3,32,96,1024]{3,2,0,1:T(8,128)(2,1)}), bf16[3,32,96,1024]{3,2,0,1:T(8,128)(2,1)}, u32[]{:S(2)}, u32[]{:S(2)}) async-start(bf16[3,32,96,1024]{3,2,0,1:T(8,128)(2,1)} %fusion), calls=%async_computation.2 | async-start | bytes 37748736 | tf_op jit(solution)/shard_map/all_to_all | solution.py:175
  774.6 425.3 %all-to-all-start = ((bf16[3,32,96,1024]{3,2,0,1:T(8,128)(2,1)}), bf16[3,32,96,1024]{3,2,0,1:T(8,128)(2,1)}, u32[]{:S(2)}, u32[]{:S(2)}) async-start(bf16[3,32,96,1024]{3,2,0,1:T(8,128)(2,1)} %copy.270), calls=%async_computation | async-start | bytes 37748736 | tf_op jit(solution)/shard_map/all_to_all | solution.py:140
  778.9 16.1 copy-start.30
  1209.3 13.1 copy-start.2
  1250.4 425.5 %all-to-all-start.3 = ((bf16[3,32,96,1024]{3,2,0,1:T(8,128)(2,1)}), bf16[3,32,96,1024]{3,2,0,1:T(8,128)(2,1)}, u32[]{:S(2)}, u32[]{:S(2)}) async-start(bf16[3,32,96,1024]{3,2,0,1:T(8,128)(2,1)} %copy.277), calls=%async_computation.3 | async-start | bytes 37748736 | tf_op jit(solution)/shard_map/all_to_all | solution.py:189
  1283.1 396.9 %copy-start.29 = (f32[8192]{0:T(1024)S(1)}, f32[8192]{0:T(1024)}, u32[]{:S(2)}) copy-start(f32[8192]{0:T(1024)} %copy-done.28) | copy-start | bytes 98308
  1283.1 397.1 %copy-start.65 = (s32[8192,1]{0,1:T(1,128)S(1)}, s32[8192,1]{0,1:T(1,128)}, u32[]{:S(2)}) copy-start(s32[8192,1]{0,1:T(1,128)} %copy-done.64) | copy-start | bytes 98308
  1675.8 425.3 %all-to-all-start.1 = ((bf16[3,32,96,1024]{3,2,0,1:T(8,128)(2,1)}), bf16[3,32,96,1024]{3,2,0,1:T(8,128)(2,1)}, u32[]{:S(2)}, u32[]{:S(2)}) async-start(bf16[3,32,96,1024]{3,2,0,1:T(8,128)(2,1)} %copy.272), calls=%async_computation.1 | async-start | bytes 37748736 | tf_op jit(solution)/shard_map/all_to_all | solution.py:147
  1679.7 957.5 %all-reduce.6.cloned.1.call-start = ((), (), s32[]{:S(2)}) async-start(), calls=%async_computation.4 | async-start | bytes 51511296 | tf_op jit(solution)/shard_map/psum | solution.py:285
  2118.2 49.6 %copy-start.10 = (f32[512,1024]{1,0:T(8,128)S(1)}, f32[512,1024]{1,0:T(8,128)}, u32[]{:S(2)}) copy-start(f32[512,1024]{1,0:T(8,128)} %bitcast_convert_fusion) | copy-start | bytes 6291460
  2167.8 12.2 copy-start.76
  2167.8 12.2 copy-start.78
  2196.7 15.5 copy-start.13
  2234.8 28.9 %slice-start.3 = ((s8[5242880]{0:T(1024)(128)(4,1)}), s8[1048576]{0:T(1024)(128)(4,1)S(1)}, s32[]{:S(2)}) async-start(s8[5242880]{0:T(1024)(128)(4,1)} %bitcast.196), calls=%async_computation.8 | async-start | bytes 2097152
  2248.0 13.5 copy-start.58
  2248.0 13.9 copy-start.21
  2248.0 15.7 slice-start.4
  2266.7 41.2 %copy-start.80 = (s32[96]{0:T(128)S(1)}, s32[96]{0:T(128)}, u32[]{:S(2)}) copy-start(s32[96]{0:T(128)} %param.32) | copy-start | bytes 1156
  2640.5 12.2 slice-start
  (61 other events, 330.5 us)
Sparse Core Ops, SparseCore 0:
  2234.2 402.9 all-reduce.5
where the time goes:
time: 2680 us; the launch traced here: 2660 us
  waiting for transfers between devices  1820 us (68%)
  local copies, waits for them, and re-layouts  491 us (18%)
  other arithmetic  143 us (5%)
  matrix products  135 us (5%)
  blocking collectives  38.6 us (1%)
    all_to_all x1, waiting for transfers between devices, on_device(): lax.all_to_all(outgoing, ('dp', 'expert'), split_axis=1, concat_axis=1, t...  398 us
    all_to_all x1, waiting for transfers between devices, on_device(): lax.all_to_all(rows_delta.reshape(local_experts, devices, slot_depth, D),...  393 us
    all_to_all x1, waiting for transfers between devices, on_device(): lax.all_to_all(grad_send, ('dp', 'expert'), split_axis=1, concat_axis=1,...  364 us
    all_to_all x1, waiting for transfers between devices, on_device(): lax.all_to_all(produced.reshape(local_experts, devices, slot_depth, D), (...  342 us
    psum x1, waiting for transfers between devices, on_device(): lax.psum((grad_attention, grad_query, grad_key, grad_value, grad_vselect,...  325 us
    gather x5, local copies, waits for them, and re-layouts, on_device(): gate_values = jax.nn.sigmoid(jnp.take_along_axis(logits, chosen, axis=1))  66 us
    another operation x3, other arithmetic  58.5 us
  transfers between devices with their start and end apart: 5, of which 5 were waited for; matrix products, arithmetic and copies ran while one was open for 8% of the time, Pallas kernels for 0%

commit v1 on v0

v1 whole, which is shorter than its diff:
```python
import functools

import jax
import jax.numpy as jnp
from jax import lax
from jax.experimental import pallas as pl
from jax.experimental.pallas import tpu as pltpu
from jax.sharding import PartitionSpec as P

D = 1024
H = 4
DH = 128
NE = 5
FF = 128
TOPK = 16
GATE_LANES = 16

epsilon = 1e-06
masked_value = -1e30
bf16 = jnp.bfloat16
f32 = jnp.float32
tanh_scale = 0.7978845608028654
cubic = 0.044715


def inverse_rms(values):
    return lax.rsqrt(jnp.mean(values * values, axis=-1, keepdims=True) + epsilon)


def norm_back(values, scaling, gain, upstream):
    weighted = upstream * gain
    middle = jnp.mean(values * weighted, axis=-1, keepdims=True)
    return scaling * weighted - values * scaling * scaling * scaling * middle


def masked_scores(query_low, key_low, allowed):
    raw = jnp.einsum(
        "qhd,khd->hqk", query_low, key_low, preferred_element_type=f32
    ) * DH ** (-0.5)
    return jnp.where(allowed[None], raw, masked_value)


def weight_grad(left, right):
    return jnp.einsum("td,tc->dc", left, right, preferred_element_type=f32)


def input_term(delta, weight):
    return jnp.einsum("tc,dc->td", delta, weight, preferred_element_type=f32)


def contract(left, right, left_dim, right_dim):
    return lax.dot_general(
        left, right, (((left_dim,), (right_dim,)), ((), ())), preferred_element_type=f32
    )


def experts_kernel(blocks, pairs, chained, opened, closed, *refs):
    refs = list(refs)

    def take(count):
        taken = refs[:count]
        del refs[:count]
        return taken

    x_hbm, u_hbm, m_hbm = take(blocks), take(blocks), take(blocks)
    select_ref, router_ref = take(2)
    weights = (take(4), take(4))
    y_prev, dx_prev = take(2) if chained else (None, None)
    gu_prev, gd_prev, gr_prev = take(3) if opened else (None, None, None)
    y_ref, dx_ref = take(2)
    grads = take(4) if closed else take(2)
    (gr_ref,) = take(1)
    (x_buf, u_buf, m_buf, sems, w_up, w_down, w_sems) = take(7)
    (y_acc, dx_acc, gup, gdown, x_turned, gate, delta, gr_acc) = refs
    step = pl.program_id(0)
    pair = pl.program_id(1)
    slot = lax.rem(step, 2)
    local = pairs // 2

    def copies(index, place):
        return (
            pltpu.make_async_copy(x_hbm[index], x_buf.at[place], sems.at[place, 0]),
            pltpu.make_async_copy(u_hbm[index], u_buf.at[place], sems.at[place, 1]),
            pltpu.make_async_copy(m_hbm[index], m_buf.at[place], sems.at[place, 2]),
        )

    def weight_copies(index):
        place = index % 2
        k = index % local
        up_a, up_b, down_a, down_b = weights[index // local]
        return (
            pltpu.make_async_copy(up_a.at[k], w_up.at[place, 0], w_sems.at[place, 0]),
            pltpu.make_async_copy(up_b.at[k], w_up.at[place, 1], w_sems.at[place, 1]),
            pltpu.make_async_copy(
                down_a.at[k], w_down.at[place, pl.ds(0, FF)], w_sems.at[place, 2]
            ),
            pltpu.make_async_copy(
                down_b.at[k], w_down.at[place, pl.ds(FF, FF)], w_sems.at[place, 3]
            ),
        )

    @pl.when(jnp.logical_and(step == 0, pair == 0))
    def _():
        for copy in (*copies(0, 0), *weight_copies(0)):
            copy.start()

    for index in range(pairs):

        @pl.when(pair == index)
        def _():
            for copy in weight_copies(index):
                copy.wait()
            if index + 1 < pairs:
                for copy in weight_copies(index + 1):
                    copy.start()
            elif blocks > 1:

                @pl.when(step < blocks - 1)
                def _():
                    for copy in weight_copies(0):
                        copy.start()

    @pl.when(pair == 0)
    def _():
        for number in range(blocks):
            place = number % 2

            @pl.when(step == number)
            def _():
                for copy in copies(number, place):
                    copy.wait()
                if number + 1 < blocks:
                    for copy in copies(number + 1, 1 - place):
                        copy.start()

        x = x_buf[slot]
        x_turned[...] = x.T
        logits = jnp.dot(x, router_ref[...], preferred_element_type=f32)
        chosen = jnp.dot(m_buf[slot], select_ref[...], preferred_element_type=f32)
        gate[...] = jax.nn.sigmoid(logits) * chosen
        delta[...] = jnp.zeros_like(delta)

    x = x_buf[slot]
    u = u_buf[slot]
    tokens = x.shape[0]
    which = lax.rem(pair, 2)
    up = jnp.concatenate([w_up[which, 0], w_up[which, 1]], axis=1)
    down = w_down[which]
    pre_act = jnp.dot(x, up, preferred_element_type=f32)
    pulled = contract(u, down, 1, 1)
    lanes = lax.broadcasted_iota(jnp.int32, gate.shape, 1)
    gates = gate[...]
    gate_a = jnp.sum(jnp.where(lanes == pair, gates, 0.0), axis=1, keepdims=True)
    gate_b = jnp.sum(jnp.where(lanes == pairs + pair, gates, 0.0), axis=1, keepdims=True)
    spread_gate = jnp.concatenate(
        [jnp.broadcast_to(gate_a, (tokens, FF)), jnp.broadcast_to(gate_b, (tokens, FF))], axis=1
    )
    square = pre_act * pre_act
    bent = jnp.tanh(tanh_scale * pre_act * (1.0 + cubic * square))
    hidden = (0.5 * pre_act * (1.0 + bent)).astype(bf16).astype(f32)
    slope = 0.5 * (1.0 + bent) + 0.5 * pre_act * (1.0 - bent * bent) * (
        tanh_scale * (1.0 + 3.0 * cubic * square)
    )
    felt = hidden * pulled
    felt_a = jnp.sum(felt[:, :FF], axis=1, keepdims=True)
    felt_b = jnp.sum(felt[:, FF:], axis=1, keepdims=True)
    kept = jnp.where(lanes == pair, felt_a, delta[...])
    delta[...] = jnp.where(lanes == pairs + pair, felt_b, kept)
    gated = (spread_gate * hidden).astype(bf16)
    hidden_delta = (spread_gate * pulled * slope).astype(bf16)
    y_new = jnp.dot(gated, down, preferred_element_type=f32)
    dx_new = contract(hidden_delta, up, 1, 1)
    gd_new = contract(gated, u, 0, 0)
    gu_new = jnp.dot(x_turned[...], hidden_delta, preferred_element_type=f32)

    @pl.when(pair == 0)
    def _():
        if chained:
            y_acc[...] = y_prev[...].astype(f32) + y_new
            dx_acc[...] = dx_prev[...].astype(f32) + dx_new
        else:
            y_acc[...] = y_new
            dx_acc[...] = dx_new

    @pl.when(pair > 0)
    def _():
        y_acc[...] += y_new
        dx_acc[...] += dx_new

    if blocks == 1:
        if opened:
            gd_new = gd_prev[0] + gd_new
            gu_new = gu_prev[0] + gu_new
        gd_now, gu_now = gd_new, gu_new
    else:

        @pl.when(step == 0)
        def _():
            if opened:
                gdown[pair] = gd_prev[0] + gd_new
                gup[pair] = gu_prev[0] + gu_new
            else:
                gdown[pair] = gd_new
                gup[pair] = gu_new

        @pl.when(step > 0)
        def _():
            gdown[pair] += gd_new
            gup[pair] += gu_new

        gd_now, gu_now = None, None

    @pl.when(step == blocks - 1)
    def _():
        gu_out = gup[pair] if gu_now is None else gu_now
        gd_out = gdown[pair] if gd_now is None else gd_now
        if closed:
            grads[0][0] = gu_out[:, :FF].astype(bf16)
            grads[1][0] = gu_out[:, FF:].astype(bf16)
            grads[2][0] = gd_out[:FF].astype(bf16)
            grads[3][0] = gd_out[FF:].astype(bf16)
        else:
            grads[0][0] = gu_out
            grads[1][0] = gd_out

    @pl.when(pair == pairs - 1)
    def _():
        gates_now = gate[...]
        logit_delta = (delta[...] * gates_now * (1.0 - gates_now)).astype(bf16)
        y_ref[...] = y_acc[...].astype(bf16)
        dx_ref[...] = (dx_acc[...] + contract(logit_delta, router_ref[...], 1, 1)).astype(bf16)
        gr_new = jnp.dot(x_turned[...], logit_delta, preferred_element_type=f32)

        @pl.when(step == 0)
        def _():
            if opened:
                gr_acc[...] = gr_prev[...] + gr_new
            else:
                gr_acc[...] = gr_new

        @pl.when(step > 0)
        def _():
            gr_acc[...] += gr_new

        @pl.when(step == blocks - 1)
        def _():
            gr_ref[...] = gr_acc[...]


def run_experts(xs, us, ms, select, router, first, second, previous, carried, finish):
    blocks = len(xs)
    local = first[0].shape[0]
    pairs = 2 * local
    tokens = xs[0].shape[0]
    experts = select.shape[0]

    def block(i, j):
        return (i, 0)

    def whole(i, j):
        return (0, 0)

    def opening(i, j):
        return (jnp.where(i == 0, j, pairs - 1), 0, 0)

    def closing(i, j):
        return (jnp.where(i == blocks - 1, j, 0), 0, 0)

    anywhere = pl.BlockSpec(memory_space=pl.ANY)
    in_specs = [anywhere] * (3 * blocks) + [
        pl.BlockSpec((experts, GATE_LANES), whole),
        pl.BlockSpec((D, GATE_LANES), whole),
        *[anywhere] * 8,
    ]
    operands = [*xs, *us, *ms, select, router, *first, *second]
    if previous is not None:
        in_specs += [pl.BlockSpec((tokens, D), block)] * 2
        operands += list(previous)
    if carried is not None:
        in_specs += [
            pl.BlockSpec((1, D, 2 * FF), opening),
            pl.BlockSpec((1, 2 * FF, D), opening),
            pl.BlockSpec((D, GATE_LANES), whole),
        ]
        operands += list(carried)
    out_shape = [jax.ShapeDtypeStruct((blocks * tokens, D), bf16)] * 2
    out_specs = [pl.BlockSpec((tokens, D), block)] * 2
    if finish:
        out_shape += [jax.ShapeDtypeStruct((pairs, D, FF), bf16)] * 2
        out_shape += [jax.ShapeDtypeStruct((pairs, FF, D), bf16)] * 2
        out_specs += [pl.BlockSpec((1, D, FF), closing)] * 2
        out_specs += [pl.BlockSpec((1, FF, D), closing)] * 2
    else:
        out_shape += [jax.ShapeDtypeStruct((pairs, D, 2 * FF), f32)]
        out_shape += [jax.ShapeDtypeStruct((pairs, 2 * FF, D), f32)]
        out_specs += [pl.BlockSpec((1, D, 2 * FF), closing), pl.BlockSpec((1, 2 * FF, D), closing)]
    out_shape.append(jax.ShapeDtypeStruct((D, GATE_LANES), f32))
    out_specs.append(pl.BlockSpec((D, GATE_LANES), whole))
    kept = pairs if blocks > 1 else 1
    return pl.pallas_call(
        functools.partial(
            experts_kernel, blocks, pairs, previous is not None, carried is not None, finish
        ),
        grid=(blocks, pairs),
        in_specs=in_specs,
        out_specs=out_specs,
        out_shape=out_shape,
        scratch_shapes=[
            pltpu.VMEM((2, tokens, D), bf16),
            pltpu.VMEM((2, tokens, D), bf16),
            pltpu.VMEM((2, tokens, experts), bf16),
            pltpu.SemaphoreType.DMA((2, 3)),
            pltpu.VMEM((2, 2, D, FF), bf16),
            pltpu.VMEM((2, 2 * FF, D), bf16),
            pltpu.SemaphoreType.DMA((2, 4)),
            pltpu.VMEM((tokens, D), f32),
            pltpu.VMEM((tokens, D), f32),
            pltpu.VMEM((kept, D, 2 * FF), f32),
            pltpu.VMEM((kept, 2 * FF, D), f32),
            pltpu.VMEM((D, tokens), bf16),
            pltpu.VMEM((tokens, GATE_LANES), f32),
            pltpu.VMEM((tokens, GATE_LANES), f32),
            pltpu.VMEM((D, GATE_LANES), f32),
        ],
        compiler_params=pltpu.CompilerParams(
            dimension_semantics=("arbitrary", "arbitrary"),
            vmem_limit_bytes=56 * 1024 * 1024,
        ),
        cost_estimate=pl.CostEstimate(
            flops=24 * blocks * tokens * D * FF * pairs,
            bytes_accessed=blocks * tokens * D * 12 + pairs * D * FF * 24,
            transcendentals=blocks * tokens * 2 * FF * pairs,
        ),
        name="experts",
    )(*operands)


class Moves:
    def __init__(self):
        self.dp = lax.axis_size("dp")
        self.ex = lax.axis_size("expert")
        self.nx = self.dp // 2
        self.nh = self.ex // 2
        self.dp_index = lax.axis_index("dp")
        self.ex_index = lax.axis_index("expert")
        self.core = self.dp_index % 2
        self.x = self.dp_index // 2
        self.lo = self.ex_index % 2
        self.hi = self.ex_index // 2
        steps = [(a, b) for a in range(self.nx) for b in range(2)]
        self.plane = sorted(steps, key=lambda s: ((s[0] > 0) + (s[1] > 0), s))

    def over_core(self, value):
        return lax.ppermute(value, "dp", [(i, i ^ 1) for i in range(self.dp)])

    def over_hi(self, value, by=1):
        pairs = [(i, (i // 2 + by) % self.nh * 2 + i % 2) for i in range(self.ex)]
        return lax.ppermute(value, "expert", pairs)

    def over_plane(self, value, offset, back=False):
        a, b = offset
        if back:
            a = (self.nx - a) % self.nx
        if a == 0:
            return lax.ppermute(value, "expert", [(i, i ^ b) for i in range(self.ex)])
        dp_to = [(i // 2 + a) % self.nx * 2 + i % 2 for i in range(self.dp)]
        if b == 0:
            return lax.ppermute(value, "dp", list(enumerate(dp_to)))
        pairs = [
            (i * self.ex + j, dp_to[i] * self.ex + (j ^ 1))
            for i in range(self.dp)
            for j in range(self.ex)
        ]
        return lax.ppermute(value, ("dp", "expert"), pairs)


def add_low(*terms):
    total = terms[0].astype(f32)
    for term in terms[1:]:
        total = total + term.astype(f32)
    return total.astype(bf16)


def tie(*values):
    return lax.optimization_barrier(values)


def copy_two(order_ref, value_a, value_b, out_a, out_b):
    out_a[...] = value_a[...]
    out_b[...] = value_b[...]


def in_relative_order(moves, value):
    nx, nh = moves.nx, moves.nh
    count = nx * 2 * nh
    rows = value.shape[0] // (2 * count)
    columns = value.shape[1]
    order = []
    for core in (moves.core, 1 - moves.core):
        for a, b in moves.plane:
            for h in range(nh):
                place = (moves.x + a) % nx * 2 + (moves.lo ^ b)
                order.append((core * nx * 2 + place) * nh + (moves.hi + h) % nh)
    order = jnp.stack(order).astype(jnp.int32)
    shape = jax.ShapeDtypeStruct((count, rows, columns), value.dtype)
    value = value.reshape(2 * count, rows, columns)
    outs = pl.pallas_call(
        copy_two,
        grid_spec=pltpu.PrefetchScalarGridSpec(
            num_scalar_prefetch=1,
            grid=(count,),
            in_specs=[
                pl.BlockSpec((1, rows, columns), lambda i, o: (o[i], 0, 0)),
                pl.BlockSpec((1, rows, columns), lambda i, o: (o[count + i], 0, 0)),
            ],
            out_specs=[pl.BlockSpec((1, rows, columns), lambda i, o: (i, 0, 0))] * 2,
        ),
        out_shape=[shape, shape],
        name="relative",
    )(order, value, value)
    return [out.reshape(count * rows, columns) for out in outs]


def in_place_order(moves, mine, theirs, widths):
    nx, nh = moves.nx, moves.nh
    count = nx * 2 * nh
    rows = mine[0].shape[0] // nh
    columns = mine[0].shape[1]
    order = []
    for core in (moves.core, 1 - moves.core):
        for a, b in moves.plane:
            for h in range(nh):
                place = (moves.x - a) % nx * 2 + (moves.lo ^ b)
                order.append((core * nx * 2 + place) * nh + (moves.hi - h) % nh)
    order = jnp.stack(order).astype(jnp.int32)

    def piece(index):
        return pl.BlockSpec(
            (1, rows, columns), lambda i, o: (jnp.clip(i - index * nh, 0, nh - 1), 0, 0)
        )

    pieces = [p.reshape(nh, rows, columns) for p in (*mine, *theirs)]
    outs = pl.pallas_call(
        functools.partial(place_pieces, nx * 4, nh, widths),
        grid_spec=pltpu.PrefetchScalarGridSpec(
            num_scalar_prefetch=1,
            grid=(2 * count,),
            in_specs=[piece(index) for index in range(nx * 4)],
            out_specs=[
                pl.BlockSpec((1, rows, width), lambda i, o: (o[i], 0, 0)) for width in widths
            ],
        ),
        out_shape=[jax.ShapeDtypeStruct((2 * count, rows, width), f32) for width in widths],
        name="assemble",
    )(order, *pieces)
    return [out.reshape(2 * count * rows, width) for out, width in zip(outs, widths)]


def place_pieces(pieces, nh, widths, order_ref, *refs):
    outs = refs[pieces:]
    step = pl.program_id(0)
    for index in range(pieces):

        @pl.when(step // nh == index)
        def _():
            start = 0
            for out, width in zip(outs, widths):
                out[...] = refs[index][:, :, start : start + width].astype(f32)
                start += width


class Sum:
    def __init__(self, moves, value, widths):
        self.moves = moves
        self.widths = widths
        self.held, self.away = in_relative_order(moves, value)

    def core(self):
        moves = self.moves
        got = moves.over_core(self.away)
        count = len(moves.plane)
        rows = got.shape[0] // count
        self.parts = [
            add_low(self.held[k * rows : (k + 1) * rows], got[k * rows : (k + 1) * rows])
            for k in range(count)
        ]

    def plane(self):
        moves = self.moves
        got = [moves.over_plane(p, s) for p, s in zip(self.parts[1:], moves.plane[1:])]
        nh = moves.nh
        rows = self.parts[0].shape[0] // nh
        terms = [self.parts[0], *got]
        self.parts = [
            add_low(*[term[h * rows : (h + 1) * rows] for term in terms]) for h in range(nh)
        ]

    def line(self):
        moves = self.moves
        got = [moves.over_hi(self.parts[h], h) for h in range(1, moves.nh)]
        self.total = add_low(self.parts[0], *got)

    def line_back(self):
        moves = self.moves
        got = [moves.over_hi(self.total, h) for h in range(1, moves.nh)]
        self.rows = jnp.concatenate([self.total, *got], axis=0)

    def plane_back(self):
        moves = self.moves
        self.mine = [self.rows] + [moves.over_plane(self.rows, s) for s in moves.plane[1:]]

    def core_back(self):
        moves = self.moves
        theirs = [moves.over_core(piece) for piece in self.mine]
        return in_place_order(moves, self.mine, theirs, self.widths)


def sum_small(moves, value):
    for axis, size in (("dp", moves.dp), ("expert", moves.ex)):
        span = 1
        while span < size:
            value = value + lax.ppermute(value, axis, [(i, i ^ span) for i in range(size)])
            span *= 2
    return value


def select_back(select):
    return select.T


def on_device(
    hidden_in,
    segment_ids,
    head_experts,
    token_experts,
    attention_gain,
    query_weight,
    key_weight,
    value_weight,
    value_selector,
    output_selector,
    output_weight,
    mixture_gain,
    router_weight,
    up_weight,
    down_weight,
    expert_counts,
    output_cotangent,
):
    moves = Moves()
    nx, nh = moves.nx, moves.nh
    length = hidden_in.shape[1]
    experts = router_weight.shape[1]
    local = up_weight.shape[0]
    expert_range = jnp.arange(experts, dtype=jnp.int32)

    chosen = token_experts[0]
    routed = jnp.sum((chosen[:, :, None] == expert_range[None, None, :]).astype(f32), axis=1)
    local_counts = jnp.sum(routed, axis=0)
    upstream_low = output_cotangent[0]
    near = [s for s in moves.plane[1:] if 0 in s]
    far = [s for s in moves.plane[1:] if 0 not in s]
    routed_low = routed.astype(bf16)

    ups, downs = [up_weight], [down_weight]
    ups.append(moves.over_hi(up_weight))
    downs.append(moves.over_hi(down_weight))
    us = {s: moves.over_plane(upstream_low, s) for s in near}
    ms = {s: moves.over_plane(routed_low, s) for s in moves.plane[1:]}

    inputs = hidden_in[0].astype(f32)
    att_rms = inverse_rms(inputs)
    normed_low = (inputs * att_rms * attention_gain).astype(bf16)
    query_low = (
        jnp.dot(normed_low, query_weight, preferred_element_type=f32)
        .astype(bf16)
        .reshape(length, H, DH)
    )
    key_low = (
        jnp.dot(normed_low, key_weight, preferred_element_type=f32)
        .astype(bf16)
        .reshape(length, H, DH)
    )
    values_all = jnp.dot(normed_low, value_weight, preferred_element_type=f32).reshape(
        length, H, NE, DH
    )
    value_sigmoid = jax.nn.sigmoid(
        jnp.dot(normed_low, value_selector, preferred_element_type=f32)
    ).reshape(length, H, NE)
    output_sigmoid = jax.nn.sigmoid(
        jnp.dot(normed_low, output_selector, preferred_element_type=f32)
    ).reshape(length, H, NE)
    chosen_mask = jnp.sum(
        (head_experts[0][:, :, :, None] == jnp.arange(NE, dtype=jnp.int32)).astype(f32),
        axis=2,
    )
    value_gate = value_sigmoid * chosen_mask
    output_gate = output_sigmoid * chosen_mask
    value_low = jnp.sum(value_gate[..., None] * values_all, axis=2).astype(bf16)
    positions = jnp.arange(length, dtype=jnp.int32)
    segments = segment_ids[0]
    allowed = (positions[None, :] <= positions[:, None]) & (segments[None, :] == segments[:, None])
    scores = masked_scores(query_low, key_low, allowed)
    log_total = jax.nn.logsumexp(scores, axis=-1, keepdims=True)
    probs_low = jnp.exp(scores - log_total).astype(bf16)
    mixed_heads = jnp.einsum("hqk,khd->qhd", probs_low, value_low, preferred_element_type=f32)
    spread_low = (
        (output_gate[..., None] * mixed_heads[:, :, None, :])
        .astype(bf16)
        .reshape(length, H * NE * DH)
    )
    middle_rows = inputs + jnp.dot(spread_low, output_weight, preferred_element_type=f32)
    moe_rms = inverse_rms(middle_rows)
    moe_low = (middle_rows * moe_rms * mixture_gain).astype(bf16)

    moe_low, ups[1], downs[1] = tie(moe_low, ups[1], downs[1])
    home = moves.plane[0]
    xs = {home: moe_low}
    us[home] = upstream_low
    ms[home] = routed_low
    for s in near:
        xs[s] = moves.over_plane(moe_low, s)
    core_ups = [moves.over_core(u) for u in ups[:2]]
    core_downs = [moves.over_core(d) for d in downs[:2]]
    ups.append(moves.over_hi(ups[1]))
    downs.append(moves.over_hi(downs[1]))

    def slot_weights(s):
        return (ups[s], core_ups[s], downs[s], core_downs[s])

    def selection(slots):
        columns = []
        for core in (0, 1):
            for s in slots:
                owner = (moves.dp_index ^ core) * moves.ex + (moves.hi - s) % nh * 2 + moves.lo
                columns += [owner * local + k for k in range(local)]
        columns += [jnp.int32(-1)] * (GATE_LANES - len(columns))
        select = (expert_range[:, None] == jnp.stack(columns)[None, :]).astype(bf16)
        return select, jnp.dot(router_weight, select, preferred_element_type=f32).astype(bf16)

    sums = {}
    router_sum = jnp.zeros((D, experts), f32)
    mine_slots, theirs_slots = [None] * nh, [None] * nh

    def visit(offsets, phase, carried, finish):
        slots = (2 * phase, 2 * phase + 1)
        select, router = chosen_by[phase]
        previous = None
        if offsets[0] in sums:
            joined = [sums[s] for s in offsets]
            previous = joined[0] if len(joined) == 1 else tuple(
                jnp.concatenate([j[w] for j in joined], axis=0) for w in (0, 1)
            )
        y, dx, *grads = run_experts(
            [xs[s] for s in offsets],
            [us[s] for s in offsets],
            [ms[s] for s in offsets],
            select,
            router,
            slot_weights(slots[0]),
            slot_weights(slots[1]),
            previous,
            carried,
            finish,
        )
        for k, s in enumerate(offsets):
            sums[s] = (y[k * length : (k + 1) * length], dx[k * length : (k + 1) * length])
        return grads

    phases = nh // 2
    chosen_by = [selection((2 * p, 2 * p + 1)) for p in range(phases)]
    held = None
    sent_back = {}
    for phase in range(phases):
        last = phase == phases - 1
        if phase == 0:
            calls = [[home], *[[s] for s in near], far]
        elif last:
            calls = [[s] for s in far] + [[s] for s in near] + [[home]]
        else:
            calls = [[home], *[[s] for s in near], far]
        grads = None
        for turn, offsets in enumerate(calls):
            grads = visit(offsets, phase, grads, turn == len(calls) - 1)
            if phase == 0 and turn == 0:
                values = tie(grads[0], moe_low, upstream_low, *[xs[s] for s in near])
                grads[0], far_x, far_u = values[:3]
                for s, value in zip(near, values[3:]):
                    xs[s] = value
                for s in far:
                    xs[s] = moves.over_plane(far_x, s)
                    us[s] = moves.over_plane(far_u, s)
            if phase == 0 and turn == 1 and nh > 2:
                grads[0], ups[2], downs[2] = tie(grads[0], ups[2], downs[2])
                for s in range(3, nh):
                    ups.append(moves.over_hi(ups[-1]))
                    downs.append(moves.over_hi(downs[-1]))
                core_ups.append(moves.over_core(ups[2]))
                core_downs.append(moves.over_core(downs[2]))
            if phase == 0 and turn == len(calls) - 2 and nh > 2:
                values = tie(grads[0], *ups[3:], *downs[3:])
                grads[0] = values[0]
                ups[3:] = values[1 : nh - 2]
                downs[3:] = values[nh - 2 :]
                core_ups += [moves.over_core(u) for u in ups[3:]]
                core_downs += [moves.over_core(d) for d in downs[3:]]
            if last and offsets != [home]:
                for s in offsets:
                    sent_back[s] = [moves.over_plane(v, s, back=True) for v in sums[s][::-1]]
        router_sum = router_sum + jnp.dot(
            grads[4].astype(bf16), select_back(chosen_by[phase][0]), preferred_element_type=f32
        )
        gu_mine, gu_theirs, gd_mine, gd_theirs = grads[:4]
        gu_got, gd_got = moves.over_core(gu_theirs), moves.over_core(gd_theirs)
        for k in range(2):
            s = 2 * phase + k
            cut = slice(k * local, (k + 1) * local)
            parts = [(gu_mine[cut], gu_got[cut]), (gd_mine[cut], gd_got[cut])]
            if s == 0:
                first_parts = parts
                continue
            if held is not None:
                parts = [(*p, moves.over_hi(h)) for p, h in zip(parts, held)]
            held = [add_low(*p) for p in parts]

    def token_sum(which):
        total = sums[home][1 - which].astype(f32)
        for s in moves.plane[1:]:
            total = total + sent_back[s][which].astype(f32)
        return total

    expert_delta = token_sum(0)

    upstream = upstream_low.astype(f32)
    middle_delta = upstream + norm_back(middle_rows, moe_rms, mixture_gain, expert_delta)
    grad_mixture = jnp.sum(expert_delta * middle_rows * moe_rms, axis=0)
    middle_low = middle_delta.astype(bf16)
    grad_output = jnp.einsum(
        "tc,td->cd", spread_low, middle_low, preferred_element_type=f32
    ).astype(bf16)
    spread_delta = jnp.einsum(
        "td,cd->tc", middle_low, output_weight, preferred_element_type=f32
    ).reshape(length, H, NE, DH)
    mixed_delta = jnp.sum(output_gate[..., None] * spread_delta, axis=2).astype(bf16)
    oselect_delta = (
        (
            jnp.sum(spread_delta * mixed_heads[:, :, None, :], axis=3)
            * chosen_mask
            * output_sigmoid
            * (1.0 - output_sigmoid)
        )
        .astype(bf16)
        .reshape(length, H * NE)
    )
    scores = masked_scores(query_low, key_low, allowed)
    probs_full = jnp.exp(scores - log_total)
    probs_again = probs_full.astype(bf16)
    weight_delta = jnp.einsum("qhd,khd->hqk", mixed_delta, value_low, preferred_element_type=f32)
    score_delta = (
        probs_full * (weight_delta - jnp.sum(probs_full * weight_delta, axis=-1, keepdims=True))
    ).astype(bf16)
    query_delta = (
        (
            jnp.einsum("hqk,khd->qhd", score_delta, key_low, preferred_element_type=f32)
            * DH ** (-0.5)
        )
        .astype(bf16)
        .reshape(length, H * DH)
    )
    key_delta = (
        (
            jnp.einsum("hqk,qhd->khd", score_delta, query_low, preferred_element_type=f32)
            * DH ** (-0.5)
        )
        .astype(bf16)
        .reshape(length, H * DH)
    )
    value_delta = jnp.einsum("hqk,qhd->khd", probs_again, mixed_delta, preferred_element_type=f32)
    values_delta = (
        (value_gate[..., None] * value_delta[:, :, None, :])
        .astype(bf16)
        .reshape(length, H * NE * DH)
    )
    vselect_delta = (
        (
            jnp.sum(value_delta[:, :, None, :] * values_all, axis=3)
            * chosen_mask
            * value_sigmoid
            * (1.0 - value_sigmoid)
        )
        .astype(bf16)
        .reshape(length, H * NE)
    )
    grad_value = weight_grad(normed_low, values_delta).astype(bf16)
    narrow = 2 * H * NE + experts
    padding = -narrow % 128
    grad_rest = jnp.concatenate(
        [
            weight_grad(normed_low, query_delta).astype(bf16),
            weight_grad(normed_low, key_delta).astype(bf16),
            jnp.concatenate(
                [
                    weight_grad(normed_low, vselect_delta),
                    weight_grad(normed_low, oselect_delta),
                    router_sum,
                    jnp.zeros((D, padding), f32),
                ],
                axis=1,
            ).astype(bf16),
        ],
        axis=1,
    )
    normed_delta = (
        input_term(query_delta, query_weight)
        + input_term(key_delta, key_weight)
        + input_term(values_delta, value_weight)
    )
    normed_delta = (
        normed_delta
        + input_term(vselect_delta, value_selector)
        + input_term(oselect_delta, output_selector)
    )
    input_delta = middle_delta + norm_back(inputs, att_rms, attention_gain, normed_delta)
    grad_attention = jnp.sum(normed_delta * inputs * att_rms, axis=0)
    out_sum = Sum(moves, grad_output, [D])
    value_sum = Sum(moves, grad_value, [H * NE * DH])
    rest_sum = Sum(moves, grad_rest, [H * DH, H * DH, narrow + padding])
    out_sum.core()
    out_sum.plane()
    value_sum.core()
    out_sum.line()
    value_sum.plane()
    out_sum.line_back()
    rest_sum.core()
    value_sum.line()
    rest_sum.plane()
    value_sum.line_back()
    rest_sum.line()
    out_sum.plane_back()
    rest_sum.line_back()
    (grad_output,) = out_sum.core_back()
    value_sum.plane_back()
    (grad_value,) = value_sum.core_back()
    rest_sum.plane_back()
    grad_query, grad_key, narrow_sum = rest_sum.core_back()
    grad_vselect = narrow_sum[:, : H * NE]
    grad_oselect = narrow_sum[:, H * NE : 2 * H * NE]
    grad_router = narrow_sum[:, 2 * H * NE : narrow]

    output_rows = middle_rows + token_sum(1)
    grad_up, grad_down = (
        moves.over_hi(h).astype(f32) + a.astype(f32) + b.astype(f32)
        for h, (a, b) in zip(held, first_parts)
    )
    small = sum_small(
        moves,
        jnp.stack([grad_attention, grad_mixture, jnp.pad(local_counts, (0, D - experts))]),
    )
    new_counts = expert_counts + small[2, :experts].astype(jnp.int32)
    return (
        output_rows.astype(bf16)[None],
        input_delta[None],
        small[0],
        grad_query,
        grad_key,
        grad_value,
        grad_vselect,
        grad_oselect,
        grad_output,
        small[1],
        grad_router,
        grad_up,
        grad_down,
        new_counts,
    )


def solution(mesh):
    rows3 = P(("dp", "expert"), None, None)
    placed = (
        rows3,
        P(("dp", "expert"), None),
        P(("dp", "expert"), None, None, None),
        rows3,
        *[P()] * 9,
        rows3,
        rows3,
        P(),
        rows3,
    )
    return jax.shard_map(
        on_device,
        mesh=mesh,
        in_specs=placed,
        out_specs=(rows3, rows3, *[P()] * 9, rows3, rows3, P()),
        check_vma=False,
    )
```

time: 2680 us -> 804 us (0.30)
  waiting for transfers between devices: 1820 us -> 258 us
  local copies, waits for them, and re-layouts: 491 us -> 51.1 us
  Pallas kernels: 0 us -> 288 us
  other arithmetic: 143 us -> 47.5 us
  matrix products: 135 us -> 54.3 us
  starting transfers between devices: 20 us -> 88.9 us
  blocking collectives: 38.6 us -> 0 us
    all_to_all x4 -> x0, waiting for transfers between devices: 1500 us -> none  [the longest x1 398 us: on_device(): lax.all_to_all(outgoing, ('dp', 'expert'), split_axis=1, concat_axis=1, t...]
    psum x1 -> x0, waiting for transfers between devices: 325 us -> none  [on_device(): lax.psum((grad_attention, grad_query, grad_key, grad_value, grad_vselect,...]
    gather x10 -> x0, local copies, waits for them, and re-layouts: 296 us -> none  [the longest x5 66 us: on_device(): gate_values = jax.nn.sigmoid(jnp.take_along_axis(logits, chosen, axis=1))]
    pallas_call x0 -> x14, Pallas kernels: none -> 288 us  [the longest x8 195 us: run_experts(): pl.pallas_call(functools.partial(experts_kernel, blocks, pairs, previous...]
    ppermute x0 -> x95, waiting for transfers between devices: none -> 258 us  [the longest x30 106 us: over_hi(): return lax.ppermute(value, 'expert', pairs)]
    ppermute x0 -> x95, starting transfers between devices: none -> 88.9 us  [the longest x30 42.2 us: over_hi(): return lax.ppermute(value, 'expert', pairs)]
    dot_general x29 -> x24, matrix products: 125 us -> 47.6 us  [the longest x5 13.6 us: input_term(): return jnp.einsum('tc,dc->td', delta, weight, preferred_element_type=f32)]
    another operation x3 -> x1, other arithmetic: 58.5 us -> 0.02 us  [on_device(): jnp.stack([grad_attention, grad_mixture, jnp.pad(local_counts, (0, D - ex...]
  transfers between devices with their start and end apart: 5 -> 95, of which waited for: 5 -> 30; matrix products, arithmetic and copies ran while one was open for 8% -> 18% of each run, Pallas kernels for 0% -> 31%
where the time goes in v1:
time: 804 us; the launch traced here: 790 us
  Pallas kernels  288 us (36%)
  waiting for transfers between devices  258 us (32%)
  starting transfers between devices  88.9 us (11%)
  matrix products  54.3 us (7%)
  local copies, waits for them, and re-layouts  51.1 us (6%)
  other arithmetic  47.5 us (6%)
    pallas_call x8, Pallas kernels, run_experts(): pl.pallas_call(functools.partial(experts_kernel, blocks, pairs, previous...  195 us
    ppermute x30, waiting for transfers between devices, over_hi(): return lax.ppermute(value, 'expert', pairs)  106 us
    pallas_call x3, Pallas kernels, in_place_order(): pl.pallas_call(functools.partial(place_pieces, nx * 4, nh, widths), grid_...  59.7 us
    ppermute x11, waiting for transfers between devices, over_plane(): return lax.ppermute(value, 'expert', [(i, i ^ b) for i in range(self.ex)])  53.6 us
    ppermute x11, waiting for transfers between devices, over_plane(): return lax.ppermute(value, ('dp', 'expert'), pairs)  46.3 us
    ppermute x30, starting transfers between devices, over_hi(): return lax.ppermute(value, 'expert', pairs)  42.2 us
    ppermute x11, waiting for transfers between devices, over_plane(): return lax.ppermute(value, 'dp', list(enumerate(dp_to)))  35.5 us
    pallas_call x3, Pallas kernels, in_relative_order(): pl.pallas_call(copy_two, grid_spec=pltpu.PrefetchScalarGridSpec(num_scala...  33.4 us
  transfers between devices with their start and end apart: 95, of which 30 were waited for; matrix products, arithmetic and copies ran while one was open for 18% of the time, Pallas kernels for 31%

profile of v1, /device:TPU:0, one launch (start us, length us, event | category | flops | bytes accessed | tf_op | source)
XLA Modules:
  0.0 790.1 jit_solution(17623964149622131399)
XLA Ops:
  11.5 7.9 %copy.141 = bf16[1024,2560]{0,1:T(8,128)(2,1)} copy(bf16[1024,2560]{1,0:T(8,128)(2,1)} %param.24) | data formatting | bytes 10485760 | tf_op args[7]
  58.2 8.6 %collective-permute-done.6.refs_0_ = bf16[512,1024]{1,0:T(8,128)(2,1)} collective-permute-done((bf16[512,1024]{1,0:T(8,128)(2,1)}, bf16[512,1024]{1,0:T(8,128)(2,1)}, u32[]{:S(2)}, u32[]{:S(2)}) %collective-permute-start.6) | collective-permute-done | bytes 1048608 | tf_op jit(solution)/shard_map/ppermute | solution.py:365
  66.9 23.2 %experts.8 = (bf16[512,1024]{1,0:T(8,128)(2,1)}, bf16[512,1024]{1,0:T(8,128)(2,1)}, f32[6,1024,256]{2,1,0:T(8,128)}, f32[6,256,1024]{2,1,0:T(8,128)}, f32[1024,16]{1,0:T(8,128)}) custom-call(bf16[512,1024]{1,0:T(8,128)(2,1)} %multiply_convert_fusion.3.refs_0_, bf16[512,1024]{1,0:T(8,128)(2,1)} %bitcast.328, bf16[512,96]{1,0:T(8,128)(2,1)} %copy.145.refs_2_, ...), custom_call_target="tpu_custom_call" | custom-call | flops 9663676416 | bytes 25165824 | tf_op jit(solution)/shard_map/experts/pallas_call | solution.py:300
  95.9 24.2 %experts.9 = (bf16[512,1024]{1,0:T(8,128)(2,1)}, bf16[512,1024]{1,0:T(8,128)(2,1)}, f32[6,1024,256]{2,1,0:T(8,128)}, f32[6,256,1024]{2,1,0:T(8,128)}, f32[1024,16]{1,0:T(8,128)}) custom-call(bf16[512,1024]{1,0:T(8,128)(2,1)} %collective-permute-done.6.refs_0_, bf16[512,1024]{1,0:T(8,128)(2,1)} %copy-done.79, bf16[512,96]{1,0:T(8,128)(2,1)} %copy-done.84, ...), custom_call_target="tpu_custom_call" | custom-call | flops 9663676416 | bytes 25165824 | tf_op jit(solution)/shard_map/experts/pallas_call | solution.py:300
  125.4 24.6 %experts.10 = (bf16[512,1024]{1,0:T(8,128)(2,1)}, bf16[512,1024]{1,0:T(8,128)(2,1)}, f32[6,1024,256]{2,1,0:T(8,128)}, f32[6,256,1024]{2,1,0:T(8,128)}, f32[1024,16]{1,0:T(8,128)}) custom-call(bf16[512,1024]{1,0:T(8,128)(2,1)} %copy-done.78, bf16[512,1024]{1,0:T(8,128)(2,1)} %copy-done.80, bf16[512,96]{1,0:T(8,128)(2,1)} %copy-done.85, ...), custom_call_target="tpu_custom_call" | custom-call | flops 9663676416 | bytes 25165824 | tf_op jit(solution)/shard_map/experts/pallas_call | solution.py:300
  156.3 23.8 %experts.11 = (bf16[512,1024]{1,0:T(8,128)(2,1)}, bf16[512,1024]{1,0:T(8,128)(2,1)}, bf16[6,1024,128]{2,1,0:T(8,128)(2,1)}, bf16[6,1024,128]{2,1,0:T(8,128)(2,1)...) custom-call(bf16[512,1024]{1,0:T(8,128)(2,1)} %collective-permute-done.20.refs_0_, ...), custom_call_target="tpu_custom_call" | custom-call | flops 9663676416 | bytes 25165824 | tf_op jit(solution)/shard_map/experts/pallas_call | solution.py:300
  181.1 23.8 %experts.12 = (bf16[512,1024]{1,0:T(8,128)(2,1)}, bf16[512,1024]{1,0:T(8,128)(2,1)}, f32[6,1024,256]{2,1,0:T(8,128)}, f32[6,256,1024]{2,1,0:T(8,128)}, f32[1024,16]{1,0:T(8,128)}) custom-call(bf16[512,1024]{1,0:T(8,128)(2,1)} %collective-permute-done.20.refs_0_, bf16[512,1024]{1,0:T(8,128)(2,1)} %collective-permute-done.21.refs_1_, ...), custom_call_target="tpu_custom_call" | custom-call | flops 9663676416 | bytes 25165824 | tf_op jit(solution)/shard_map/experts/pallas_call | solution.py:300
  205.9 24.9 %experts.13 = (bf16[512,1024]{1,0:T(8,128)(2,1)}, bf16[512,1024]{1,0:T(8,128)(2,1)}, f32[6,1024,256]{2,1,0:T(8,128)}, f32[6,256,1024]{2,1,0:T(8,128)}, f32[1024,16]{1,0:T(8,128)}) custom-call(bf16[512,1024]{1,0:T(8,128)(2,1)} %collective-permute-done.6.refs_0_, bf16[512,1024]{1,0:T(8,128)(2,1)} %copy-done.79, bf16[512,96]{1,0:T(8,128)(2,1)} %copy-done.84, ...), custom_call_target="tpu_custom_call" | custom-call | flops 9663676416 | bytes 25165824 | tf_op jit(solution)/shard_map/experts/pallas_call | solution.py:300
  230.8 25.2 %experts.14 = (bf16[512,1024]{1,0:T(8,128)(2,1)}, bf16[512,1024]{1,0:T(8,128)(2,1)}, f32[6,1024,256]{2,1,0:T(8,128)}, f32[6,256,1024]{2,1,0:T(8,128)}, f32[1024,16]{1,0:T(8,128)}) custom-call(bf16[512,1024]{1,0:T(8,128)(2,1)} %copy-done.78, bf16[512,1024]{1,0:T(8,128)(2,1)} %copy-done.80, bf16[512,96]{1,0:T(8,128)(2,1)} %copy-done.85, ...), custom_call_target="tpu_custom_call" | custom-call | flops 9663676416 | bytes 25165824 | tf_op jit(solution)/shard_map/experts/pallas_call | solution.py:300
  260.7 24.8 %experts.15 = (bf16[512,1024]{1,0:T(8,128)(2,1)}, bf16[512,1024]{1,0:T(8,128)(2,1)}, bf16[6,1024,128]{2,1,0:T(8,128)(2,1)}, bf16[6,1024,128]{2,1,0:T(8,128)(2,1)...) custom-call(bf16[512,1024]{1,0:T(8,128)(2,1)} %multiply_convert_fusion.3.refs_0_, ...), custom_call_target="tpu_custom_call" | custom-call | flops 9663676416 | bytes 25165824 | tf_op jit(solution)/shard_map/experts/pallas_call | solution.py:300
  290.3 14.3 %collective-permute-done.26 = bf16[512,1024]{1,0:T(8,128)(2,1)S(1)} collective-permute-done((bf16[512,1024]{1,0:T(8,128)(2,1)}, bf16[512,1024]{1,0:T(8,128)(2,1)S(1)}, u32[]{:S(2)}, u32[]{:S(2)}) %collective-permute-start.26) | collective-permute-done | bytes 1048608 | tf_op jit(solution)/shard_map/ppermute | solution.py:365
  306.2 20.5 %collective-permute-done.24 = bf16[512,1024]{1,0:T(8,128)(2,1)} collective-permute-done((bf16[512,1024]{1,0:T(8,128)(2,1)}, bf16[512,1024]{1,0:T(8,128)(2,1)}, u32[]{:S(2)}, u32[]{:S(2)}) %collective-permute-start.24) | collective-permute-done | bytes 1048608 | tf_op jit(solution)/shard_map/ppermute | solution.py:368
  373.2 11.6 %relative.4 = (bf16[16,32,2560]{2,1,0:T(8,128)(2,1)}, bf16[16,32,2560]{2,1,0:T(8,128)(2,1)}) custom-call(s32[32]{0:T(128)} %stack.503.order_ref, bf16[32,32,2560]{2,1,0:T(8,128)(2,1)} %bitcast.298, bf16[32,32,2560]{2,1,0:T(8,128)(2,1)} %bitcast.299), custom_call_target="tpu_custom_call" | custom-call | tf_op jit(solution)/shard_map/relative/pallas_call | solution.py:407
  389.5 12.4 %concatenate.15 = bf16[1024,1280]{0,1:T(8,128)(2,1)} concatenate(bf16[1024,512]{0,1:T(8,128)(2,1)S(1)} %copy-done.36, bf16[1024,512]{0,1:T(8,128)(2,1)} %convolution_convert_fusion.2, bf16[1024,20]{0,1:T(8,128)(2,1)S(1)} %convolution_convert_fusion.7, bf16[1024,20]{0,1:T(8,128)(2,1)} %convolution_convert_fusion.6, bf16[1024,96]{0,1:T(8,128)(2,1)} %fusion.31, ...), dimensions={1} | concatenate | bytes 5242880 | tf_op jit(solution)/shard_map/concatenate | solution.py:797
  406.3 10.4 %relative.3 = (bf16[16,32,1280]{2,1,0:T(8,128)(2,1)}, bf16[16,32,1280]{2,1,0:T(8,128)(2,1)}) custom-call(s32[32]{0:T(128)} %stack.503.order_ref, bf16[32,32,1280]{2,1,0:T(8,128)(2,1)} %bitcast.294, bf16[32,32,1280]{2,1,0:T(8,128)(2,1)} %bitcast.295), custom_call_target="tpu_custom_call" | custom-call | tf_op jit(solution)/shard_map/relative/pallas_call | solution.py:407
  425.8 11.4 %relative.5 = (bf16[16,80,1024]{2,1,0:T(8,128)(2,1)}, bf16[16,80,1024]{2,1,0:T(8,128)(2,1)}) custom-call(s32[32]{0:T(128)} %stack.503.order_ref, bf16[32,80,1024]{2,1,0:T(8,128)(2,1)} %bitcast.296, bf16[32,80,1024]{2,1,0:T(8,128)(2,1)} %bitcast.297), custom_call_target="tpu_custom_call" | custom-call | tf_op jit(solution)/shard_map/relative/pallas_call | solution.py:407
  448.2 12.0 %collective-permute-done.32 = f32[3,1024]{1,0:T(4,128)S(1)} collective-permute-done((f32[3,1024]{1,0:T(4,128)S(1)}, f32[3,1024]{1,0:T(4,128)S(1)}, u32[]{:S(2)}, u32[]{:S(2)}) %collective-permute-start.32) | collective-permute-done | bytes 12320 | tf_op jit(solution)/shard_map/ppermute | solution.py:522
  484.1 20.3 %collective-permute-done.39 = bf16[32,1280]{1,0:T(8,128)(2,1)S(1)} collective-permute-done((bf16[32,1280]{1,0:T(8,128)(2,1)S(1)}, bf16[32,1280]{1,0:T(8,128)(2,1)S(1)}, u32[]{:S(2)}, u32[]{:S(2)}) %collective-permute-start.39) | collective-permute-done | bytes 81952 | tf_op jit(solution)/shard_map/ppermute | solution.py:358
  524.1 21.3 %collective-permute-done.44 = bf16[128,1280]{1,0:T(8,128)(2,1)S(1)} collective-permute-done((bf16[128,1280]{1,0:T(8,128)(2,1)S(1)}, bf16[128,1280]{1,0:T(8,128)(2,1)S(1)}, u32[]{:S(2)}, u32[]{:S(2)}) %collective-permute-start.44) | collective-permute-done | bytes 327712 | tf_op jit(solution)/shard_map/ppermute | solution.py:365
  550.5 20.5 %collective-permute-done.71 = bf16[320,1024]{1,0:T(8,128)(2,1)S(1)} collective-permute-done((bf16[320,1024]{1,0:T(8,128)(2,1)S(1)}, bf16[320,1024]{1,0:T(8,128)(2,1)S(1)}, u32[]{:S(2)}, u32[]{:S(2)}) %collective-permute-start.71) | collective-permute-done | bytes 655392 | tf_op jit(solution)/shard_map/ppermute | solution.py:374
  573.4 9.7 %collective-permute-done.70 = bf16[320,1024]{1,0:T(8,128)(2,1)S(1)} collective-permute-done((bf16[320,1024]{1,0:T(8,128)(2,1)S(1)}, bf16[320,1024]{1,0:T(8,128)(2,1)S(1)}, u32[]{:S(2)}, u32[]{:S(2)}) %collective-permute-start.70) | collective-permute-done | bytes 655392 | tf_op jit(solution)/shard_map/ppermute | solution.py:368
  591.5 40.9 %collective-permute-done.56 = bf16[32,2560]{1,0:T(8,128)(2,1)S(1)} collective-permute-done((bf16[32,2560]{1,0:T(8,128)(2,1)S(1)}, bf16[32,2560]{1,0:T(8,128)(2,1)S(1)}, u32[]{:S(2)}, u32[]{:S(2)}) %collective-permute-start.56) | collective-permute-done | bytes 163872 | tf_op jit(solution)/shard_map/ppermute | solution.py:358
  636.4 8.7 %collective-permute-done.73 = bf16[80,1024]{1,0:T(8,128)(2,1)S(1)} collective-permute-done((bf16[80,1024]{1,0:T(8,128)(2,1)S(1)}, bf16[80,1024]{1,0:T(8,128)(2,1)S(1)}, u32[]{:S(2)}, u32[]{:S(2)}) %collective-permute-start.73) | collective-permute-done | bytes 163872 | tf_op jit(solution)/shard_map/ppermute | solution.py:358
  645.2 6.7 collective-permute-start.58
  663.8 5.6 collective-permute-done.76
  671.0 6.7 collective-permute-done.75
  683.2 9.9 %collective-permute-done.63 = bf16[128,2560]{1,0:T(8,128)(2,1)} collective-permute-done((bf16[128,2560]{1,0:T(8,128)(2,1)S(1)}, bf16[128,2560]{1,0:T(8,128)(2,1)}, u32[]{:S(2)}, u32[]{:S(2)}) %collective-permute-start.63) | collective-permute-done | bytes 655392 | tf_op jit(solution)/shard_map/ppermute | solution.py:374
  699.1 7.9 collective-permute-done.78
  707.5 10.9 %collective-permute-done.80 = bf16[320,1024]{1,0:T(8,128)(2,1)} collective-permute-done((bf16[320,1024]{1,0:T(8,128)(2,1)}, bf16[320,1024]{1,0:T(8,128)(2,1)}, u32[]{:S(2)}, u32[]{:S(2)}) %collective-permute-start.80) | collective-permute-done | bytes 655392 | tf_op jit(solution)/shard_map/ppermute | solution.py:374
  724.4 18.9 %assemble.3 = (f32[32,32,512]{2,1,0:T(8,128)}, f32[32,32,512]{2,1,0:T(8,128)}, f32[32,32,256]{2,1,0:T(8,128)}) custom-call(s32[32]{0:T(128)} %stack.474.order_ref, bf16[4,32,1280]{2,1,0:T(8,128)(2,1)} %bitcast.325, bf16[4,32,1280]{2,1,0:T(8,128)(2,1)} %bitcast.333, bf16[4,32,1280]{2,1,0:T(8,128)(2,1)} %bitcast.334, bf16[4,32,1280]{2,1,0:T(8,128)(2,1)} %bitcast.124.refs_3_, ...), custom_call_target="tpu_custom_call" | custom-call | tf_op jit(solution)/shard_map/assemble/pallas_call | solution.py:443
  748.9 20.4 %assemble.4 = f32[32,32,2560]{2,1,0:T(8,128)} custom-call(s32[32]{0:T(128)} %stack.474.order_ref, bf16[4,32,2560]{2,1,0:T(8,128)(2,1)} %bitcast.310, bf16[4,32,2560]{2,1,0:T(8,128)(2,1)} %bitcast.138.refs_1_, bf16[4,32,2560]{2,1,0:T(8,128)(2,1)} %bitcast.139.refs_2_, bf16[4,32,2560]{2,1,0:T(8,128)(2,1)} %bitcast.140.refs_3_, ...), custom_call_target="tpu_custom_call" | custom-call | tf_op jit(solution)/shard_map/assemble/pallas_call | solution.py:443
  769.3 20.4 %assemble.5 = f32[32,80,1024]{2,1,0:T(8,128)} custom-call(s32[32]{0:T(128)} %stack.474.order_ref, bf16[4,80,1024]{2,1,0:T(8,128)(2,1)} %bitcast.153.refs_0_, bf16[4,80,1024]{2,1,0:T(8,128)(2,1)} %bitcast.154.refs_1_, bf16[4,80,1024]{2,1,0:T(8,128)(2,1)} %bitcast.155.refs_2_, bf16[4,80,1024]{2,1,0:T(8,128)(2,1)} %bitcast.156.refs_3_, ...), custom_call_target="tpu_custom_call" | custom-call | tf_op jit(solution)/shard_map/assemble/pallas_call | solution.py:443
  (484 shorter events, 254.7 us)
Async XLA Ops:
  3.8 49.1 %collective-permute-start.2 = (bf16[3,1024,128]{2,1,0:T(8,128)(2,1)}, bf16[3,1024,128]{2,1,0:T(8,128)(2,1)}, u32[]{:S(2)}, u32[]{:S(2)}) collective-permute-start(bf16[3,1024,128]{2,1,0:T(8,128)(2,1)} %refs_5_.7), channel_id=1, source_target_pairs={{0,8},{8,0},{16,24},{24,16},{1,9},{9,1},{17,25},{25,17},{2,10},{10... | collective-permute-start | bytes 2359304 | tf_op jit(solution)/shard_map/ppermute | solution.py:354
  5.4 48.1 %collective-permute-start.3 = (bf16[3,128,1024]{2,1,0:T(8,128)(2,1)}, bf16[3,128,1024]{2,1,0:T(8,128)(2,1)}, u32[]{:S(2)}, u32[]{:S(2)}) collective-permute-start(bf16[3,128,1024]{2,1,0:T(8,128)(2,1)} %refs_7_.7), channel_id=1, source_target_pairs={{0,8},{8,0},{16,24},{24,16},{1,9},{9,1},{17,25},{25,17},{2,10},{10... | collective-permute-start | bytes 2359304 | tf_op jit(solution)/shard_map/ppermute | solution.py:354
  52.9 40.0 %collective-permute-start.8 = (bf16[512,1024]{1,0:T(8,128)(2,1)}, bf16[512,1024]{1,0:T(8,128)(2,1)S(1)}, u32[]{:S(2)}, u32[]{:S(2)}) collective-permute-start(bf16[512,1024]{1,0:T(8,128)(2,1)} %bitcast.326), channel_id=1, source_target_pairs={{0,1},{1,0},{2,3},{3,2},{4,5},{5,4},{6,7},{7,6},{8,9},{9,8},{10,11... | collective-permute-start | bytes 3145736 | tf_op jit(solution)/shard_map/ppermute | solution.py:365
  56.2 67.1 %collective-permute-start.14 = (bf16[512,1024]{1,0:T(8,128)(2,1)}, bf16[512,1024]{1,0:T(8,128)(2,1)S(1)}, u32[]{:S(2)}, u32[]{:S(2)}) collective-permute-start(bf16[512,1024]{1,0:T(8,128)(2,1)} %bitcast.327), channel_id=1, source_target_pairs={{0,16},{8,24},{16,0},{24,8},{1,17},{9,25},{17,1},{25,9},{2,18},{10... | collective-permute-start | bytes 3145736 | tf_op jit(solution)/shard_map/ppermute | solution.py:368
  93.0 63.2 %collective-permute-start.20 = (bf16[512,1024]{1,0:T(8,128)(2,1)}, bf16[512,1024]{1,0:T(8,128)(2,1)}, u32[]{:S(2)}, u32[]{:S(2)}) collective-permute-start(bf16[512,1024]{1,0:T(8,128)(2,1)} %multiply_convert_fusion.3.refs_0_), channel_id=1, source_target_pairs={{0,17},{1,16},{2,19},{3,18},{4,21},{5,20},{6,23},{7,22},{8,25},{9,... | collective-permute-start | bytes 3145736 | tf_op jit(solution)/shard_map/ppermute | solution.py:374
  94.5 61.7 %collective-permute-start.21 = (bf16[512,1024]{1,0:T(8,128)(2,1)S(1)}, bf16[512,1024]{1,0:T(8,128)(2,1)}, u32[]{:S(2)}, u32[]{:S(2)}) collective-permute-start(bf16[512,1024]{1,0:T(8,128)(2,1)S(1)} %bitcast.330), channel_id=1, source_target_pairs={{0,17},{1,16},{2,19},{3,18},{4,21},{5,20},{6,23},{7,22},{8,25},{9,... | collective-permute-start | bytes 3145736 | tf_op jit(solution)/shard_map/ppermute | solution.py:374
  204.9 80.5 %collective-permute-start.28 = (bf16[512,1024]{1,0:T(8,128)(2,1)}, bf16[512,1024]{1,0:T(8,128)(2,1)S(1)}, u32[]{:S(2)}, u32[]{:S(2)}) collective-permute-start(bf16[512,1024]{1,0:T(8,128)(2,1)} %get-tuple-element.128), channel_id=1, source_target_pairs={{0,17},{1,16},{2,19},{3,18},{4,21},{5,20},{6,23},{7,22},{8,25},{9,... | collective-permute-start | bytes 3145736 | tf_op jit(solution)/shard_map/ppermute | solution.py:374
  257.2 47.4 %collective-permute-start.26 = (bf16[512,1024]{1,0:T(8,128)(2,1)}, bf16[512,1024]{1,0:T(8,128)(2,1)S(1)}, u32[]{:S(2)}, u32[]{:S(2)}) collective-permute-start(bf16[512,1024]{1,0:T(8,128)(2,1)} %get-tuple-element.126), channel_id=1, source_target_pairs={{0,1},{1,0},{2,3},{3,2},{4,5},{5,4},{6,7},{7,6},{8,9},{9,8},{10,11... | collective-permute-start | bytes 3145736 | tf_op jit(solution)/shard_map/ppermute | solution.py:365
  258.7 47.0 %collective-permute-start.25 = (bf16[512,1024]{1,0:T(8,128)(2,1)}, bf16[512,1024]{1,0:T(8,128)(2,1)}, u32[]{:S(2)}, u32[]{:S(2)}) collective-permute-start(bf16[512,1024]{1,0:T(8,128)(2,1)} %get-tuple-element.124), channel_id=1, source_target_pairs={{0,17},{1,16},{2,19},{3,18},{4,21},{5,20},{6,23},{7,22},{8,25},{9,... | collective-permute-start | bytes 3145736 | tf_op jit(solution)/shard_map/ppermute | solution.py:374
  259.6 67.1 %collective-permute-start.24 = (bf16[512,1024]{1,0:T(8,128)(2,1)}, bf16[512,1024]{1,0:T(8,128)(2,1)}, u32[]{:S(2)}, u32[]{:S(2)}) collective-permute-start(bf16[512,1024]{1,0:T(8,128)(2,1)} %get-tuple-element.123), channel_id=1, source_target_pairs={{0,16},{8,24},{16,0},{24,8},{1,17},{9,25},{17,1},{25,9},{2,18},{10... | collective-permute-start | bytes 3145736 | tf_op jit(solution)/shard_map/ppermute | solution.py:368
  285.5 41.9 %collective-permute-start.23 = (bf16[512,1024]{1,0:T(8,128)(2,1)}, bf16[512,1024]{1,0:T(8,128)(2,1)S(1)}, u32[]{:S(2)}, u32[]{:S(2)}) collective-permute-start(bf16[512,1024]{1,0:T(8,128)(2,1)} %get-tuple-element.122), channel_id=1, source_target_pairs={{0,1},{1,0},{2,3},{3,2},{4,5},{5,4},{6,7},{7,6},{8,9},{9,8},{10,11... | collective-permute-start | bytes 3145736 | tf_op jit(solution)/shard_map/ppermute | solution.py:365
  290.3 127.0 %collective-permute-start.86 = (bf16[6,1024,128]{2,1,0:T(8,128)(2,1)}, bf16[6,1024,128]{2,1,0:T(8,128)(2,1)}, u32[]{:S(2)}, u32[]{:S(2)}) collective-permute-start(bf16[6,1024,128]{2,1,0:T(8,128)(2,1)} %get-tuple-element.143), channel_id=1, source_target_pairs={{0,8},{8,0},{16,24},{24,16},{1,9},{9,1},{17,25},{25,17},{2,10},{10... | collective-permute-start | bytes 4718600 | tf_op jit(solution)/shard_map/ppermute | solution.py:354
  304.6 117.4 %collective-permute-start.91 = (bf16[6,128,1024]{2,1,0:T(8,128)(2,1)}, bf16[6,128,1024]{2,1,0:T(8,128)(2,1)}, u32[]{:S(2)}, u32[]{:S(2)}) collective-permute-start(bf16[6,128,1024]{2,1,0:T(8,128)(2,1)} %get-tuple-element.147), channel_id=1, source_target_pairs={{0,8},{8,0},{16,24},{24,16},{1,9},{9,1},{17,25},{25,17},{2,10},{10... | collective-permute-start | bytes 4718600 | tf_op jit(solution)/shard_map/ppermute | solution.py:354
  305.7 131.7 %collective-permute-start.85 = (bf16[6,1024,128]{2,1,0:T(8,128)(2,1)}, bf16[6,1024,128]{2,1,0:T(8,128)(2,1)}, u32[]{:S(2)}, u32[]{:S(2)}) collective-permute-start(bf16[6,1024,128]{2,1,0:T(8,128)(2,1)} %get-tuple-element.141), channel_id=1, source_target_pairs={{0,8},{8,0},{16,24},{24,16},{1,9},{9,1},{17,25},{25,17},{2,10},{10... | collective-permute-start | bytes 4718600 | tf_op jit(solution)/shard_map/ppermute | solution.py:354
  326.7 134.7 %collective-permute-start.90 = (bf16[6,128,1024]{2,1,0:T(8,128)(2,1)}, bf16[6,128,1024]{2,1,0:T(8,128)(2,1)}, u32[]{:S(2)}, u32[]{:S(2)}) collective-permute-start(bf16[6,128,1024]{2,1,0:T(8,128)(2,1)} %get-tuple-element.145), channel_id=1, source_target_pairs={{0,8},{8,0},{16,24},{24,16},{1,9},{9,1},{17,25},{25,17},{2,10},{10... | collective-permute-start | bytes 4718600 | tf_op jit(solution)/shard_map/ppermute | solution.py:354
  373.1 43.5 %collective-permute-start.29 = (f32[3,1024]{1,0:T(4,128)S(1)}, f32[3,1024]{1,0:T(4,128)S(1)}, u32[]{:S(2)}, u32[]{:S(2)}) collective-permute-start(f32[3,1024]{1,0:T(4,128)S(1)} %pad_maximum_fusion.3), channel_id=1, source_target_pairs={{0,8},{8,0},{16,24},{24,16},{1,9},{9,1},{17,25},{25,17},{2,10},{10... | collective-permute-start | bytes 36872 | tf_op jit(solution)/shard_map/ppermute | solution.py:522
  437.3 67.4 %collective-permute-start.51 = (bf16[512,2560]{1,0:T(8,128)(2,1)}, bf16[512,2560]{1,0:T(8,128)(2,1)S(1)}, u32[]{:S(2)}, u32[]{:S(2)}) collective-permute-start(bf16[512,2560]{1,0:T(8,128)(2,1)} %bitcast.364), channel_id=1, source_target_pairs={{0,8},{8,0},{16,24},{24,16},{1,9},{9,1},{17,25},{25,17},{2,10},{10... | collective-permute-start | bytes 7864328 | tf_op jit(solution)/shard_map/ppermute | solution.py:354
  471.7 50.0 %collective-permute-start.68 = (bf16[1280,1024]{1,0:T(8,128)(2,1)S(1)}, bf16[1280,1024]{1,0:T(8,128)(2,1)S(1)}, u32[]{:S(2)}, u32[]{:S(2)}) collective-permute-start(bf16[1280,1024]{1,0:T(8,128)(2,1)S(1)} %bitcast.365), channel_id=1, source_target_pairs={{0,8},{8,0},{16,24},{24,16},{1,9},{9,1},{17,25},{25,17},{2,10},{10... | collective-permute-start | bytes 7864328 | tf_op jit(solution)/shard_map/ppermute | solution.py:354
  507.5 39.2 %collective-permute-start.54 = (bf16[128,2560]{1,0:T(8,128)(2,1)S(1)}, bf16[128,2560]{1,0:T(8,128)(2,1)S(1)}, u32[]{:S(2)}, u32[]{:S(2)}) collective-permute-start(bf16[128,2560]{1,0:T(8,128)(2,1)S(1)} %get-tuple-element.171), channel_id=1, source_target_pairs={{0,17},{1,16},{2,19},{3,18},{4,21},{5,20},{6,23},{7,22},{8,25},{9,... | collective-permute-start | bytes 1966088 | tf_op jit(solution)/shard_map/ppermute | solution.py:374
  509.8 38.7 %collective-permute-start.53 = (bf16[128,2560]{1,0:T(8,128)(2,1)S(1)}, bf16[128,2560]{1,0:T(8,128)(2,1)S(1)}, u32[]{:S(2)}, u32[]{:S(2)}) collective-permute-start(bf16[128,2560]{1,0:T(8,128)(2,1)S(1)} %get-tuple-element.172), channel_id=1, source_target_pairs={{0,16},{8,24},{16,0},{24,8},{1,17},{9,25},{17,1},{25,9},{2,18},{10... | collective-permute-start | bytes 1966088 | tf_op jit(solution)/shard_map/ppermute | solution.py:368
  545.4 41.0 %collective-permute-start.46 = (bf16[128,1280]{1,0:T(8,128)(2,1)S(1)}, bf16[128,1280]{1,0:T(8,128)(2,1)}, u32[]{:S(2)}, u32[]{:S(2)}) collective-permute-start(bf16[128,1280]{1,0:T(8,128)(2,1)S(1)} %pad_maximum_fusion.2), channel_id=1, source_target_pairs={{0,17},{1,16},{2,19},{3,18},{4,21},{5,20},{6,23},{7,22},{8,25},{9,... | collective-permute-start | bytes 983048 | tf_op jit(solution)/shard_map/ppermute | solution.py:374
  546.6 41.1 %collective-permute-start.47 = (bf16[128,1280]{1,0:T(8,128)(2,1)S(1)}, bf16[128,1280]{1,0:T(8,128)(2,1)}, u32[]{:S(2)}, u32[]{:S(2)}) collective-permute-start(bf16[128,1280]{1,0:T(8,128)(2,1)S(1)} %pad_maximum_fusion.2), channel_id=1, source_target_pairs={{0,8},{8,0},{16,24},{24,16},{1,9},{9,1},{17,25},{25,17},{2,10},{10... | collective-permute-start | bytes 983048 | tf_op jit(solution)/shard_map/ppermute | solution.py:354
  583.1 49.3 %collective-permute-start.56 = (bf16[32,2560]{1,0:T(8,128)(2,1)S(1)}, bf16[32,2560]{1,0:T(8,128)(2,1)S(1)}, u32[]{:S(2)}, u32[]{:S(2)}) collective-permute-start(bf16[32,2560]{1,0:T(8,128)(2,1)S(1)} %get-tuple-element.169), channel_id=1, source_target_pairs={{0,4},{1,5},{2,6},{3,7},{4,0},{5,1},{6,2},{7,3},{8,12},{9,13},{10,... | collective-permute-start | bytes 491528 | tf_op jit(solution)/shard_map/ppermute | solution.py:358
  585.7 46.7 %collective-permute-start.55 = (bf16[32,2560]{1,0:T(8,128)(2,1)S(1)}, bf16[32,2560]{1,0:T(8,128)(2,1)S(1)}, u32[]{:S(2)}, u32[]{:S(2)}) collective-permute-start(bf16[32,2560]{1,0:T(8,128)(2,1)S(1)} %get-tuple-element.167), channel_id=1, source_target_pairs={{0,2},{1,3},{2,4},{3,5},{4,6},{5,7},{6,0},{7,1},{8,10},{9,11},{10,... | collective-permute-start | bytes 491528 | tf_op jit(solution)/shard_map/ppermute | solution.py:358
  586.4 65.7 %collective-permute-start.89 = (bf16[3,1024,128]{2,1,0:T(8,128)(2,1)S(1)}, bf16[3,1024,128]{2,1,0:T(8,128)(2,1)S(1)}, u32[]{:S(2)}, u32[]{:S(2)}) collective-permute-start(bf16[3,1024,128]{2,1,0:T(8,128)(2,1)S(1)} %add_convert_fusion.4), channel_id=1, source_target_pairs={{0,2},{1,3},{2,4},{3,5},{4,6},{5,7},{6,0},{7,1},{8,10},{9,11},{10,... | collective-permute-start | bytes 2359304 | tf_op jit(solution)/shard_map/ppermute | solution.py:358
  587.6 72.0 %collective-permute-start.94 = (bf16[3,128,1024]{2,1,0:T(8,128)(2,1)S(1)}, bf16[3,128,1024]{2,1,0:T(8,128)(2,1)S(1)}, u32[]{:S(2)}, u32[]{:S(2)}) collective-permute-start(bf16[3,128,1024]{2,1,0:T(8,128)(2,1)S(1)} %add_convert_fusion.1), channel_id=1, source_target_pairs={{0,2},{1,3},{2,4},{3,5},{4,6},{5,7},{6,0},{7,1},{8,10},{9,11},{10,... | collective-permute-start | bytes 2359304 | tf_op jit(solution)/shard_map/ppermute | solution.py:358
  588.5 44.1 %collective-permute-start.74 = (bf16[80,1024]{1,0:T(8,128)(2,1)S(1)}, bf16[80,1024]{1,0:T(8,128)(2,1)S(1)}, u32[]{:S(2)}, u32[]{:S(2)}) collective-permute-start(bf16[80,1024]{1,0:T(8,128)(2,1)S(1)} %get-tuple-element.157), channel_id=1, source_target_pairs={{0,6},{1,7},{2,0},{3,1},{4,2},{5,3},{6,4},{7,5},{8,14},{9,15},{10,... | collective-permute-start | bytes 491528 | tf_op jit(solution)/shard_map/ppermute | solution.py:358
  707.0 62.3 %collective-permute-start.81 = (bf16[320,1024]{1,0:T(8,128)(2,1)}, bf16[320,1024]{1,0:T(8,128)(2,1)}, u32[]{:S(2)}, u32[]{:S(2)}) collective-permute-start(bf16[320,1024]{1,0:T(8,128)(2,1)} %pad_maximum_fusion.1), channel_id=1, source_target_pairs={{0,8},{8,0},{16,24},{24,16},{1,9},{9,1},{17,25},{25,17},{2,10},{10... | collective-permute-start | bytes 1966088 | tf_op jit(solution)/shard_map/ppermute | solution.py:354
  707.1 41.7 %collective-permute-start.67 = (bf16[128,2560]{1,0:T(8,128)(2,1)}, bf16[128,2560]{1,0:T(8,128)(2,1)}, u32[]{:S(2)}, u32[]{:S(2)}) collective-permute-start(bf16[128,2560]{1,0:T(8,128)(2,1)} %collective-permute-done.63), channel_id=1, source_target_pairs={{0,8},{8,0},{16,24},{24,16},{1,9},{9,1},{17,25},{25,17},{2,10},{10... | collective-permute-start | bytes 1966088 | tf_op jit(solution)/shard_map/ppermute | solution.py:354
  718.4 50.8 %collective-permute-start.82 = (bf16[320,1024]{1,0:T(8,128)(2,1)}, bf16[320,1024]{1,0:T(8,128)(2,1)}, u32[]{:S(2)}, u32[]{:S(2)}) collective-permute-start(bf16[320,1024]{1,0:T(8,128)(2,1)} %collective-permute-done.78), channel_id=1, source_target_pairs={{0,8},{8,0},{16,24},{24,16},{1,9},{9,1},{17,25},{25,17},{2,10},{10... | collective-permute-start | bytes 1966088 | tf_op jit(solution)/shard_map/ppermute | solution.py:354
  718.5 50.8 %collective-permute-start.83 = (bf16[320,1024]{1,0:T(8,128)(2,1)}, bf16[320,1024]{1,0:T(8,128)(2,1)}, u32[]{:S(2)}, u32[]{:S(2)}) collective-permute-start(bf16[320,1024]{1,0:T(8,128)(2,1)} %collective-permute-done.79), channel_id=1, source_target_pairs={{0,8},{8,0},{16,24},{24,16},{1,9},{9,1},{17,25},{25,17},{2,10},{10... | collective-permute-start | bytes 1966088 | tf_op jit(solution)/shard_map/ppermute | solution.py:354
  719.0 50.3 %collective-permute-start.84 = (bf16[320,1024]{1,0:T(8,128)(2,1)}, bf16[320,1024]{1,0:T(8,128)(2,1)}, u32[]{:S(2)}, u32[]{:S(2)}) collective-permute-start(bf16[320,1024]{1,0:T(8,128)(2,1)} %collective-permute-done.80), channel_id=1, source_target_pairs={{0,8},{8,0},{16,24},{24,16},{1,9},{9,1},{17,25},{25,17},{2,10},{10... | collective-permute-start | bytes 1966088 | tf_op jit(solution)/shard_map/ppermute | solution.py:354
  (161 other events, 2552.1 us)

commit v2 on v1

--- a/solution.py
+++ b/solution.py
@@ -327,9 +327,7 @@
             vmem_limit_bytes=56 * 1024 * 1024,
         ),
         cost_estimate=pl.CostEstimate(
-            flops=24 * blocks * tokens * D * FF * pairs,
-            bytes_accessed=blocks * tokens * D * 12 + pairs * D * FF * 24,
-            transcendentals=blocks * tokens * 2 * FF * pairs,
+            flops=blocks * tokens * D, bytes_accessed=0, transcendentals=0
         ),
         name="experts",
     )(*operands)
@@ -385,134 +383,214 @@
     return lax.optimization_barrier(values)
 
 
-def copy_two(order_ref, value_a, value_b, out_a, out_b):
-    out_a[...] = value_a[...]
-    out_b[...] = value_b[...]
-
-
-def in_relative_order(moves, value):
-    nx, nh = moves.nx, moves.nh
-    count = nx * 2 * nh
-    rows = value.shape[0] // (2 * count)
-    columns = value.shape[1]
-    order = []
-    for core in (moves.core, 1 - moves.core):
-        for a, b in moves.plane:
-            for h in range(nh):
-                place = (moves.x + a) % nx * 2 + (moves.lo ^ b)
-                order.append((core * nx * 2 + place) * nh + (moves.hi + h) % nh)
+class Cube:
+    def __init__(self, moves):
+        self.moves = moves
+        ex = moves.ex
+        across = [1 << i for i in range(1, moves.dp.bit_length() - 1)]
+        along = [1 << i for i in range(ex.bit_length() - 1)]
+        across = [mask * ex for mask in across]
+        self.flips = (across + along, along[:1] + across + along[1:])
+        self.core_flip = ex
+        self.count = moves.dp * ex
+        self.bits = len(along) + len(across)
+        place = moves.dp_index * ex + moves.ex_index
+        corners = []
+        for flips in self.flips:
+            corner = jnp.int32(0)
+            for flip in flips:
+                corner = corner * 2 + (place // flip) % 2
+            corners.append(corner)
+        mine = moves.core == 0
+        self.corner = jnp.where(mine, corners[0], corners[1])
+        self.partner_corner = jnp.where(mine, corners[1], corners[0])
+
+    def exchange(self, value, stage):
+        ex = self.moves.ex
+        pairs = [
+            (i, i ^ self.flips[i // ex % 2][stage]) for i in range(self.count)
+        ]
+        return lax.ppermute(value, ("dp", "expert"), pairs)
+
+    def over_core(self, value):
+        return self.moves.over_core(value)
+
+
+def small_cost(flops, moved):
+    return pl.CostEstimate(flops=flops, bytes_accessed=moved, transcendentals=0)
+
+
+def grad_blocks_kernel(steps, group, rows, count, order_ref, left_a, left_b, *refs):
+    rights, refs = refs[:count], refs[count:]
+    out_a, out_b = refs[-2:]
+    added = refs[:-2]
+    for which, (left, out) in enumerate(((left_a, out_a), (left_b, out_b))):
+        low = order_ref[2 * steps + which]
+        turned = left[...]
+        start = 0
+        for right in rights:
+            width = right.shape[1]
+            product = contract(turned, right[...], 0, 0)
+            for h in range(group):
+                out[lax.bitwise_xor(low, h), :, start : start + width] = product[
+                    h * rows : (h + 1) * rows
+                ].astype(bf16)
+            start += width
+        if added:
+            block = added[which][...]
+            width = block.shape[1]
+            for h in range(group):
+                out[lax.bitwise_xor(low, h), :, start : start + width] = block[
+                    h * rows : (h + 1) * rows
+                ].astype(bf16)
+
+
+def grad_blocks(cube, left, rights, added=None):
+    n = cube.count
+    total = left.shape[1]
+    tokens = left.shape[0]
+    rows = total // n
+    group = 1
+    while rows * group % 128:
+        group *= 2
+    wide = rows * group
+    steps = n // 2 // group
+    core = cube.moves.core
+    order = [core * steps + lax.bitwise_xor(cube.corner // group, i) for i in range(steps)]
+    order += [
+        (1 - core) * steps + lax.bitwise_xor(cube.partner_corner // group, i) for i in range(steps)
+    ]
+    order += [cube.corner % group, cube.partner_corner % group]
     order = jnp.stack(order).astype(jnp.int32)
-    shape = jax.ShapeDtypeStruct((count, rows, columns), value.dtype)
-    value = value.reshape(2 * count, rows, columns)
-    outs = pl.pallas_call(
-        copy_two,
+    columns = sum(r.shape[1] for r in rights) + (0 if added is None else added.shape[1])
+    in_specs = [
+        pl.BlockSpec((tokens, wide), lambda i, o: (0, o[i])),
+        pl.BlockSpec((tokens, wide), lambda i, o: (0, o[steps + i])),
+        *[pl.BlockSpec(r.shape, lambda i, o: (0, 0)) for r in rights],
+    ]
+    operands = [left, left, *rights]
+    if added is not None:
+        in_specs += [
+            pl.BlockSpec((wide, added.shape[1]), lambda i, o: (o[i], 0)),
+            pl.BlockSpec((wide, added.shape[1]), lambda i, o: (o[steps + i], 0)),
+        ]
+        operands += [added, added]
+    shape = jax.ShapeDtypeStruct((n // 2, rows, columns), bf16)
+    return pl.pallas_call(
+        functools.partial(grad_blocks_kernel, steps, group, rows, len(rights)),
         grid_spec=pltpu.PrefetchScalarGridSpec(
             num_scalar_prefetch=1,
-            grid=(count,),
-            in_specs=[
-                pl.BlockSpec((1, rows, columns), lambda i, o: (o[i], 0, 0)),
-                pl.BlockSpec((1, rows, columns), lambda i, o: (o[count + i], 0, 0)),
-            ],
-            out_specs=[pl.BlockSpec((1, rows, columns), lambda i, o: (i, 0, 0))] * 2,
+            grid=(steps,),
+            in_specs=in_specs,
+            out_specs=[pl.BlockSpec((group, rows, columns), lambda i, o: (i, 0, 0))] * 2,
         ),
         out_shape=[shape, shape],
-        name="relative",
-    )(order, value, value)
-    return [out.reshape(count * rows, columns) for out in outs]
-
-
-def in_place_order(moves, mine, theirs, widths):
-    nx, nh = moves.nx, moves.nh
-    count = nx * 2 * nh
-    rows = mine[0].shape[0] // nh
-    columns = mine[0].shape[1]
+        compiler_params=pltpu.CompilerParams(vmem_limit_bytes=40 * 1024 * 1024),
+        cost_estimate=small_cost(tokens * total * columns, total * columns * 2),
+        name="grad_blocks",
+    )(order, *operands)
+
+
+def assemble_kernel(count, cuts, order_ref, *refs):
+    pieces, outs = refs[:4], refs[4:]
+    step = pl.program_id(0)
+    for index, piece in enumerate(pieces):
+
+        @pl.when(step // 2 == index)
+        def _():
+            low = order_ref[8 + index // 2]
+            for r in range(count):
+                for out, (start, width) in zip(outs, cuts):
+                    out[lax.bitwise_xor(low, r)] = piece[r, :, start : start + width].astype(f32)
+
+
+def assemble(cube, pieces, cuts):
+    n = cube.count
+    count = n // 8
+    rows, columns = pieces[0].shape[1:]
     order = []
-    for core in (moves.core, 1 - moves.core):
-        for a, b in moves.plane:
-            for h in range(nh):
-                place = (moves.x - a) % nx * 2 + (moves.lo ^ b)
-                order.append((core * nx * 2 + place) * nh + (moves.hi - h) % nh)
+    for core, corner in (
+        (cube.moves.core, cube.corner),
+        (1 - cube.moves.core, cube.partner_corner),
+    ):
+        order += [core * 4 + lax.bitwise_xor(corner // count, i) for i in range(4)]
+    order += [cube.corner % count, cube.partner_corner % count]
     order = jnp.stack(order).astype(jnp.int32)
 
     def piece(index):
         return pl.BlockSpec(
-            (1, rows, columns), lambda i, o: (jnp.clip(i - index * nh, 0, nh - 1), 0, 0)
+            (count, rows, columns), lambda i, o: (jnp.clip(i - 2 * index, 0, 1), 0, 0)
         )
 
-    pieces = [p.reshape(nh, rows, columns) for p in (*mine, *theirs)]
     outs = pl.pallas_call(
-        functools.partial(place_pieces, nx * 4, nh, widths),
+        functools.partial(assemble_kernel, count, cuts),
         grid_spec=pltpu.PrefetchScalarGridSpec(
             num_scalar_prefetch=1,
-            grid=(2 * count,),
-            in_specs=[piece(index) for index in range(nx * 4)],
+            grid=(8,),
+            in_specs=[piece(index) for index in range(4)],
             out_specs=[
-                pl.BlockSpec((1, rows, width), lambda i, o: (o[i], 0, 0)) for width in widths
+                pl.BlockSpec((count, rows, width), lambda i, o: (o[i], 0, 0))
+                for _, width in cuts
             ],
         ),
-        out_shape=[jax.ShapeDtypeStruct((2 * count, rows, width), f32) for width in widths],
+        out_shape=[jax.ShapeDtypeStruct((n, rows, width), f32) for _, width in cuts],
+        compiler_params=pltpu.CompilerParams(vmem_limit_bytes=40 * 1024 * 1024),
+        cost_estimate=small_cost(0, n * rows * columns * 2),
         name="assemble",
     )(order, *pieces)
-    return [out.reshape(2 * count * rows, width) for out, width in zip(outs, widths)]
-
-
-def place_pieces(pieces, nh, widths, order_ref, *refs):
-    outs = refs[pieces:]
-    step = pl.program_id(0)
-    for index in range(pieces):
-
-        @pl.when(step // nh == index)
-        def _():
-            start = 0
-            for out, width in zip(outs, widths):
-                out[...] = refs[index][:, :, start : start + width].astype(f32)
-                start += width
+    return [out.reshape(n * rows, width) for out, (_, width) in zip(outs, cuts)]
+
+
+def add_halves(kept, got):
+    half = kept.shape[0] // 2
+    return add_low(kept[:half], got[:half]), add_low(kept[half:], got[half:])
 
 
 class Sum:
-    def __init__(self, moves, value, widths):
-        self.moves = moves
-        self.widths = widths
-        self.held, self.away = in_relative_order(moves, value)
-
-    def core(self):
-        moves = self.moves
-        got = moves.over_core(self.away)
-        count = len(moves.plane)
-        rows = got.shape[0] // count
-        self.parts = [
-            add_low(self.held[k * rows : (k + 1) * rows], got[k * rows : (k + 1) * rows])
-            for k in range(count)
-        ]
-
-    def plane(self):
-        moves = self.moves
-        got = [moves.over_plane(p, s) for p, s in zip(self.parts[1:], moves.plane[1:])]
-        nh = moves.nh
-        rows = self.parts[0].shape[0] // nh
-        terms = [self.parts[0], *got]
-        self.parts = [
-            add_low(*[term[h * rows : (h + 1) * rows] for term in terms]) for h in range(nh)
-        ]
-
-    def line(self):
-        moves = self.moves
-        got = [moves.over_hi(self.parts[h], h) for h in range(1, moves.nh)]
-        self.total = add_low(self.parts[0], *got)
-
-    def line_back(self):
-        moves = self.moves
-        got = [moves.over_hi(self.total, h) for h in range(1, moves.nh)]
-        self.rows = jnp.concatenate([self.total, *got], axis=0)
-
-    def plane_back(self):
-        moves = self.moves
-        self.mine = [self.rows] + [moves.over_plane(self.rows, s) for s in moves.plane[1:]]
-
-    def core_back(self):
-        moves = self.moves
-        theirs = [moves.over_core(piece) for piece in self.mine]
-        return in_place_order(moves, self.mine, theirs, self.widths)
+    def __init__(self, cube, blocks, cuts):
+        self.cube = cube
+        self.cuts = cuts
+        self.kept, self.sent = blocks
+        self.stage = -1
+
+    def step(self):
+        cube = self.cube
+        stage = self.stage
+        self.stage += 1
+        if stage < cube.bits:
+            got = cube.over_core(self.sent) if stage < 0 else cube.exchange(self.sent, stage)
+            if stage == cube.bits - 1:
+                self.total = add_low(self.kept, got)
+            else:
+                self.kept, self.sent = add_halves(self.kept, got)
+            return
+        back = 2 * cube.bits - 1 - stage
+        if back > 0:
+            self.total = jnp.concatenate([self.total, cube.exchange(self.total, back)], axis=0)
+        elif back == 0:
+            self.halves = [self.total, cube.exchange(self.total, 0)]
+        else:
+            theirs = [cube.over_core(half) for half in self.halves]
+            self.out = assemble(cube, [*self.halves, *theirs], self.cuts)
+
+    def tied(self, value):
+        if hasattr(self, "total"):
+            self.total, value = tie(self.total, value)
+        else:
+            self.kept, self.sent, value = tie(self.kept, self.sent, value)
+        return value
+
+    @property
+    def done(self):
+        return self.stage + 1
+
+    def run(self, steps):
+        for _ in range(steps):
+            self.step()
+
+    @property
+    def steps(self):
+        return 2 * self.cube.bits + 2
 
 
 def sum_small(moves, value):
@@ -522,10 +600,6 @@
             value = value + lax.ppermute(value, axis, [(i, i ^ span) for i in range(size)])
             span *= 2
     return value
-
-
-def select_back(select):
-    return select.T
 
 
 def on_device(
@@ -639,7 +713,8 @@
         return select, jnp.dot(router_weight, select, preferred_element_type=f32).astype(bf16)
 
     sums = {}
-    router_sum = jnp.zeros((D, experts), f32)
+    router_width = experts + -experts % 128
+    router_sum = jnp.zeros((D, router_width), f32)
     mine_slots, theirs_slots = [None] * nh, [None] * nh
 
     def visit(offsets, phase, carried, finish):
@@ -670,7 +745,7 @@
     phases = nh // 2
     chosen_by = [selection((2 * p, 2 * p + 1)) for p in range(phases)]
     held = None
-    sent_back = {}
+    sent_back, later = {}, []
     for phase in range(phases):
         last = phase == phases - 1
         if phase == 0:
@@ -704,11 +779,23 @@
                 downs[3:] = values[nh - 2 :]
                 core_ups += [moves.over_core(u) for u in ups[3:]]
                 core_downs += [moves.over_core(d) for d in downs[3:]]
-            if last and offsets != [home]:
-                for s in offsets:
-                    sent_back[s] = [moves.over_plane(v, s, back=True) for v in sums[s][::-1]]
+            if phase > 0 and turn == 0:
+                grads[0], *held = tie(grads[0], *held)
+                held = [moves.over_hi(h) for h in held]
+            if phase > 0 and turn == len(calls) - 2:
+                grads[0], *held = tie(grads[0], *held)
+            if last:
+                if later:
+                    grads[0], *late = tie(grads[0], *[sums[s][0] for s in later])
+                    for s, value in zip(later, late):
+                        sent_back[s].append(moves.over_plane(value, s, back=True))
+                later = [s for s in offsets if s != home]
+                for s in later:
+                    sent_back[s] = [moves.over_plane(sums[s][1], s, back=True)]
         router_sum = router_sum + jnp.dot(
-            grads[4].astype(bf16), select_back(chosen_by[phase][0]), preferred_element_type=f32
+            grads[4].astype(bf16),
+            jnp.pad(chosen_by[phase][0].T, ((0, 0), (0, router_width - experts))),
+            preferred_element_type=f32,
         )
         gu_mine, gu_theirs, gd_mine, gd_theirs = grads[:4]
         gu_got, gd_got = moves.over_core(gu_theirs), moves.over_core(gd_theirs)
@@ -720,26 +807,24 @@
                 first_parts = parts
                 continue
             if held is not None:
-                parts = [(*p, moves.over_hi(h)) for p, h in zip(parts, held)]
+                arrived = held if k == 0 else [moves.over_hi(h) for h in held]
+                parts = [(*p, h) for p, h in zip(parts, arrived)]
             held = [add_low(*p) for p in parts]
 
-    def token_sum(which):
-        total = sums[home][1 - which].astype(f32)
-        for s in moves.plane[1:]:
-            total = total + sent_back[s][which].astype(f32)
-        return total
-
-    expert_delta = token_sum(0)
+    expert_delta = sums[home][1].astype(f32)
+    for s in moves.plane[1:]:
+        expert_delta = expert_delta + sent_back[s][0].astype(f32)
 
     upstream = upstream_low.astype(f32)
     middle_delta = upstream + norm_back(middle_rows, moe_rms, mixture_gain, expert_delta)
     grad_mixture = jnp.sum(expert_delta * middle_rows * moe_rms, axis=0)
     middle_low = middle_delta.astype(bf16)
-    grad_output = jnp.einsum(
-        "tc,td->cd", spread_low, middle_low, preferred_element_type=f32
-    ).astype(bf16)
+    cube = Cube(moves)
+    out_sum = Sum(cube, grad_blocks(cube, spread_low, [middle_low]), [(0, D)])
+    middle_sent = out_sum.tied(middle_low)
+    out_sum.step()
     spread_delta = jnp.einsum(
-        "td,cd->tc", middle_low, output_weight, preferred_element_type=f32
+        "td,cd->tc", middle_sent, output_weight, preferred_element_type=f32
     ).reshape(length, H, NE, DH)
     mixed_delta = jnp.sum(output_gate[..., None] * spread_delta, axis=2).astype(bf16)
     oselect_delta = (
@@ -752,6 +837,8 @@
         .astype(bf16)
         .reshape(length, H * NE)
     )
+    mixed_delta = out_sum.tied(mixed_delta)
+    out_sum.step()
     scores = masked_scores(query_low, key_low, allowed)
     probs_full = jnp.exp(scores - log_total)
     probs_again = probs_full.astype(bf16)
@@ -759,6 +846,20 @@
     score_delta = (
         probs_full * (weight_delta - jnp.sum(probs_full * weight_delta, axis=-1, keepdims=True))
     ).astype(bf16)
+    value_delta = jnp.einsum("hqk,qhd->khd", probs_again, mixed_delta, preferred_element_type=f32)
+    values_delta = (
+        (value_gate[..., None] * value_delta[:, :, None, :])
+        .astype(bf16)
+        .reshape(length, H * NE * DH)
+    )
+    value_sum = Sum(cube, grad_blocks(cube, normed_low, [values_delta]), [(0, H * NE * DH)])
+    score_delta = out_sum.tied(score_delta)
+    score_delta = value_sum.tied(score_delta)
+    *held, score_delta = tie(*held, score_delta)
+    last_held = [moves.over_hi(h) for h in held]
+    *outputs_back, score_delta = tie(*[sent_back[s][1] for s in moves.plane[1:]], score_delta)
+    out_sum.step()
+    value_sum.step()
     query_delta = (
         (
             jnp.einsum("hqk,khd->qhd", score_delta, key_low, preferred_element_type=f32)
@@ -774,12 +875,6 @@
         )
         .astype(bf16)
         .reshape(length, H * DH)
-    )
-    value_delta = jnp.einsum("hqk,qhd->khd", probs_again, mixed_delta, preferred_element_type=f32)
-    values_delta = (
-        (value_gate[..., None] * value_delta[:, :, None, :])
-        .astype(bf16)
-        .reshape(length, H * NE * DH)
     )
     vselect_delta = (
         (
@@ -791,27 +886,27 @@
         .astype(bf16)
         .reshape(length, H * NE)
     )
-    grad_value = weight_grad(normed_low, values_delta).astype(bf16)
-    narrow = 2 * H * NE + experts
-    padding = -narrow % 128
-    grad_rest = jnp.concatenate(
-        [
-            weight_grad(normed_low, query_delta).astype(bf16),
-            weight_grad(normed_low, key_delta).astype(bf16),
-            jnp.concatenate(
-                [
-                    weight_grad(normed_low, vselect_delta),
-                    weight_grad(normed_low, oselect_delta),
-                    router_sum,
-                    jnp.zeros((D, padding), f32),
-                ],
-                axis=1,
-            ).astype(bf16),
-        ],
-        axis=1,
-    )
+    narrow = 128
+    margin = ((0, 0), (0, narrow - H * NE))
+    select_delta = jnp.concatenate(
+        [jnp.pad(vselect_delta, margin), jnp.pad(oselect_delta, margin)], axis=1
+    )
+    cuts = [(0, H * DH), (H * DH, H * DH)]
+    start = 2 * H * DH
+    cuts += [(start, H * NE), (start + narrow, H * NE), (start + 2 * narrow, experts)]
+    rest_sum = Sum(
+        cube,
+        grad_blocks(cube, normed_low, [query_delta, key_delta, select_delta], router_sum),
+        cuts,
+    )
+    query_sent = rest_sum.tied(query_delta)
+    query_sent = out_sum.tied(query_sent)
+    query_sent = value_sum.tied(query_sent)
+    last_held[0], last_held[1], query_sent = tie(*last_held, query_sent)
+    for each in (rest_sum, out_sum, value_sum):
+        each.step()
     normed_delta = (
-        input_term(query_delta, query_weight)
+        input_term(query_sent, query_weight)
         + input_term(key_delta, key_weight)
         + input_term(values_delta, value_weight)
     )
@@ -820,37 +915,21 @@
         + input_term(vselect_delta, value_selector)
         + input_term(oselect_delta, output_selector)
     )
+    for each in (rest_sum, out_sum, value_sum):
+        normed_delta = each.tied(normed_delta)
+    for each in (rest_sum, out_sum, value_sum):
+        each.run(each.steps - each.done)
+    (grad_output,) = out_sum.out
+    (grad_value,) = value_sum.out
+    grad_query, grad_key, grad_vselect, grad_oselect, grad_router = rest_sum.out
     input_delta = middle_delta + norm_back(inputs, att_rms, attention_gain, normed_delta)
     grad_attention = jnp.sum(normed_delta * inputs * att_rms, axis=0)
-    out_sum = Sum(moves, grad_output, [D])
-    value_sum = Sum(moves, grad_value, [H * NE * DH])
-    rest_sum = Sum(moves, grad_rest, [H * DH, H * DH, narrow + padding])
-    out_sum.core()
-    out_sum.plane()
-    value_sum.core()
-    out_sum.line()
-    value_sum.plane()
-    out_sum.line_back()
-    rest_sum.core()
-    value_sum.line()
-    rest_sum.plane()
-    value_sum.line_back()
-    rest_sum.line()
-    out_sum.plane_back()
-    rest_sum.line_back()
-    (grad_output,) = out_sum.core_back()
-    value_sum.plane_back()
-    (grad_value,) = value_sum.core_back()
-    rest_sum.plane_back()
-    grad_query, grad_key, narrow_sum = rest_sum.core_back()
-    grad_vselect = narrow_sum[:, : H * NE]
-    grad_oselect = narrow_sum[:, H * NE : 2 * H * NE]
-    grad_router = narrow_sum[:, 2 * H * NE : narrow]
-
-    output_rows = middle_rows + token_sum(1)
+    output_rows = middle_rows + sums[home][0].astype(f32)
+    for value in outputs_back:
+        output_rows = output_rows + value.astype(f32)
     grad_up, grad_down = (
-        moves.over_hi(h).astype(f32) + a.astype(f32) + b.astype(f32)
-        for h, (a, b) in zip(held, first_parts)
+        h.astype(f32) + a.astype(f32) + b.astype(f32)
+        for h, (a, b) in zip(last_held, first_parts)
     )
     small = sum_small(
         moves,

time: 804 us -> 679 us (0.84)
  Pallas kernels: 288 us -> 229 us
  waiting for transfers between devices: 258 us -> 226 us
  starting transfers between devices: 88.9 us -> 61.4 us
  other arithmetic: 47.5 us -> 56.7 us
  matrix products: 54.3 us -> 46.1 us
    ppermute x0 -> x24, waiting for transfers between devices: none -> 106 us  [exchange(): return lax.ppermute(value, ('dp', 'expert'), pairs)]
    pallas_call x6, Pallas kernels: 93.1 us -> 35.3 us  [the longest x3 22.5 us: assemble(): pl.pallas_call(functools.partial(assemble_kernel, count, cuts), grid_spec...]
    ppermute x30 -> x12, waiting for transfers between devices: 106 us -> 58 us  [over_hi(): return lax.ppermute(value, 'expert', pairs)]
    ppermute x11 -> x5, waiting for transfers between devices: 46.3 us -> 0.01 us  [over_plane(): return lax.ppermute(value, ('dp', 'expert'), pairs)]
    ppermute x11 -> x5, waiting for transfers between devices: 53.6 us -> 17.1 us  [over_plane(): return lax.ppermute(value, 'expert', [(i, i ^ b) for i in range(self.ex)])]
    ppermute x30 -> x12, starting transfers between devices: 42.2 us -> 14.6 us  [over_hi(): return lax.ppermute(value, 'expert', pairs)]
    ppermute x0 -> x24, starting transfers between devices: none -> 19.1 us  [exchange(): return lax.ppermute(value, ('dp', 'expert'), pairs)]
    dot_general x10 -> x3, matrix products: 22.6 us -> 5.56 us  [the longest x1 5.16 us: on_device(): jnp.einsum('td,cd->tc', middle_sent, output_weight, preferred_element_typ...]
  transfers between devices with their start and end apart: 95 -> 77, of which waited for: 30 -> 29; matrix products, arithmetic and copies ran while one was open for 18% -> 20% of each run, Pallas kernels for 31% -> 33%
where the time goes in v2:
time: 679 us; the launch traced here: 669 us
  Pallas kernels  229 us (34%)
  waiting for transfers between devices  226 us (33%)
  starting transfers between devices  61.4 us (9%)
  other arithmetic  56.7 us (8%)
  local copies, waits for them, and re-layouts  47.2 us (7%)
  matrix products  46.1 us (7%)
    pallas_call x8, Pallas kernels, run_experts(): pl.pallas_call(functools.partial(experts_kernel, blocks, pairs, previous...  194 us
    ppermute x24, waiting for transfers between devices, exchange(): return lax.ppermute(value, ('dp', 'expert'), pairs)  106 us
    ppermute x12, waiting for transfers between devices, over_hi(): return lax.ppermute(value, 'expert', pairs)  58 us
    unnamed x184, local copies, waits for them, and re-layouts  26.2 us
    pallas_call x3, Pallas kernels, assemble(): pl.pallas_call(functools.partial(assemble_kernel, count, cuts), grid_spec...  22.5 us
    convert_element_type x21, other arithmetic, add_low(): return total.astype(bf16)  21.8 us
    ppermute x5, waiting for transfers between devices, over_plane(): return lax.ppermute(value, 'dp', list(enumerate(dp_to)))  19.3 us
    ppermute x24, starting transfers between devices, exchange(): return lax.ppermute(value, ('dp', 'expert'), pairs)  19.1 us
  transfers between devices with their start and end apart: 77, of which 29 were waited for; matrix products, arithmetic and copies ran while one was open for 20% of the time, Pallas kernels for 33%

profile of v2, /device:TPU:0, one launch (start us, length us, event | category | flops | bytes accessed | tf_op | source)
XLA Modules:
  0.0 669.3 jit_solution(3474325313103425703)
XLA Ops:
  14.4 8.0 %copy.193 = bf16[1024,2560]{0,1:T(8,128)(2,1)} copy(bf16[1024,2560]{1,0:T(8,128)(2,1)} %param.24) | data formatting | bytes 10485760 | tf_op args[7]
  29.1 5.0 multiply_reduce_fusion.3
  51.9 17.1 %collective-permute-done.6.refs_0_ = bf16[512,1024]{1,0:T(8,128)(2,1)} collective-permute-done((bf16[512,1024]{1,0:T(8,128)(2,1)}, bf16[512,1024]{1,0:T(8,128)(2,1)}, u32[]{:S(2)}, u32[]{:S(2)}) %collective-permute-start.6) | collective-permute-done | bytes 1048608 | tf_op jit(solution)/shard_map/ppermute | solution.py:363
  73.4 22.8 %experts.8 = (bf16[512,1024]{1,0:T(8,128)(2,1)}, bf16[512,1024]{1,0:T(8,128)(2,1)}, f32[6,1024,256]{2,1,0:T(8,128)}, f32[6,256,1024]{2,1,0:T(8,128)}, f32[1024,16]{1,0:T(8,128)}) custom-call(bf16[512,1024]{1,0:T(8,128)(2,1)} %multiply_convert_fusion.3.refs_0_, bf16[512,1024]{1,0:T(8,128)(2,1)} %bitcast.12.refs_1_, bf16[512,96]{1,0:T(8,128)(2,1)} %copy-done.41, ...), custom_call_target="tpu_custom_call" | custom-call | flops 524288 | tf_op jit(solution)/shard_map/experts/pallas_call | solution.py:300
  99.8 24.3 %experts.9 = (bf16[512,1024]{1,0:T(8,128)(2,1)}, bf16[512,1024]{1,0:T(8,128)(2,1)}, f32[6,1024,256]{2,1,0:T(8,128)}, f32[6,256,1024]{2,1,0:T(8,128)}, f32[1024,16]{1,0:T(8,128)}) custom-call(bf16[512,1024]{1,0:T(8,128)(2,1)} %collective-permute-done.6.refs_0_, bf16[512,1024]{1,0:T(8,128)(2,1)} %collective-permute-done.8.refs_1_, ...), custom_call_target="tpu_custom_call" | custom-call | flops 524288 | tf_op jit(solution)/shard_map/experts/pallas_call | solution.py:300
  125.7 19.3 %collective-permute-done.15.refs_2_ = bf16[512,96]{1,0:T(8,128)(2,1)S(1)} collective-permute-done((bf16[512,96]{1,0:T(8,128)(2,1)}, bf16[512,96]{1,0:T(8,128)(2,1)S(1)}, u32[]{:S(2)}, u32[]{:S(2)}) %collective-permute-start.15) | collective-permute-done | bytes 98336 | tf_op jit(solution)/shard_map/ppermute | solution.py:366
  148.3 24.2 %experts.10 = (bf16[512,1024]{1,0:T(8,128)(2,1)}, bf16[512,1024]{1,0:T(8,128)(2,1)}, f32[6,1024,256]{2,1,0:T(8,128)}, f32[6,256,1024]{2,1,0:T(8,128)}, f32[1024,16]{1,0:T(8,128)}) custom-call(bf16[512,1024]{1,0:T(8,128)(2,1)} %collective-permute-done.7.refs_0_, bf16[512,1024]{1,0:T(8,128)(2,1)} %collective-permute-done.14.refs_1_, ...), custom_call_target="tpu_custom_call" | custom-call | flops 524288 | tf_op jit(solution)/shard_map/experts/pallas_call | solution.py:300
  174.0 23.8 %experts.11 = (bf16[512,1024]{1,0:T(8,128)(2,1)}, bf16[512,1024]{1,0:T(8,128)(2,1)}, bf16[6,1024,128]{2,1,0:T(8,128)(2,1)}, bf16[6,1024,128]{2,1,0:T(8,128)(2,1)...) custom-call(bf16[512,1024]{1,0:T(8,128)(2,1)} %copy-done.25, ...), custom_call_target="tpu_custom_call" | custom-call | flops 524288 | tf_op jit(solution)/shard_map/experts/pallas_call | solution.py:300
  208.2 23.9 %experts.12 = (bf16[512,1024]{1,0:T(8,128)(2,1)}, bf16[512,1024]{1,0:T(8,128)(2,1)}, f32[6,1024,256]{2,1,0:T(8,128)}, f32[6,256,1024]{2,1,0:T(8,128)}, f32[1024,16]{1,0:T(8,128)}) custom-call(bf16[512,1024]{1,0:T(8,128)(2,1)} %copy-done.25, bf16[512,1024]{1,0:T(8,128)(2,1)} %copy-done.26, bf16[512,96]{1,0:T(8,128)(2,1)} %copy-done.57, ...), custom_call_target="tpu_custom_call" | custom-call | flops 524288 | tf_op jit(solution)/shard_map/experts/pallas_call | solution.py:300
  238.1 25.0 %experts.13 = (bf16[512,1024]{1,0:T(8,128)(2,1)}, bf16[512,1024]{1,0:T(8,128)(2,1)}, f32[6,1024,256]{2,1,0:T(8,128)}, f32[6,256,1024]{2,1,0:T(8,128)}, f32[1024,16]{1,0:T(8,128)}) custom-call(bf16[512,1024]{1,0:T(8,128)(2,1)} %collective-permute-done.6.refs_0_, bf16[512,1024]{1,0:T(8,128)(2,1)} %collective-permute-done.8.refs_1_, ...), custom_call_target="tpu_custom_call" | custom-call | flops 524288 | tf_op jit(solution)/shard_map/experts/pallas_call | solution.py:300
  263.1 25.0 %experts.14 = (bf16[512,1024]{1,0:T(8,128)(2,1)}, bf16[512,1024]{1,0:T(8,128)(2,1)}, f32[6,1024,256]{2,1,0:T(8,128)}, f32[6,256,1024]{2,1,0:T(8,128)}, f32[1024,16]{1,0:T(8,128)}) custom-call(bf16[512,1024]{1,0:T(8,128)(2,1)} %collective-permute-done.7.refs_0_, bf16[512,1024]{1,0:T(8,128)(2,1)} %collective-permute-done.14.refs_1_, ...), custom_call_target="tpu_custom_call" | custom-call | flops 524288 | tf_op jit(solution)/shard_map/experts/pallas_call | solution.py:300
  292.0 4.8 copy.200.left_a.left_b
  297.1 15.6 %collective-permute-done.25 = bf16[3,1024,128]{2,1,0:T(8,128)(2,1)} collective-permute-done((bf16[3,1024,128]{2,1,0:T(8,128)(2,1)}, bf16[3,1024,128]{2,1,0:T(8,128)(2,1)}, u32[]{:S(2)}, u32[]{:S(2)}) %collective-permute-start.25) | collective-permute-done | bytes 786464 | tf_op jit(solution)/shard_map/ppermute | solution.py:356
  314.2 14.0 %collective-permute-done.26 = bf16[3,128,1024]{2,1,0:T(8,128)(2,1)} collective-permute-done((bf16[3,128,1024]{2,1,0:T(8,128)(2,1)}, bf16[3,128,1024]{2,1,0:T(8,128)(2,1)}, u32[]{:S(2)}, u32[]{:S(2)}) %collective-permute-start.26) | collective-permute-done | bytes 786464 | tf_op jit(solution)/shard_map/ppermute | solution.py:356
  329.4 25.1 %experts.15 = (bf16[512,1024]{1,0:T(8,128)(2,1)}, bf16[512,1024]{1,0:T(8,128)(2,1)}, bf16[6,1024,128]{2,1,0:T(8,128)(2,1)}, bf16[6,1024,128]{2,1,0:T(8,128)(2,1)...) custom-call(bf16[512,1024]{1,0:T(8,128)(2,1)} %multiply_convert_fusion.3.refs_0_, ...), custom_call_target="tpu_custom_call" | custom-call | flops 524288 | tf_op jit(solution)/shard_map/experts/pallas_call | solution.py:300
  371.1 5.2 fusion.74
  377.3 14.3 %collective-permute-done.31 = bf16[3,1024,128]{2,1,0:T(8,128)(2,1)S(1)} collective-permute-done((bf16[3,1024,128]{2,1,0:T(8,128)(2,1)S(1)}, bf16[3,1024,128]{2,1,0:T(8,128)(2,1)S(1)}, u32[]{:S(2)}, u32[]{:S(2)}) %collective-permute-start.31) | collective-permute-done | bytes 786464 | tf_op jit(solution)/shard_map/ppermute | solution.py:356
  393.6 14.0 %collective-permute-done.33 = bf16[3,128,1024]{2,1,0:T(8,128)(2,1)S(1)} collective-permute-done((bf16[3,128,1024]{2,1,0:T(8,128)(2,1)S(1)}, bf16[3,128,1024]{2,1,0:T(8,128)(2,1)S(1)}, u32[]{:S(2)}, u32[]{:S(2)}) %collective-permute-start.33) | collective-permute-done | bytes 786464 | tf_op jit(solution)/shard_map/ppermute | solution.py:356
  424.5 5.6 grad_blocks.4
  433.6 8.7 %multiply_convert_fusion.2 = bf16[4,512,512]{1,2,0:T(8,128)(2,1)} fusion(f32[4,512,512]{1,2,0:T(8,128)} %copy-done.10, f32[4,512]{1,0:T(4,128)S(1)} %copy-done.80, pred[512,512]{0,1:T(8,128)(4,1)S(1)} %fusion.43, bf16[512,4,128]{0,2,1:T(8,128)(2,1)} %copy-done.60, bf16[512,4,128]{0,2,1:T(8,128)(2,1)} %copy-done.83), kind=kOutput, calls=%fused_computation.9 | convolution fusion | flops 547359232 | bytes 7610368 | tf_op jit(solution)/shard_map/sub | solution.py:847
  445.8 6.9 %fusion.76 = f32[512,1024]{1,0:T(8,128)} fusion(bf16[512,2560]{0,1:T(8,128)(2,1)S(1)} %bitcast.184, bf16[1024,2560]{1,0:T(8,128)(2,1)} %param.24), kind=kOutput, calls=%fused_computation.170 | convolution fusion | flops 2684354560 | bytes 9961472 | tf_op jit(solution)/shard_map/tc,dc->td/dot_general | solution.py:48
  472.0 40.1 %collective-permute-done.42 = bf16[2,80,1024]{2,1,0:T(8,128)(2,1)S(1)} collective-permute-done((bf16[2,80,1024]{2,1,0:T(8,128)(2,1)S(1)}, bf16[2,80,1024]{2,1,0:T(8,128)(2,1)S(1)}, u32[]{:S(2)}, u32[]{:S(2)}) %collective-permute-start.42) | collective-permute-done | bytes 327712 | tf_op jit(solution)/shard_map/ppermute | solution.py:413
  518.0 9.0 %collective-permute-done.70 = bf16[1,80,1024]{2,1,0:T(8,128)(2,1)S(1)} collective-permute-done((bf16[1,80,1024]{2,1,0:T(8,128)(2,1)S(1)}, bf16[1,80,1024]{2,1,0:T(8,128)(2,1)S(1)}, u32[]{:S(2)}, u32[]{:S(2)}) %collective-permute-start.70) | collective-permute-done | bytes 163872 | tf_op jit(solution)/shard_map/ppermute | solution.py:413
  527.1 5.4 collective-permute-done.41
  535.2 8.0 %collective-permute-done.72 = bf16[2,80,1024]{2,1,0:T(8,128)(2,1)S(1)} collective-permute-done((bf16[2,80,1024]{2,1,0:T(8,128)(2,1)S(1)}, bf16[2,80,1024]{2,1,0:T(8,128)(2,1)S(1)}, u32[]{:S(2)}, u32[]{:S(2)}) %collective-permute-start.72) | collective-permute-done | bytes 327712 | tf_op jit(solution)/shard_map/ppermute | solution.py:413
  543.8 6.7 collective-permute-done.61
  554.3 4.7 collective-permute-done.62
  562.0 9.5 %collective-permute-done.63 = bf16[1,32,2560]{2,1,0:T(8,128)(2,1)S(1)} collective-permute-done((bf16[1,32,2560]{2,1,0:T(8,128)(2,1)S(1)}, bf16[1,32,2560]{2,1,0:T(8,128)(2,1)S(1)}, u32[]{:S(2)}, u32[]{:S(2)}) %collective-permute-start.63) | collective-permute-done | bytes 163872 | tf_op jit(solution)/shard_map/ppermute | solution.py:413
  585.3 5.3 collective-permute-start.66
  602.5 15.9 %collective-permute-done.47 = f32[3,1024]{1,0:T(4,128)S(1)} collective-permute-done((f32[3,1024]{1,0:T(4,128)S(1)}, f32[3,1024]{1,0:T(4,128)S(1)}, u32[]{:S(2)}, u32[]{:S(2)}) %collective-permute-start.47) | collective-permute-done | bytes 12320 | tf_op jit(solution)/shard_map/ppermute | solution.py:600
  650.5 9.1 %assemble.5 = f32[32,80,1024]{2,1,0:T(8,128)} custom-call(s32[10]{0:T(128)S(1)} %stack.224.order_ref, bf16[8,80,1024]{2,1,0:T(8,128)(2,1)S(1)} %pad_maximum_fusion.1.refs_0_, bf16[8,80,1024]{2,1,0:T(8,128)(2,1)} %collective-permute-done.74.refs_1_, bf16[8,80,1024]{2,1,0:T(8,128)(2,1)} %collective-permute-done.75.refs_2_, ...), custom_call_target="tpu_custom_call" | custom-call | bytes 5242880 | tf_op jit(solution)/shard_map/assemble/pallas_call | solution.py:525
  659.6 9.3 %assemble.4 = f32[32,32,2560]{2,1,0:T(8,128)} custom-call(s32[10]{0:T(128)S(1)} %stack.224.order_ref, bf16[8,32,2560]{2,1,0:T(8,128)(2,1)} %pad_maximum_fusion.refs_0_, bf16[8,32,2560]{2,1,0:T(8,128)(2,1)} %collective-permute-done.67.refs_1_, bf16[8,32,2560]{2,1,0:T(8,128)(2,1)} %collective-permute-done.68.refs_2_, ...), custom_call_target="tpu_custom_call" | custom-call | bytes 5242880 | tf_op jit(solution)/shard_map/assemble/pallas_call | solution.py:525
  (440 shorter events, 211.4 us)
Async XLA Ops:
  0.7 41.3 %collective-permute-start = (bf16[3,1024,128]{2,1,0:T(8,128)(2,1)}, bf16[3,1024,128]{2,1,0:T(8,128)(2,1)S(1)}, u32[]{:S(2)}, u32[]{:S(2)}) collective-permute-start(bf16[3,1024,128]{2,1,0:T(8,128)(2,1)} %refs_5_.7), channel_id=1, source_target_pairs={{0,2},{1,3},{2,4},{3,5},{4,6},{5,7},{6,0},{7,1},{8,10},{9,11},{10,... | collective-permute-start | bytes 2359304 | tf_op jit(solution)/shard_map/ppermute | solution.py:356
  3.8 40.3 %collective-permute-start.2 = (bf16[3,1024,128]{2,1,0:T(8,128)(2,1)}, bf16[3,1024,128]{2,1,0:T(8,128)(2,1)}, u32[]{:S(2)}, u32[]{:S(2)}) collective-permute-start(bf16[3,1024,128]{2,1,0:T(8,128)(2,1)} %refs_5_.7), channel_id=1, source_target_pairs={{0,8},{8,0},{16,24},{24,16},{1,9},{9,1},{17,25},{25,17},{2,10},{10... | collective-permute-start | bytes 2359304 | tf_op jit(solution)/shard_map/ppermute | solution.py:352
  3.8 38.2 %collective-permute-start.1 = (bf16[3,128,1024]{2,1,0:T(8,128)(2,1)}, bf16[3,128,1024]{2,1,0:T(8,128)(2,1)}, u32[]{:S(2)}, u32[]{:S(2)}) collective-permute-start(bf16[3,128,1024]{2,1,0:T(8,128)(2,1)} %refs_7_.7), channel_id=1, source_target_pairs={{0,2},{1,3},{2,4},{3,5},{4,6},{5,7},{6,0},{7,1},{8,10},{9,11},{10,... | collective-permute-start | bytes 2359304 | tf_op jit(solution)/shard_map/ppermute | solution.py:356
  5.4 40.3 %collective-permute-start.3 = (bf16[3,128,1024]{2,1,0:T(8,128)(2,1)}, bf16[3,128,1024]{2,1,0:T(8,128)(2,1)}, u32[]{:S(2)}, u32[]{:S(2)}) collective-permute-start(bf16[3,128,1024]{2,1,0:T(8,128)(2,1)} %refs_7_.7), channel_id=1, source_target_pairs={{0,8},{8,0},{16,24},{24,16},{1,9},{9,1},{17,25},{25,17},{2,10},{10... | collective-permute-start | bytes 2359304 | tf_op jit(solution)/shard_map/ppermute | solution.py:352
  45.6 51.2 %collective-permute-start.8 = (bf16[512,1024]{1,0:T(8,128)(2,1)}, bf16[512,1024]{1,0:T(8,128)(2,1)}, u32[]{:S(2)}, u32[]{:S(2)}) collective-permute-start(bf16[512,1024]{1,0:T(8,128)(2,1)} %bitcast.12.refs_1_), channel_id=1, source_target_pairs={{0,1},{1,0},{2,3},{3,2},{4,5},{5,4},{6,7},{7,6},{8,9},{9,8},{10,11... | collective-permute-start | bytes 3145736 | tf_op jit(solution)/shard_map/ppermute | solution.py:363
  47.0 52.2 %collective-permute-start.10 = (bf16[3,1024,128]{2,1,0:T(8,128)(2,1)}, bf16[3,1024,128]{2,1,0:T(8,128)(2,1)S(1)}, u32[]{:S(2)}, u32[]{:S(2)}) collective-permute-start(bf16[3,1024,128]{2,1,0:T(8,128)(2,1)} %copy-done.17), channel_id=1, source_target_pairs={{0,2},{1,3},{2,4},{3,5},{4,6},{5,7},{6,0},{7,1},{8,10},{9,11},{10,... | collective-permute-start | bytes 2359304 | tf_op jit(solution)/shard_map/ppermute | solution.py:356
  48.6 75.5 %collective-permute-start.11 = (bf16[3,128,1024]{2,1,0:T(8,128)(2,1)}, bf16[3,128,1024]{2,1,0:T(8,128)(2,1)}, u32[]{:S(2)}, u32[]{:S(2)}) collective-permute-start(bf16[3,128,1024]{2,1,0:T(8,128)(2,1)} %collective-permute-done.1.refs_11_), channel_id=1, source_target_pairs={{0,2},{1,3},{2,4},{3,5},{4,6},{5,7},{6,0},{7,1},{8,10},{9,11},{10,... | collective-permute-start | bytes 2359304 | tf_op jit(solution)/shard_map/ppermute | solution.py:356
  68.9 77.8 %collective-permute-start.14 = (bf16[512,1024]{1,0:T(8,128)(2,1)}, bf16[512,1024]{1,0:T(8,128)(2,1)}, u32[]{:S(2)}, u32[]{:S(2)}) collective-permute-start(bf16[512,1024]{1,0:T(8,128)(2,1)} %bitcast.12.refs_1_), channel_id=1, source_target_pairs={{0,16},{8,24},{16,0},{24,8},{1,17},{9,25},{17,1},{25,9},{2,18},{10... | collective-permute-start | bytes 3145736 | tf_op jit(solution)/shard_map/ppermute | solution.py:366
  96.3 76.4 %collective-permute-start.20 = (bf16[512,1024]{1,0:T(8,128)(2,1)}, bf16[512,1024]{1,0:T(8,128)(2,1)S(1)}, u32[]{:S(2)}, u32[]{:S(2)}) collective-permute-start(bf16[512,1024]{1,0:T(8,128)(2,1)} %multiply_convert_fusion.3.refs_0_), channel_id=1, source_target_pairs={{0,17},{1,16},{2,19},{3,18},{4,21},{5,20},{6,23},{7,22},{8,25},{9,... | collective-permute-start | bytes 3145736 | tf_op jit(solution)/shard_map/ppermute | solution.py:372
  96.8 75.8 %collective-permute-start.21 = (bf16[512,1024]{1,0:T(8,128)(2,1)}, bf16[512,1024]{1,0:T(8,128)(2,1)S(1)}, u32[]{:S(2)}, u32[]{:S(2)}) collective-permute-start(bf16[512,1024]{1,0:T(8,128)(2,1)} %bitcast.12.refs_1_), channel_id=1, source_target_pairs={{0,17},{1,16},{2,19},{3,18},{4,21},{5,20},{6,23},{7,22},{8,25},{9,... | collective-permute-start | bytes 3145736 | tf_op jit(solution)/shard_map/ppermute | solution.py:372
  99.3 45.7 %collective-permute-start.15 = (bf16[512,96]{1,0:T(8,128)(2,1)}, bf16[512,96]{1,0:T(8,128)(2,1)S(1)}, u32[]{:S(2)}, u32[]{:S(2)}) collective-permute-start(bf16[512,96]{1,0:T(8,128)(2,1)} %copy-done.41), channel_id=1, source_target_pairs={{0,16},{8,24},{16,0},{24,8},{1,17},{9,25},{17,1},{25,9},{2,18},{10... | collective-permute-start | bytes 294920 | tf_op jit(solution)/shard_map/ppermute | solution.py:366
  124.1 48.4 %collective-permute-start.16 = (bf16[3,1024,128]{2,1,0:T(8,128)(2,1)S(1)}, bf16[3,1024,128]{2,1,0:T(8,128)(2,1)}, u32[]{:S(2)}, u32[]{:S(2)}) collective-permute-start(bf16[3,1024,128]{2,1,0:T(8,128)(2,1)S(1)} %collective-permute-done.10.refs_5_), channel_id=1, source_target_pairs={{0,2},{1,3},{2,4},{3,5},{4,6},{5,7},{6,0},{7,1},{8,10},{9,11},{10,... | collective-permute-start | bytes 2359304 | tf_op jit(solution)/shard_map/ppermute | solution.py:356
  145.0 27.6 %collective-permute-start.17 = (bf16[3,128,1024]{2,1,0:T(8,128)(2,1)}, bf16[3,128,1024]{2,1,0:T(8,128)(2,1)}, u32[]{:S(2)}, u32[]{:S(2)}) collective-permute-start(bf16[3,128,1024]{2,1,0:T(8,128)(2,1)} %collective-permute-done.11.refs_7_), channel_id=1, source_target_pairs={{0,2},{1,3},{2,4},{3,5},{4,6},{5,7},{6,0},{7,1},{8,10},{9,11},{10,... | collective-permute-start | bytes 2359304 | tf_op jit(solution)/shard_map/ppermute | solution.py:356
  197.8 35.7 %collective-permute-start.23 = (bf16[6,1024,128]{2,1,0:T(8,128)(2,1)}, bf16[6,1024,128]{2,1,0:T(8,128)(2,1)}, u32[]{:S(2)}, u32[]{:S(2)}) collective-permute-start(bf16[6,1024,128]{2,1,0:T(8,128)(2,1)} %get-tuple-element.168), channel_id=1, source_target_pairs={{0,8},{8,0},{16,24},{24,16},{1,9},{9,1},{17,25},{25,17},{2,10},{10... | collective-permute-start | bytes 4718600 | tf_op jit(solution)/shard_map/ppermute | solution.py:352
  198.4 37.4 %collective-permute-start.24 = (bf16[6,128,1024]{2,1,0:T(8,128)(2,1)}, bf16[6,128,1024]{2,1,0:T(8,128)(2,1)}, u32[]{:S(2)}, u32[]{:S(2)}) collective-permute-start(bf16[6,128,1024]{2,1,0:T(8,128)(2,1)} %get-tuple-element.170), channel_id=1, source_target_pairs={{0,8},{8,0},{16,24},{24,16},{1,9},{9,1},{17,25},{25,17},{2,10},{10... | collective-permute-start | bytes 4718600 | tf_op jit(solution)/shard_map/ppermute | solution.py:352
  232.1 122.4 %collective-permute-start.36 = (bf16[512,1024]{1,0:T(8,128)(2,1)}, bf16[512,1024]{1,0:T(8,128)(2,1)S(1)}, u32[]{:S(2)}, u32[]{:S(2)}) collective-permute-start(bf16[512,1024]{1,0:T(8,128)(2,1)} %get-tuple-element.202), channel_id=1, source_target_pairs={{0,17},{1,16},{2,19},{3,18},{4,21},{5,20},{6,23},{7,22},{8,25},{9,... | collective-permute-start | bytes 3145736 | tf_op jit(solution)/shard_map/ppermute | solution.py:372
  288.1 66.5 %collective-permute-start.35 = (bf16[512,1024]{1,0:T(8,128)(2,1)}, bf16[512,1024]{1,0:T(8,128)(2,1)}, u32[]{:S(2)}, u32[]{:S(2)}) collective-permute-start(bf16[512,1024]{1,0:T(8,128)(2,1)} %get-tuple-element.201), channel_id=1, source_target_pairs={{0,16},{8,24},{16,0},{24,8},{1,17},{9,25},{17,1},{25,9},{2,18},{10... | collective-permute-start | bytes 3145736 | tf_op jit(solution)/shard_map/ppermute | solution.py:366
  289.4 65.7 %collective-permute-start.34 = (bf16[512,1024]{1,0:T(8,128)(2,1)}, bf16[512,1024]{1,0:T(8,128)(2,1)}, u32[]{:S(2)}, u32[]{:S(2)}) collective-permute-start(bf16[512,1024]{1,0:T(8,128)(2,1)} %get-tuple-element.200), channel_id=1, source_target_pairs={{0,1},{1,0},{2,3},{3,2},{4,5},{5,4},{6,7},{7,6},{8,9},{9,8},{10,11... | collective-permute-start | bytes 3145736 | tf_op jit(solution)/shard_map/ppermute | solution.py:363
  290.4 37.8 %collective-permute-start.26 = (bf16[3,128,1024]{2,1,0:T(8,128)(2,1)}, bf16[3,128,1024]{2,1,0:T(8,128)(2,1)}, u32[]{:S(2)}, u32[]{:S(2)}) collective-permute-start(bf16[3,128,1024]{2,1,0:T(8,128)(2,1)} %add_convert_fusion.9), channel_id=1, source_target_pairs={{0,2},{1,3},{2,4},{3,5},{4,6},{5,7},{6,0},{7,1},{8,10},{9,11},{10,... | collective-permute-start | bytes 2359304 | tf_op jit(solution)/shard_map/ppermute | solution.py:356
  312.8 140.0 %collective-permute-start.29 = (bf16[512,1024]{1,0:T(8,128)(2,1)}, bf16[512,1024]{1,0:T(8,128)(2,1)}, u32[]{:S(2)}, u32[]{:S(2)}) collective-permute-start(bf16[512,1024]{1,0:T(8,128)(2,1)} %get-tuple-element.192), channel_id=1, source_target_pairs={{0,17},{1,16},{2,19},{3,18},{4,21},{5,20},{6,23},{7,22},{8,25},{9,... | collective-permute-start | bytes 3145736 | tf_op jit(solution)/shard_map/ppermute | solution.py:372
  328.2 124.6 %collective-permute-start.27 = (bf16[512,1024]{1,0:T(8,128)(2,1)}, bf16[512,1024]{1,0:T(8,128)(2,1)}, u32[]{:S(2)}, u32[]{:S(2)}) collective-permute-start(bf16[512,1024]{1,0:T(8,128)(2,1)} %get-tuple-element.188), channel_id=1, source_target_pairs={{0,1},{1,0},{2,3},{3,2},{4,5},{5,4},{6,7},{7,6},{8,9},{9,8},{10,11... | collective-permute-start | bytes 3145736 | tf_op jit(solution)/shard_map/ppermute | solution.py:363
  366.6 42.4 %collective-permute-start.37 = (bf16[16,80,1024]{2,1,0:T(8,128)(2,1)S(1)}, bf16[16,80,1024]{2,1,0:T(8,128)(2,1)S(1)}, u32[]{:S(2)}, u32[]{:S(2)}) collective-permute-start(bf16[16,80,1024]{2,1,0:T(8,128)(2,1)S(1)} %get-tuple-element.206), channel_id=1, source_target_pairs={{0,8},{8,0},{16,24},{24,16},{1,9},{9,1},{17,25},{25,17},{2,10},{10... | collective-permute-start | bytes 7864328 | tf_op jit(solution)/shard_map/ppermute | solution.py:352
  371.1 36.6 %collective-permute-start.33 = (bf16[3,128,1024]{2,1,0:T(8,128)(2,1)S(1)}, bf16[3,128,1024]{2,1,0:T(8,128)(2,1)S(1)}, u32[]{:S(2)}, u32[]{:S(2)}) collective-permute-start(bf16[3,128,1024]{2,1,0:T(8,128)(2,1)S(1)} %add_convert_fusion.6), channel_id=1, source_target_pairs={{0,2},{1,3},{2,4},{3,5},{4,6},{5,7},{6,0},{7,1},{8,10},{9,11},{10,... | collective-permute-start | bytes 2359304 | tf_op jit(solution)/shard_map/ppermute | solution.py:356
  391.7 61.1 %collective-permute-start.28 = (bf16[512,1024]{1,0:T(8,128)(2,1)}, bf16[512,1024]{1,0:T(8,128)(2,1)}, u32[]{:S(2)}, u32[]{:S(2)}) collective-permute-start(bf16[512,1024]{1,0:T(8,128)(2,1)} %get-tuple-element.191), channel_id=1, source_target_pairs={{0,16},{8,24},{16,0},{24,8},{1,17},{9,25},{17,1},{25,9},{2,18},{10... | collective-permute-start | bytes 3145736 | tf_op jit(solution)/shard_map/ppermute | solution.py:366
  445.7 66.4 %collective-permute-start.39 = (bf16[16,32,2560]{2,1,0:T(8,128)(2,1)}, bf16[16,32,2560]{2,1,0:T(8,128)(2,1)}, u32[]{:S(2)}, u32[]{:S(2)}) collective-permute-start(bf16[16,32,2560]{2,1,0:T(8,128)(2,1)} %get-tuple-element.220), channel_id=1, source_target_pairs={{0,8},{8,0},{16,24},{24,16},{1,9},{9,1},{17,25},{25,17},{2,10},{10... | collective-permute-start | bytes 7864328 | tf_op jit(solution)/shard_map/ppermute | solution.py:352
  466.8 48.8 %collective-permute-start.43 = (bf16[16,32,1408]{2,1,0:T(8,128)(2,1)S(1)}, bf16[16,32,1408]{2,1,0:T(8,128)(2,1)S(1)}, u32[]{:S(2)}, u32[]{:S(2)}) collective-permute-start(bf16[16,32,1408]{2,1,0:T(8,128)(2,1)S(1)} %get-tuple-element.235), channel_id=1, source_target_pairs={{0,8},{8,0},{16,24},{24,16},{1,9},{9,1},{17,25},{25,17},{2,10},{10... | collective-permute-start | bytes 4325384 | tf_op jit(solution)/shard_map/ppermute | solution.py:352
  468.3 43.7 %collective-permute-start.42 = (bf16[2,80,1024]{2,1,0:T(8,128)(2,1)S(1)}, bf16[2,80,1024]{2,1,0:T(8,128)(2,1)S(1)}, u32[]{:S(2)}, u32[]{:S(2)}) collective-permute-start(bf16[2,80,1024]{2,1,0:T(8,128)(2,1)S(1)} %get-tuple-element.233), channel_id=1, source_target_pairs={{0,2},{1,3},{2,0},{3,1},{4,6},{5,7},{6,4},{7,5},{8,10},{9,11},{10,... | collective-permute-start | bytes 983048 | tf_op jit(solution)/shard_map/ppermute | solution.py:413
  468.8 47.1 %collective-permute-start.44 = (bf16[3,1024,128]{2,1,0:T(8,128)(2,1)S(1)}, bf16[3,1024,128]{2,1,0:T(8,128)(2,1)S(1)}, u32[]{:S(2)}, u32[]{:S(2)}) collective-permute-start(bf16[3,1024,128]{2,1,0:T(8,128)(2,1)S(1)} %copy-done.52), channel_id=1, source_target_pairs={{0,2},{1,3},{2,4},{3,5},{4,6},{5,7},{6,0},{7,1},{8,10},{9,11},{10,... | collective-permute-start | bytes 2359304 | tf_op jit(solution)/shard_map/ppermute | solution.py:356
  470.9 45.1 %collective-permute-start.45 = (bf16[3,128,1024]{2,1,0:T(8,128)(2,1)S(1)}, bf16[3,128,1024]{2,1,0:T(8,128)(2,1)S(1)}, u32[]{:S(2)}, u32[]{:S(2)}) collective-permute-start(bf16[3,128,1024]{2,1,0:T(8,128)(2,1)S(1)} %copy-done.53), channel_id=1, source_target_pairs={{0,2},{1,3},{2,4},{3,5},{4,6},{5,7},{6,0},{7,1},{8,10},{9,11},{10,... | collective-permute-start | bytes 2359304 | tf_op jit(solution)/shard_map/ppermute | solution.py:356
  543.2 31.5 %collective-permute-start.73 = (bf16[4,80,1024]{2,1,0:T(8,128)(2,1)S(1)}, bf16[4,80,1024]{2,1,0:T(8,128)(2,1)S(1)}, u32[]{:S(2)}, u32[]{:S(2)}) collective-permute-start(bf16[4,80,1024]{2,1,0:T(8,128)(2,1)S(1)} %pad_maximum_fusion.4), channel_id=1, source_target_pairs={{0,1},{1,0},{2,3},{3,2},{4,5},{5,4},{6,7},{7,6},{8,24},{9,25},{10,... | collective-permute-start | bytes 1966088 | tf_op jit(solution)/shard_map/ppermute | solution.py:413
  574.8 57.4 %collective-permute-start.74 = (bf16[8,80,1024]{2,1,0:T(8,128)(2,1)S(1)}, bf16[8,80,1024]{2,1,0:T(8,128)(2,1)}, u32[]{:S(2)}, u32[]{:S(2)}) collective-permute-start(bf16[8,80,1024]{2,1,0:T(8,128)(2,1)S(1)} %pad_maximum_fusion.1.refs_0_), channel_id=1, source_target_pairs={{0,16},{1,17},{2,18},{3,19},{4,20},{5,21},{6,22},{7,23},{8,9},{9,8... | collective-permute-start | bytes 3932168 | tf_op jit(solution)/shard_map/ppermute | solution.py:413
  600.3 33.5 %collective-permute-start.67 = (bf16[8,32,2560]{2,1,0:T(8,128)(2,1)}, bf16[8,32,2560]{2,1,0:T(8,128)(2,1)}, u32[]{:S(2)}, u32[]{:S(2)}) collective-permute-start(bf16[8,32,2560]{2,1,0:T(8,128)(2,1)} %pad_maximum_fusion.refs_0_), channel_id=1, source_target_pairs={{0,16},{1,17},{2,18},{3,19},{4,20},{5,21},{6,22},{7,23},{8,9},{9,8... | collective-permute-start | bytes 3932168 | tf_op jit(solution)/shard_map/ppermute | solution.py:413
  (135 other events, 1440.0 us)

commit v3 on v2

--- a/solution.py
+++ b/solution.py
@@ -33,17 +33,6 @@
     return scaling * weighted - values * scaling * scaling * scaling * middle
 
 
-def masked_scores(query_low, key_low, allowed):
-    raw = jnp.einsum(
-        "qhd,khd->hqk", query_low, key_low, preferred_element_type=f32
-    ) * DH ** (-0.5)
-    return jnp.where(allowed[None], raw, masked_value)
-
-
-def weight_grad(left, right):
-    return jnp.einsum("td,tc->dc", left, right, preferred_element_type=f32)
-
-
 def input_term(delta, weight):
     return jnp.einsum("tc,dc->td", delta, weight, preferred_element_type=f32)
 
@@ -62,16 +51,17 @@
         del refs[:count]
         return taken
 
-    x_hbm, u_hbm, m_hbm = take(blocks), take(blocks), take(blocks)
+    x_hbm, um_hbm = take(blocks), take(blocks)
     select_ref, router_ref = take(2)
-    weights = (take(4), take(4))
+    weights = (take(2), take(2))
     y_prev, dx_prev = take(2) if chained else (None, None)
     gu_prev, gd_prev, gr_prev = take(3) if opened else (None, None, None)
     y_ref, dx_ref = take(2)
-    grads = take(4) if closed else take(2)
+    grads = take(2)
     (gr_ref,) = take(1)
     (x_buf, u_buf, m_buf, sems, w_up, w_down, w_sems) = take(7)
-    (y_acc, dx_acc, gup, gdown, x_turned, gate, delta, gr_acc) = refs
+    (y_acc, dx_acc, gup, gdown, x_turned, u_turned, gate, delta, gr_acc) = take(9)
+    gated_buf, hidden_buf = refs
     step = pl.program_id(0)
     pair = pl.program_id(1)
     slot = lax.rem(step, 2)
@@ -80,24 +70,28 @@
     def copies(index, place):
         return (
             pltpu.make_async_copy(x_hbm[index], x_buf.at[place], sems.at[place, 0]),
-            pltpu.make_async_copy(u_hbm[index], u_buf.at[place], sems.at[place, 1]),
-            pltpu.make_async_copy(m_hbm[index], m_buf.at[place], sems.at[place, 2]),
+            pltpu.make_async_copy(
+                um_hbm[index].at[:, pl.ds(0, D)], u_buf.at[place], sems.at[place, 1]
+            ),
+            pltpu.make_async_copy(
+                um_hbm[index].at[:, pl.ds(D, m_buf.shape[2])], m_buf.at[place], sems.at[place, 2]
+            ),
         )
 
     def weight_copies(index):
         place = index % 2
         k = index % local
-        up_a, up_b, down_a, down_b = weights[index // local]
-        return (
-            pltpu.make_async_copy(up_a.at[k], w_up.at[place, 0], w_sems.at[place, 0]),
-            pltpu.make_async_copy(up_b.at[k], w_up.at[place, 1], w_sems.at[place, 1]),
-            pltpu.make_async_copy(
-                down_a.at[k], w_down.at[place, pl.ds(0, FF)], w_sems.at[place, 2]
-            ),
-            pltpu.make_async_copy(
-                down_b.at[k], w_down.at[place, pl.ds(FF, FF)], w_sems.at[place, 3]
-            ),
-        )
+        ways = []
+        for side, weight in enumerate(weights[index // local]):
+            for part, buffer in enumerate((w_up, w_down)):
+                ways.append(
+                    pltpu.make_async_copy(
+                        weight.at[k, :, pl.ds(part * FF, FF)],
+                        buffer.at[place, :, pl.ds(side * FF, FF)],
+                        w_sems.at[place, 2 * side + part],
+                    )
+                )
+        return ways
 
     @pl.when(jnp.logical_and(step == 0, pair == 0))
     def _():
@@ -135,93 +129,99 @@
 
         x = x_buf[slot]
         x_turned[...] = x.T
+        u_turned[...] = u_buf[slot].T
         logits = jnp.dot(x, router_ref[...], preferred_element_type=f32)
         chosen = jnp.dot(m_buf[slot], select_ref[...], preferred_element_type=f32)
         gate[...] = jax.nn.sigmoid(logits) * chosen
         delta[...] = jnp.zeros_like(delta)
 
-    x = x_buf[slot]
-    u = u_buf[slot]
-    tokens = x.shape[0]
-    which = lax.rem(pair, 2)
-    up = jnp.concatenate([w_up[which, 0], w_up[which, 1]], axis=1)
-    down = w_down[which]
-    pre_act = jnp.dot(x, up, preferred_element_type=f32)
-    pulled = contract(u, down, 1, 1)
-    lanes = lax.broadcasted_iota(jnp.int32, gate.shape, 1)
-    gates = gate[...]
-    gate_a = jnp.sum(jnp.where(lanes == pair, gates, 0.0), axis=1, keepdims=True)
-    gate_b = jnp.sum(jnp.where(lanes == pairs + pair, gates, 0.0), axis=1, keepdims=True)
-    spread_gate = jnp.concatenate(
-        [jnp.broadcast_to(gate_a, (tokens, FF)), jnp.broadcast_to(gate_b, (tokens, FF))], axis=1
-    )
-    square = pre_act * pre_act
-    bent = jnp.tanh(tanh_scale * pre_act * (1.0 + cubic * square))
-    hidden = (0.5 * pre_act * (1.0 + bent)).astype(bf16).astype(f32)
-    slope = 0.5 * (1.0 + bent) + 0.5 * pre_act * (1.0 - bent * bent) * (
-        tanh_scale * (1.0 + 3.0 * cubic * square)
-    )
-    felt = hidden * pulled
-    felt_a = jnp.sum(felt[:, :FF], axis=1, keepdims=True)
-    felt_b = jnp.sum(felt[:, FF:], axis=1, keepdims=True)
-    kept = jnp.where(lanes == pair, felt_a, delta[...])
-    delta[...] = jnp.where(lanes == pairs + pair, felt_b, kept)
-    gated = (spread_gate * hidden).astype(bf16)
-    hidden_delta = (spread_gate * pulled * slope).astype(bf16)
-    y_new = jnp.dot(gated, down, preferred_element_type=f32)
-    dx_new = contract(hidden_delta, up, 1, 1)
-    gd_new = contract(gated, u, 0, 0)
-    gu_new = jnp.dot(x_turned[...], hidden_delta, preferred_element_type=f32)
-
     @pl.when(pair == 0)
     def _():
         if chained:
-            y_acc[...] = y_prev[...].astype(f32) + y_new
-            dx_acc[...] = dx_prev[...].astype(f32) + dx_new
+            y_acc[...] = y_prev[...].astype(f32)
+            dx_acc[...] = dx_prev[...].astype(f32)
         else:
-            y_acc[...] = y_new
-            dx_acc[...] = dx_new
-
-    @pl.when(pair > 0)
-    def _():
-        y_acc[...] += y_new
-        dx_acc[...] += dx_new
+            y_acc[...] = jnp.zeros_like(y_acc)
+            dx_acc[...] = jnp.zeros_like(dx_acc)
+
+    tokens = x_buf.shape[1]
+    rows = tokens // 2
+    which = lax.rem(pair, 2)
+    up = w_up[which]
+    down = w_down[which]
+    lanes = lax.broadcasted_iota(jnp.int32, (rows, GATE_LANES), 1)
+    cuts = [pl.ds(c * rows, rows) for c in range(2)]
+
+    def first(cut):
+        pre_act = jnp.dot(x_buf[slot, cut], up, preferred_element_type=f32)
+        return pre_act, jnp.dot(u_buf[slot, cut], down, preferred_element_type=f32)
+
+    def bend(cut, pre_act, pulled):
+        gates = gate[cut]
+        gate_a = jnp.sum(jnp.where(lanes == pair, gates, 0.0), axis=1, keepdims=True)
+        gate_b = jnp.sum(jnp.where(lanes == pairs + pair, gates, 0.0), axis=1, keepdims=True)
+        spread_gate = jnp.concatenate(
+            [jnp.broadcast_to(gate_a, (rows, FF)), jnp.broadcast_to(gate_b, (rows, FF))], axis=1
+        )
+        square = pre_act * pre_act
+        bent = jnp.tanh(pre_act * (tanh_scale + tanh_scale * cubic * square))
+        half = 0.5 + 0.5 * bent
+        hidden = (pre_act * half).astype(bf16).astype(f32)
+        slope = half + (0.5 * pre_act) * (1.0 - bent * bent) * (
+            tanh_scale + 3.0 * tanh_scale * cubic * square
+        )
+        felt = hidden * pulled
+        felt_a = jnp.sum(felt[:, :FF], axis=1, keepdims=True)
+        felt_b = jnp.sum(felt[:, FF:], axis=1, keepdims=True)
+        kept = jnp.where(lanes == pair, felt_a, delta[cut])
+        delta[cut] = jnp.where(lanes == pairs + pair, felt_b, kept)
+        gated_buf[cut] = (spread_gate * hidden).astype(bf16)
+        hidden_buf[cut] = (spread_gate * pulled * slope).astype(bf16)
+
+    def second(cut):
+        y_acc[cut] += contract(gated_buf[cut], down, 1, 1)
+        dx_acc[cut] += contract(hidden_buf[cut], up, 1, 1)
+
+    ready = first(cuts[0])
+    for c, cut in enumerate(cuts):
+        later = first(cuts[c + 1]) if c + 1 < 2 else None
+        bend(cut, *ready)
+        second(cut)
+        ready = later
+    gd_new = jnp.dot(u_turned[...], gated_buf[...], preferred_element_type=f32)
+    gu_new = jnp.dot(x_turned[...], hidden_buf[...], preferred_element_type=f32)
+
+    def put(gu_out, gd_out):
+        if closed:
+            for side in (0, 1):
+                grads[side][0, :, :FF] = gu_out[:, side * FF : (side + 1) * FF].astype(bf16)
+                grads[side][0, :, FF:] = gd_out[:, side * FF : (side + 1) * FF].astype(bf16)
+        else:
+            grads[0][0] = gu_out
+            grads[1][0] = gd_out
 
     if blocks == 1:
         if opened:
             gd_new = gd_prev[0] + gd_new
             gu_new = gu_prev[0] + gu_new
-        gd_now, gu_now = gd_new, gu_new
+        put(gu_new, gd_new)
     else:
 
         @pl.when(step == 0)
         def _():
             if opened:
-                gdown[pair] = gd_prev[0] + gd_new
-                gup[pair] = gu_prev[0] + gu_new
+                gdown[pair] = gd_prev[0]
+                gup[pair] = gu_prev[0]
             else:
-                gdown[pair] = gd_new
-                gup[pair] = gu_new
-
-        @pl.when(step > 0)
+                gdown[pair] = jnp.zeros_like(gd_new)
+                gup[pair] = jnp.zeros_like(gu_new)
+
+        gdown[pair] += gd_new
+        gup[pair] += gu_new
+
+        @pl.when(step == blocks - 1)
         def _():
-            gdown[pair] += gd_new
-            gup[pair] += gu_new
-
-        gd_now, gu_now = None, None
-
-    @pl.when(step == blocks - 1)
-    def _():
-        gu_out = gup[pair] if gu_now is None else gu_now
-        gd_out = gdown[pair] if gd_now is None else gd_now
-        if closed:
-            grads[0][0] = gu_out[:, :FF].astype(bf16)
-            grads[1][0] = gu_out[:, FF:].astype(bf16)
-            grads[2][0] = gd_out[:FF].astype(bf16)
-            grads[3][0] = gd_out[FF:].astype(bf16)
-        else:
-            grads[0][0] = gu_out
-            grads[1][0] = gd_out
+            put(gup[pair], gdown[pair])
 
     @pl.when(pair == pairs - 1)
     def _():
@@ -247,7 +247,7 @@
             gr_ref[...] = gr_acc[...]
 
 
-def run_experts(xs, us, ms, select, router, first, second, previous, carried, finish):
+def run_experts(xs, ums, select, router, first, second, previous, carried, finish):
     blocks = len(xs)
     local = first[0].shape[0]
     pairs = 2 * local
@@ -267,33 +267,29 @@
         return (jnp.where(i == blocks - 1, j, 0), 0, 0)
 
     anywhere = pl.BlockSpec(memory_space=pl.ANY)
-    in_specs = [anywhere] * (3 * blocks) + [
+    in_specs = [anywhere] * (2 * blocks) + [
         pl.BlockSpec((experts, GATE_LANES), whole),
         pl.BlockSpec((D, GATE_LANES), whole),
-        *[anywhere] * 8,
+        *[anywhere] * 4,
     ]
-    operands = [*xs, *us, *ms, select, router, *first, *second]
+    operands = [*xs, *ums, select, router, *first, *second]
     if previous is not None:
         in_specs += [pl.BlockSpec((tokens, D), block)] * 2
         operands += list(previous)
     if carried is not None:
         in_specs += [
             pl.BlockSpec((1, D, 2 * FF), opening),
-            pl.BlockSpec((1, 2 * FF, D), opening),
+            pl.BlockSpec((1, D, 2 * FF), opening),
             pl.BlockSpec((D, GATE_LANES), whole),
         ]
         operands += list(carried)
     out_shape = [jax.ShapeDtypeStruct((blocks * tokens, D), bf16)] * 2
     out_specs = [pl.BlockSpec((tokens, D), block)] * 2
     if finish:
-        out_shape += [jax.ShapeDtypeStruct((pairs, D, FF), bf16)] * 2
-        out_shape += [jax.ShapeDtypeStruct((pairs, FF, D), bf16)] * 2
-        out_specs += [pl.BlockSpec((1, D, FF), closing)] * 2
-        out_specs += [pl.BlockSpec((1, FF, D), closing)] * 2
+        out_shape += [jax.ShapeDtypeStruct((pairs, D, 2 * FF), bf16)] * 2
     else:
-        out_shape += [jax.ShapeDtypeStruct((pairs, D, 2 * FF), f32)]
-        out_shape += [jax.ShapeDtypeStruct((pairs, 2 * FF, D), f32)]
-        out_specs += [pl.BlockSpec((1, D, 2 * FF), closing), pl.BlockSpec((1, 2 * FF, D), closing)]
+        out_shape += [jax.ShapeDtypeStruct((pairs, D, 2 * FF), f32)] * 2
+    out_specs += [pl.BlockSpec((1, D, 2 * FF), closing)] * 2
     out_shape.append(jax.ShapeDtypeStruct((D, GATE_LANES), f32))
     out_specs.append(pl.BlockSpec((D, GATE_LANES), whole))
     kept = pairs if blocks > 1 else 1
@@ -310,27 +306,270 @@
             pltpu.VMEM((2, tokens, D), bf16),
             pltpu.VMEM((2, tokens, experts), bf16),
             pltpu.SemaphoreType.DMA((2, 3)),
-            pltpu.VMEM((2, 2, D, FF), bf16),
-            pltpu.VMEM((2, 2 * FF, D), bf16),
+            pltpu.VMEM((2, D, 2 * FF), bf16),
+            pltpu.VMEM((2, D, 2 * FF), bf16),
             pltpu.SemaphoreType.DMA((2, 4)),
             pltpu.VMEM((tokens, D), f32),
             pltpu.VMEM((tokens, D), f32),
             pltpu.VMEM((kept, D, 2 * FF), f32),
-            pltpu.VMEM((kept, 2 * FF, D), f32),
+            pltpu.VMEM((kept, D, 2 * FF), f32),
+            pltpu.VMEM((D, tokens), bf16),
             pltpu.VMEM((D, tokens), bf16),
             pltpu.VMEM((tokens, GATE_LANES), f32),
             pltpu.VMEM((tokens, GATE_LANES), f32),
             pltpu.VMEM((D, GATE_LANES), f32),
+            pltpu.VMEM((tokens, 2 * FF), bf16),
+            pltpu.VMEM((tokens, 2 * FF), bf16),
         ],
         compiler_params=pltpu.CompilerParams(
             dimension_semantics=("arbitrary", "arbitrary"),
             vmem_limit_bytes=56 * 1024 * 1024,
         ),
         cost_estimate=pl.CostEstimate(
-            flops=blocks * tokens * D, bytes_accessed=0, transcendentals=0
+            flops=12 * blocks * tokens * D * FF * pairs, bytes_accessed=0, transcendentals=0
         ),
         name="experts",
     )(*operands)
+
+
+def column(values, index):
+    lanes = lax.broadcasted_iota(jnp.int32, values.shape, 1)
+    return jnp.sum(jnp.where(lanes == index, values, 0.0), axis=1, keepdims=True)
+
+
+def head_probs(query, key, segment_col, segment_row):
+    raw = contract(query, key, 1, 1) * DH ** (-0.5)
+    rows = lax.broadcasted_iota(jnp.int32, raw.shape, 0)
+    columns = lax.broadcasted_iota(jnp.int32, raw.shape, 1)
+    allowed = jnp.logical_and(columns <= rows, segment_col == segment_row)
+    scores = jnp.where(allowed, raw, masked_value)
+    powers = jnp.exp(scores - jnp.max(scores, axis=1, keepdims=True))
+    return powers * (1.0 / jnp.sum(powers, axis=1, keepdims=True))
+
+
+def head_sigmoids(head, chosen_ref, sigmoids, expert):
+    first, second = chosen_ref[0, :, 0:1], chosen_ref[0, :, 1:2]
+    chosen = jnp.logical_or(first == expert, second == expert).astype(f32)
+    half = sigmoids.shape[1] // 2
+    place = head * NE + expert
+    return chosen, column(sigmoids[:, :half], place), column(sigmoids[:, half:], place)
+
+
+def part(expert):
+    return slice(expert * DH, (expert + 1) * DH)
+
+
+def attend_kernel(
+    normed_ref,
+    query_weight,
+    key_weight,
+    value_weight,
+    selectors,
+    chosen_ref,
+    segment_col,
+    segment_row,
+    query_ref,
+    key_ref,
+    values_ref,
+    low_ref,
+    mixed_ref,
+    spread_ref,
+    sigmoids_ref,
+):
+    head = pl.program_id(0)
+    normed = normed_ref[...]
+
+    @pl.when(head == 0)
+    def _():
+        sigmoids_ref[...] = jax.nn.sigmoid(
+            jnp.dot(normed, selectors[...], preferred_element_type=f32)
+        )
+
+    query = jnp.dot(normed, query_weight[...], preferred_element_type=f32).astype(bf16)
+    key = jnp.dot(normed, key_weight[...], preferred_element_type=f32).astype(bf16)
+    query_ref[...] = query
+    key_ref[...] = key
+    values_ref[...] = jnp.dot(normed, value_weight[...], preferred_element_type=f32)
+    sigmoids = sigmoids_ref[...]
+    gates = [head_sigmoids(head, chosen_ref, sigmoids, e) for e in range(NE)]
+    low = gates[0][0] * gates[0][1] * values_ref[:, part(0)]
+    for e in range(1, NE):
+        low = low + gates[e][0] * gates[e][1] * values_ref[:, part(e)]
+    low = low.astype(bf16)
+    low_ref[...] = low
+    probs = head_probs(query, key, segment_col[...], segment_row[...]).astype(bf16)
+    mixed = jnp.dot(probs, low, preferred_element_type=f32)
+    mixed_ref[...] = mixed
+    for e in range(NE):
+        spread_ref[:, part(e)] = (gates[e][0] * gates[e][2] * mixed).astype(bf16)
+
+
+def attend_specs(tokens):
+    whole = pl.BlockSpec((tokens, D), lambda h: (0, 0))
+    narrow = pl.BlockSpec((tokens, DH), lambda h: (0, h))
+    wide = pl.BlockSpec((tokens, NE * DH), lambda h: (0, h))
+    rest = [
+        pl.BlockSpec((1, tokens, 2), lambda h: (h, 0, 0)),
+        pl.BlockSpec((tokens, 1), lambda h: (0, 0)),
+        pl.BlockSpec((1, tokens), lambda h: (0, 0)),
+    ]
+    sigmoids = pl.BlockSpec((tokens, 256), lambda h: (0, 0))
+    return whole, narrow, wide, rest, sigmoids
+
+
+def attend(normed, query_weight, key_weight, value_weight, selectors, chosen, segments):
+    tokens = normed.shape[0]
+    whole, narrow, wide, rest, sigmoids = attend_specs(tokens)
+    return pl.pallas_call(
+        attend_kernel,
+        grid=(H,),
+        in_specs=[
+            whole,
+            pl.BlockSpec((D, DH), lambda h: (0, h)),
+            pl.BlockSpec((D, DH), lambda h: (0, h)),
+            pl.BlockSpec((D, NE * DH), lambda h: (0, h)),
+            pl.BlockSpec((D, 256), lambda h: (0, 0)),
+            *rest,
+        ],
+        out_specs=[narrow, narrow, wide, narrow, narrow, wide, sigmoids],
+        out_shape=[
+            jax.ShapeDtypeStruct((tokens, H * DH), bf16),
+            jax.ShapeDtypeStruct((tokens, H * DH), bf16),
+            jax.ShapeDtypeStruct((tokens, H * NE * DH), f32),
+            jax.ShapeDtypeStruct((tokens, H * DH), bf16),
+            jax.ShapeDtypeStruct((tokens, H * DH), f32),
+            jax.ShapeDtypeStruct((tokens, H * NE * DH), bf16),
+            jax.ShapeDtypeStruct((tokens, 256), f32),
+        ],
+        compiler_params=pltpu.CompilerParams(vmem_limit_bytes=48 * 1024 * 1024),
+        cost_estimate=pl.CostEstimate(
+            flops=2 * tokens * H * DH * (D * (NE + 2) + 2 * tokens),
+            bytes_accessed=0,
+            transcendentals=0,
+        ),
+        name="attend",
+    )(
+        normed,
+        query_weight,
+        key_weight,
+        value_weight,
+        selectors,
+        chosen,
+        segments[:, None],
+        segments[None, :],
+    )
+
+
+def attend_back_kernel(
+    middle_ref,
+    output_weight,
+    query_ref,
+    key_ref,
+    low_ref,
+    mixed_ref,
+    values_ref,
+    sigmoids_ref,
+    chosen_ref,
+    segment_col,
+    segment_row,
+    query_delta,
+    key_delta,
+    values_delta,
+    select_delta,
+    spread_buf,
+    value_acc,
+    output_acc,
+):
+    head = pl.program_id(0)
+
+    @pl.when(head == 0)
+    def _():
+        value_acc[...] = jnp.zeros_like(value_acc)
+        output_acc[...] = jnp.zeros_like(output_acc)
+
+    spread_buf[...] = contract(middle_ref[...], output_weight[...], 1, 1)
+    sigmoids = sigmoids_ref[...]
+    gates = [head_sigmoids(head, chosen_ref, sigmoids, e) for e in range(NE)]
+    query, key, low = query_ref[...], key_ref[...], low_ref[...]
+    mixed = mixed_ref[...]
+    mixed_delta = gates[0][0] * gates[0][2] * spread_buf[:, part(0)]
+    for e in range(1, NE):
+        mixed_delta = mixed_delta + gates[e][0] * gates[e][2] * spread_buf[:, part(e)]
+    mixed_delta = mixed_delta.astype(bf16)
+    probs = head_probs(query, key, segment_col[...], segment_row[...])
+    weight_delta = contract(mixed_delta, low, 1, 1)
+    pulled = jnp.sum(probs * weight_delta, axis=1, keepdims=True)
+    score_delta = (probs * (weight_delta - pulled)).astype(bf16)
+    query_delta[...] = (
+        jnp.dot(score_delta, key, preferred_element_type=f32) * DH ** (-0.5)
+    ).astype(bf16)
+    key_delta[...] = (contract(score_delta, query, 0, 0) * DH ** (-0.5)).astype(bf16)
+    value_delta = contract(probs.astype(bf16), mixed_delta, 0, 0)
+    lanes = lax.broadcasted_iota(jnp.int32, value_acc.shape, 1)
+    for e in range(NE):
+        chosen, value_sigmoid, output_sigmoid = gates[e]
+        values_delta[:, part(e)] = (chosen * value_sigmoid * value_delta).astype(bf16)
+        felt = jnp.sum(value_delta * values_ref[:, part(e)], axis=1, keepdims=True)
+        felt = felt * chosen * value_sigmoid * (1.0 - value_sigmoid)
+        value_acc[...] = jnp.where(lanes == head * NE + e, felt, value_acc[...])
+        felt = jnp.sum(spread_buf[:, part(e)] * mixed, axis=1, keepdims=True)
+        felt = felt * chosen * output_sigmoid * (1.0 - output_sigmoid)
+        output_acc[...] = jnp.where(lanes == head * NE + e, felt, output_acc[...])
+
+    @pl.when(head == H - 1)
+    def _():
+        half = value_acc.shape[1]
+        select_delta[:, :half] = value_acc[...].astype(bf16)
+        select_delta[:, half:] = output_acc[...].astype(bf16)
+
+
+def attend_back(middle_low, output_weight, query, key, low, mixed, values, sigmoids, chosen, segments):
+    tokens = middle_low.shape[0]
+    whole, narrow, wide, rest, sigmoid_spec = attend_specs(tokens)
+    return pl.pallas_call(
+        attend_back_kernel,
+        grid=(H,),
+        in_specs=[
+            whole,
+            pl.BlockSpec((NE * DH, D), lambda h: (h, 0)),
+            narrow,
+            narrow,
+            narrow,
+            narrow,
+            wide,
+            sigmoid_spec,
+            *rest,
+        ],
+        out_specs=[narrow, narrow, wide, sigmoid_spec],
+        out_shape=[
+            jax.ShapeDtypeStruct((tokens, H * DH), bf16),
+            jax.ShapeDtypeStruct((tokens, H * DH), bf16),
+            jax.ShapeDtypeStruct((tokens, H * NE * DH), bf16),
+            jax.ShapeDtypeStruct((tokens, 256), bf16),
+        ],
+        scratch_shapes=[
+            pltpu.VMEM((tokens, NE * DH), f32),
+            pltpu.VMEM((tokens, 128), f32),
+            pltpu.VMEM((tokens, 128), f32),
+        ],
+        compiler_params=pltpu.CompilerParams(vmem_limit_bytes=48 * 1024 * 1024),
+        cost_estimate=pl.CostEstimate(
+            flops=2 * tokens * H * DH * (D * NE + 5 * tokens), bytes_accessed=0, transcendentals=0
+        ),
+        name="attend_back",
+    )(
+        middle_low,
+        output_weight,
+        query,
+        key,
+        low,
+        mixed,
+        values,
+        sigmoids,
+        chosen,
+        segments[:, None],
+        segments[None, :],
+    )
 
 
 class Moves:
@@ -574,7 +813,9 @@
             self.out = assemble(cube, [*self.halves, *theirs], self.cuts)
 
     def tied(self, value):
-        if hasattr(self, "total"):
+        if hasattr(self, "halves"):
+            *self.halves, value = tie(*self.halves, value)
+        elif hasattr(self, "total"):
             self.total, value = tie(self.total, value)
         else:
             self.kept, self.sent, value = tie(self.kept, self.sent, value)
@@ -593,13 +834,19 @@
         return 2 * self.cube.bits + 2
 
 
-def sum_small(moves, value):
+def small_steps(moves):
+    steps = []
     for axis, size in (("dp", moves.dp), ("expert", moves.ex)):
         span = 1
         while span < size:
-            value = value + lax.ppermute(value, axis, [(i, i ^ span) for i in range(size)])
+            steps.append((axis, span))
             span *= 2
-    return value
+    return steps
+
+
+def sum_step(moves, value, axis, span):
+    size = moves.dp if axis == "dp" else moves.ex
+    return value + lax.ppermute(value, axis, [(i, i ^ span) for i in range(size)])
 
 
 def on_device(
@@ -636,71 +883,44 @@
     far = [s for s in moves.plane[1:] if 0 not in s]
     routed_low = routed.astype(bf16)
 
-    ups, downs = [up_weight], [down_weight]
-    ups.append(moves.over_hi(up_weight))
-    downs.append(moves.over_hi(down_weight))
-    us = {s: moves.over_plane(upstream_low, s) for s in near}
-    ms = {s: moves.over_plane(routed_low, s) for s in moves.plane[1:]}
+    weights = [jnp.concatenate([up_weight, jnp.swapaxes(down_weight, 1, 2)], axis=2)]
+    weights.append(moves.over_hi(weights[0]))
+    core_weights = [moves.over_core(weights[0])]
+    masks = jnp.pad(routed_low, ((0, 0), (0, -experts % 128)))
+    ums = {moves.plane[0]: jnp.concatenate([upstream_low, masks], axis=1)}
+    ums[moves.plane[0]], weights[0] = tie(ums[moves.plane[0]], weights[0])
+    for s in near:
+        ums[s] = moves.over_plane(ums[moves.plane[0]], s)
 
     inputs = hidden_in[0].astype(f32)
     att_rms = inverse_rms(inputs)
     normed_low = (inputs * att_rms * attention_gain).astype(bf16)
-    query_low = (
-        jnp.dot(normed_low, query_weight, preferred_element_type=f32)
-        .astype(bf16)
-        .reshape(length, H, DH)
+    narrow = 128
+    margin = ((0, 0), (0, narrow - H * NE))
+    selectors = jnp.concatenate(
+        [jnp.pad(value_selector, margin), jnp.pad(output_selector, margin)], axis=1
     )
-    key_low = (
-        jnp.dot(normed_low, key_weight, preferred_element_type=f32)
-        .astype(bf16)
-        .reshape(length, H, DH)
-    )
-    values_all = jnp.dot(normed_low, value_weight, preferred_element_type=f32).reshape(
-        length, H, NE, DH
-    )
-    value_sigmoid = jax.nn.sigmoid(
-        jnp.dot(normed_low, value_selector, preferred_element_type=f32)
-    ).reshape(length, H, NE)
-    output_sigmoid = jax.nn.sigmoid(
-        jnp.dot(normed_low, output_selector, preferred_element_type=f32)
-    ).reshape(length, H, NE)
-    chosen_mask = jnp.sum(
-        (head_experts[0][:, :, :, None] == jnp.arange(NE, dtype=jnp.int32)).astype(f32),
-        axis=2,
-    )
-    value_gate = value_sigmoid * chosen_mask
-    output_gate = output_sigmoid * chosen_mask
-    value_low = jnp.sum(value_gate[..., None] * values_all, axis=2).astype(bf16)
-    positions = jnp.arange(length, dtype=jnp.int32)
+    head_chosen = jnp.swapaxes(head_experts[0], 0, 1)
     segments = segment_ids[0]
-    allowed = (positions[None, :] <= positions[:, None]) & (segments[None, :] == segments[:, None])
-    scores = masked_scores(query_low, key_low, allowed)
-    log_total = jax.nn.logsumexp(scores, axis=-1, keepdims=True)
-    probs_low = jnp.exp(scores - log_total).astype(bf16)
-    mixed_heads = jnp.einsum("hqk,khd->qhd", probs_low, value_low, preferred_element_type=f32)
-    spread_low = (
-        (output_gate[..., None] * mixed_heads[:, :, None, :])
-        .astype(bf16)
-        .reshape(length, H * NE * DH)
+    query_low, key_low, values_all, value_low, mixed, spread_low, sigmoids = attend(
+        normed_low, query_weight, key_weight, value_weight, selectors, head_chosen, segments
     )
     middle_rows = inputs + jnp.dot(spread_low, output_weight, preferred_element_type=f32)
     moe_rms = inverse_rms(middle_rows)
     moe_low = (middle_rows * moe_rms * mixture_gain).astype(bf16)
 
-    moe_low, ups[1], downs[1] = tie(moe_low, ups[1], downs[1])
     home = moves.plane[0]
+    moe_low, *values = tie(moe_low, *[ums[s] for s in near])
     xs = {home: moe_low}
-    us[home] = upstream_low
-    ms[home] = routed_low
-    for s in near:
+    for s, value in zip(near, values):
+        ums[s] = value
         xs[s] = moves.over_plane(moe_low, s)
-    core_ups = [moves.over_core(u) for u in ups[:2]]
-    core_downs = [moves.over_core(d) for d in downs[:2]]
-    ups.append(moves.over_hi(ups[1]))
-    downs.append(moves.over_hi(downs[1]))
+    weights[1], xs[home] = tie(weights[1], moe_low)
+    core_weights.append(moves.over_core(weights[1]))
+    weights.append(moves.over_hi(weights[1]))
 
     def slot_weights(s):
-        return (ups[s], core_ups[s], downs[s], core_downs[s])
+        return weights[s], core_weights[s]
 
     def selection(slots):
         columns = []
@@ -709,13 +929,13 @@
                 owner = (moves.dp_index ^ core) * moves.ex + (moves.hi - s) % nh * 2 + moves.lo
                 columns += [owner * local + k for k in range(local)]
         columns += [jnp.int32(-1)] * (GATE_LANES - len(columns))
-        select = (expert_range[:, None] == jnp.stack(columns)[None, :]).astype(bf16)
-        return select, jnp.dot(router_weight, select, preferred_element_type=f32).astype(bf16)
+        rows = jnp.arange(experts + -experts % 128, dtype=jnp.int32)
+        select = (rows[:, None] == jnp.stack(columns)[None, :]).astype(bf16)
+        router = jnp.dot(router_weight, select[:experts], preferred_element_type=f32)
+        return select, router.astype(bf16)
 
     sums = {}
-    router_width = experts + -experts % 128
-    router_sum = jnp.zeros((D, router_width), f32)
-    mine_slots, theirs_slots = [None] * nh, [None] * nh
+    router_sum = jnp.zeros((D, experts + -experts % 128), f32)
 
     def visit(offsets, phase, carried, finish):
         slots = (2 * phase, 2 * phase + 1)
@@ -728,8 +948,7 @@
             )
         y, dx, *grads = run_experts(
             [xs[s] for s in offsets],
-            [us[s] for s in offsets],
-            [ms[s] for s in offsets],
+            [ums[s] for s in offsets],
             select,
             router,
             slot_weights(slots[0]),
@@ -758,32 +977,26 @@
         for turn, offsets in enumerate(calls):
             grads = visit(offsets, phase, grads, turn == len(calls) - 1)
             if phase == 0 and turn == 0:
-                values = tie(grads[0], moe_low, upstream_low, *[xs[s] for s in near])
-                grads[0], far_x, far_u = values[:3]
+                values = tie(grads[0], moe_low, ums[home], *[xs[s] for s in near])
+                grads[0], far_x, far_um = values[:3]
                 for s, value in zip(near, values[3:]):
                     xs[s] = value
                 for s in far:
                     xs[s] = moves.over_plane(far_x, s)
-                    us[s] = moves.over_plane(far_u, s)
+                    ums[s] = moves.over_plane(far_um, s)
             if phase == 0 and turn == 1 and nh > 2:
-                grads[0], ups[2], downs[2] = tie(grads[0], ups[2], downs[2])
+                grads[0], weights[2] = tie(grads[0], weights[2])
                 for s in range(3, nh):
-                    ups.append(moves.over_hi(ups[-1]))
-                    downs.append(moves.over_hi(downs[-1]))
-                core_ups.append(moves.over_core(ups[2]))
-                core_downs.append(moves.over_core(downs[2]))
+                    weights.append(moves.over_hi(weights[-1]))
+                core_weights.append(moves.over_core(weights[2]))
             if phase == 0 and turn == len(calls) - 2 and nh > 2:
-                values = tie(grads[0], *ups[3:], *downs[3:])
-                grads[0] = values[0]
-                ups[3:] = values[1 : nh - 2]
-                downs[3:] = values[nh - 2 :]
-                core_ups += [moves.over_core(u) for u in ups[3:]]
-                core_downs += [moves.over_core(d) for d in downs[3:]]
+                grads[0], core_weights[2] = tie(grads[0], core_weights[2])
+                core_weights += [moves.over_core(w) for w in weights[3:]]
             if phase > 0 and turn == 0:
-                grads[0], *held = tie(grads[0], *held)
-                held = [moves.over_hi(h) for h in held]
+                grads[0], held = tie(grads[0], held)
+                held = moves.over_hi(held)
             if phase > 0 and turn == len(calls) - 2:
-                grads[0], *held = tie(grads[0], *held)
+                grads[0], held = tie(grads[0], held)
             if last:
                 if later:
                     grads[0], *late = tie(grads[0], *[sums[s][0] for s in later])
@@ -793,23 +1006,20 @@
                 for s in later:
                     sent_back[s] = [moves.over_plane(sums[s][1], s, back=True)]
         router_sum = router_sum + jnp.dot(
-            grads[4].astype(bf16),
-            jnp.pad(chosen_by[phase][0].T, ((0, 0), (0, router_width - experts))),
+            grads[2].astype(bf16),
+            chosen_by[phase][0].T,
             preferred_element_type=f32,
         )
-        gu_mine, gu_theirs, gd_mine, gd_theirs = grads[:4]
-        gu_got, gd_got = moves.over_core(gu_theirs), moves.over_core(gd_theirs)
+        mine, got = grads[0], moves.over_core(grads[1])
         for k in range(2):
             s = 2 * phase + k
-            cut = slice(k * local, (k + 1) * local)
-            parts = [(gu_mine[cut], gu_got[cut]), (gd_mine[cut], gd_got[cut])]
+            parts = [grad[k * local : (k + 1) * local] for grad in (mine, got)]
             if s == 0:
                 first_parts = parts
                 continue
             if held is not None:
-                arrived = held if k == 0 else [moves.over_hi(h) for h in held]
-                parts = [(*p, h) for p, h in zip(parts, arrived)]
-            held = [add_low(*p) for p in parts]
+                parts.append(held if k == 0 else moves.over_hi(held))
+            held = add_low(*parts)
 
     expert_delta = sums[home][1].astype(f32)
     for s in moves.plane[1:]:
@@ -823,74 +1033,25 @@
     out_sum = Sum(cube, grad_blocks(cube, spread_low, [middle_low]), [(0, D)])
     middle_sent = out_sum.tied(middle_low)
     out_sum.step()
-    spread_delta = jnp.einsum(
-        "td,cd->tc", middle_sent, output_weight, preferred_element_type=f32
-    ).reshape(length, H, NE, DH)
-    mixed_delta = jnp.sum(output_gate[..., None] * spread_delta, axis=2).astype(bf16)
-    oselect_delta = (
-        (
-            jnp.sum(spread_delta * mixed_heads[:, :, None, :], axis=3)
-            * chosen_mask
-            * output_sigmoid
-            * (1.0 - output_sigmoid)
-        )
-        .astype(bf16)
-        .reshape(length, H * NE)
+    query_delta, key_delta, values_delta, select_delta = attend_back(
+        middle_sent,
+        output_weight,
+        query_low,
+        key_low,
+        value_low,
+        mixed,
+        values_all,
+        sigmoids,
+        head_chosen,
+        segments,
     )
-    mixed_delta = out_sum.tied(mixed_delta)
+    values_delta = out_sum.tied(values_delta)
+    held, values_delta = tie(held, values_delta)
+    *outputs_back, values_delta = tie(*[sent_back[s][1] for s in moves.plane[1:]], values_delta)
     out_sum.step()
-    scores = masked_scores(query_low, key_low, allowed)
-    probs_full = jnp.exp(scores - log_total)
-    probs_again = probs_full.astype(bf16)
-    weight_delta = jnp.einsum("qhd,khd->hqk", mixed_delta, value_low, preferred_element_type=f32)
-    score_delta = (
-        probs_full * (weight_delta - jnp.sum(probs_full * weight_delta, axis=-1, keepdims=True))
-    ).astype(bf16)
-    value_delta = jnp.einsum("hqk,qhd->khd", probs_again, mixed_delta, preferred_element_type=f32)
-    values_delta = (
-        (value_gate[..., None] * value_delta[:, :, None, :])
-        .astype(bf16)
-        .reshape(length, H * NE * DH)
-    )
     value_sum = Sum(cube, grad_blocks(cube, normed_low, [values_delta]), [(0, H * NE * DH)])
-    score_delta = out_sum.tied(score_delta)
-    score_delta = value_sum.tied(score_delta)
-    *held, score_delta = tie(*held, score_delta)
-    last_held = [moves.over_hi(h) for h in held]
-    *outputs_back, score_delta = tie(*[sent_back[s][1] for s in moves.plane[1:]], score_delta)
-    out_sum.step()
     value_sum.step()
-    query_delta = (
-        (
-            jnp.einsum("hqk,khd->qhd", score_delta, key_low, preferred_element_type=f32)
-            * DH ** (-0.5)
-        )
-        .astype(bf16)
-        .reshape(length, H * DH)
-    )
-    key_delta = (
-        (
-            jnp.einsum("hqk,qhd->khd", score_delta, query_low, preferred_element_type=f32)
-            * DH ** (-0.5)
-        )
-        .astype(bf16)
-        .reshape(length, H * DH)
-    )
-    vselect_delta = (
-        (
-            jnp.sum(value_delta[:, :, None, :] * values_all, axis=3)
-            * chosen_mask
-            * value_sigmoid
-            * (1.0 - value_sigmoid)
-        )
-        .astype(bf16)
-        .reshape(length, H * NE)
-    )
-    narrow = 128
-    margin = ((0, 0), (0, narrow - H * NE))
-    select_delta = jnp.concatenate(
-        [jnp.pad(vselect_delta, margin), jnp.pad(oselect_delta, margin)], axis=1
-    )
+    query_delta = value_sum.tied(query_delta)
     cuts = [(0, H * DH), (H * DH, H * DH)]
     start = 2 * H * DH
     cuts += [(start, H * NE), (start + narrow, H * NE), (start + 2 * narrow, experts)]
@@ -901,40 +1062,47 @@
     )
     query_sent = rest_sum.tied(query_delta)
     query_sent = out_sum.tied(query_sent)
-    query_sent = value_sum.tied(query_sent)
-    last_held[0], last_held[1], query_sent = tie(*last_held, query_sent)
-    for each in (rest_sum, out_sum, value_sum):
+    for each in (value_sum, rest_sum, out_sum):
         each.step()
     normed_delta = (
         input_term(query_sent, query_weight)
         + input_term(key_delta, key_weight)
         + input_term(values_delta, value_weight)
-    )
-    normed_delta = (
-        normed_delta
-        + input_term(vselect_delta, value_selector)
-        + input_term(oselect_delta, output_selector)
+        + input_term(select_delta, selectors)
     )
     for each in (rest_sum, out_sum, value_sum):
         normed_delta = each.tied(normed_delta)
-    for each in (rest_sum, out_sum, value_sum):
+    grad_attention = jnp.sum(normed_delta * inputs * att_rms, axis=0)
+    small = jnp.stack([grad_attention, grad_mixture, jnp.pad(local_counts, (0, D - experts))])
+    for axis, span in small_steps(moves):
+        small = out_sum.tied(small)
+        small = sum_step(moves, small, axis, span)
+        for each in (out_sum, rest_sum, value_sum):
+            if each.done < each.steps:
+                each.step()
+    while value_sum.done < 2 * cube.bits - 2:
+        for each in (out_sum, rest_sum, value_sum):
+            if each.done < each.steps:
+                each.step()
+    last_held = moves.over_hi(value_sum.tied(held))
+    while value_sum.done < value_sum.steps - 1:
+        for each in (out_sum, rest_sum, value_sum):
+            if each.done < each.steps:
+                each.step()
+    out_sum.out[0] = value_sum.tied(out_sum.out[0])
+    for each in (out_sum, rest_sum, value_sum):
         each.run(each.steps - each.done)
     (grad_output,) = out_sum.out
     (grad_value,) = value_sum.out
     grad_query, grad_key, grad_vselect, grad_oselect, grad_router = rest_sum.out
     input_delta = middle_delta + norm_back(inputs, att_rms, attention_gain, normed_delta)
-    grad_attention = jnp.sum(normed_delta * inputs * att_rms, axis=0)
     output_rows = middle_rows + sums[home][0].astype(f32)
     for value in outputs_back:
         output_rows = output_rows + value.astype(f32)
-    grad_up, grad_down = (
-        h.astype(f32) + a.astype(f32) + b.astype(f32)
-        for h, (a, b) in zip(last_held, first_parts)
-    )
-    small = sum_small(
-        moves,
-        jnp.stack([grad_attention, grad_mixture, jnp.pad(local_counts, (0, D - experts))]),
-    )
+    expert_grads = last_held.astype(f32)
+    for part in first_parts:
+        expert_grads = expert_grads + part.astype(f32)
+    grad_up, grad_down = expert_grads[:, :, :FF], jnp.swapaxes(expert_grads[:, :, FF:], 1, 2)
     new_counts = expert_counts + small[2, :experts].astype(jnp.int32)
     return (
         output_rows.astype(bf16)[None],

time: 679 us -> 568 us (0.84)
  waiting for transfers between devices: 226 us -> 176 us
  matrix products: 46.1 us -> 16.2 us
  local copies, waits for them, and re-layouts: 47.2 us -> 26.2 us
  other arithmetic: 56.7 us -> 44.2 us
  Pallas kernels: 229 us -> 239 us
    ppermute x12 -> x6, waiting for transfers between devices: 58 us -> 9.81 us  [over_hi(): return lax.ppermute(value, 'expert', pairs)]
    pallas_call x0 -> x2, Pallas kernels: none -> 34.6 us  [the longest x1 20.9 us: attend_back(): pl.pallas_call(attend_back_kernel, grid=(H,), in_specs=[whole, pl.BlockSp...]
    ppermute x5 -> x4, waiting for transfers between devices: 0.01 us -> 26.4 us  [over_plane(): return lax.ppermute(value, ('dp', 'expert'), pairs)]
    pallas_call x8, Pallas kernels: 194 us -> 170 us  [run_experts(): pl.pallas_call(functools.partial(experts_kernel, blocks, pairs, previous...]
    dot_general x15 -> x4, matrix products: 23.7 us -> 0.85 us  [the longest x2 0.47 us: on_device(): jnp.dot(grads[2].astype(bf16), chosen_by[phase][0].T, preferred_element_t...]
    ppermute x5 -> x4, waiting for transfers between devices: 19.3 us -> 1.84 us  [over_plane(): return lax.ppermute(value, 'dp', list(enumerate(dp_to)))]
    ppermute x24, waiting for transfers between devices: 106 us -> 91.4 us  [exchange(): return lax.ppermute(value, ('dp', 'expert'), pairs)]
    ppermute x5, waiting for transfers between devices: 18.4 us -> 31 us  [sum_step(): lax.ppermute(value, axis, [(i, i ^ span) for i in range(size)])]
  transfers between devices with their start and end apart: 77 -> 62, of which waited for: 29 -> 28; matrix products, arithmetic and copies ran while one was open for 20% -> 12% of each run, Pallas kernels for 33% -> 40%
where the time goes in v3:
time: 568 us; the launch traced here: 561 us
  Pallas kernels  239 us (42%)
  waiting for transfers between devices  176 us (31%)
  starting transfers between devices  58 us (10%)
  other arithmetic  44.2 us (8%)
  local copies, waits for them, and re-layouts  26.2 us (5%)
  matrix products  16.2 us (3%)
    pallas_call x8, Pallas kernels, run_experts(): pl.pallas_call(functools.partial(experts_kernel, blocks, pairs, previous...  170 us
    ppermute x24, waiting for transfers between devices, exchange(): return lax.ppermute(value, ('dp', 'expert'), pairs)  91.4 us
    ppermute x5, waiting for transfers between devices, sum_step(): lax.ppermute(value, axis, [(i, i ^ span) for i in range(size)])  31 us
    ppermute x4, waiting for transfers between devices, over_plane(): return lax.ppermute(value, ('dp', 'expert'), pairs)  26.4 us
    ppermute x24, starting transfers between devices, exchange(): return lax.ppermute(value, ('dp', 'expert'), pairs)  25.4 us
    unnamed x128, local copies, waits for them, and re-layouts  21.4 us
    pallas_call x3, Pallas kernels, assemble(): pl.pallas_call(functools.partial(assemble_kernel, count, cuts), grid_spec...  21.2 us
    pallas_call x1, Pallas kernels, attend_back(): pl.pallas_call(attend_back_kernel, grid=(H,), in_specs=[whole, pl.BlockSp...  20.9 us
  transfers between devices with their start and end apart: 62, of which 28 were waited for; matrix products, arithmetic and copies ran while one was open for 12% of the time, Pallas kernels for 40%

profile of v3, /device:TPU:0, one launch (start us, length us, event | category | flops | bytes accessed | tf_op | source)
XLA Modules:
  0.0 561.2 jit_solution(120061705406674153)
XLA Ops:
  15.5 13.7 %attend.1 = (bf16[512,512]{1,0:T(8,128)(2,1)S(1)}, bf16[512,512]{1,0:T(8,128)(2,1)S(1)}, f32[512,2560]{1,0:T(8,128)}, bf16[512,512]{1,0:T(8,128)(2,1)S(1)}, f32[...) custom-call(bf16[512,1024]{1,0:T(8,128)(2,1)S(1)} %fusion.3.normed_ref.left_a.left_b, ...), custom_call_target="tpu_custom_call" | custom-call | flops 4294967296 | tf_op jit(solution)/shard_map/attend/pallas_call | solution.py:423
  29.2 7.0 %multiply_reduce_fusion.2 = (f32[512]{0:T(512)S(1)}, f32[512,1024]{1,0:T(8,128)}) fusion(bf16[512,2560]{1,0:T(8,128)(2,1)} %get-tuple-element.149.left_a.left_b, bf16[2560,1024]{1,0:T(8,128)(2,1)S(1)} %bitcast.99, bf16[1,512,1024]{2,1,0:T(8,128)(2,1)S(1)} %copy-done.21), kind=kOutput, calls=%fused_computation.37 | convolution fusion | flops 2686451200 | bytes 11012096 | tf_op jit(solution)/shard_map/dot_general | solution.py:908
  38.1 5.3 collective-permute-done.refs_6_
  48.5 19.9 %experts.8 = (bf16[512,1024]{1,0:T(8,128)(2,1)}, bf16[512,1024]{1,0:T(8,128)(2,1)}, f32[6,1024,256]{2,1,0:T(8,128)}, f32[6,1024,256]{2,1,0:T(8,128)}, f32[1024,16]{1,0:T(8,128)}) custom-call(bf16[512,1024]{1,0:T(8,128)(2,1)} %copy-done.27, bf16[512,1152]{1,0:T(8,128)(2,1)} %fusion.13.refs_1_, bf16[128,16]{1,0:T(8,128)(2,1)} %get-tuple-element.375.refs_2_, ...), custom_call_target="tpu_custom_call" | custom-call | flops 4831838208 | tf_op jit(solution)/shard_map/experts/pallas_call | solution.py:296
  70.6 21.6 %experts.9 = (bf16[512,1024]{1,0:T(8,128)(2,1)}, bf16[512,1024]{1,0:T(8,128)(2,1)}, f32[6,1024,256]{2,1,0:T(8,128)}, f32[6,1024,256]{2,1,0:T(8,128)}, f32[1024,16]{1,0:T(8,128)}) custom-call(bf16[512,1024]{1,0:T(8,128)(2,1)} %collective-permute-done.5.refs_0_, bf16[512,1152]{1,0:T(8,128)(2,1)} %collective-permute-done.1.refs_1_, ...), custom_call_target="tpu_custom_call" | custom-call | flops 4831838208 | tf_op jit(solution)/shard_map/experts/pallas_call | solution.py:296
  96.3 21.4 %experts.10 = (bf16[512,1024]{1,0:T(8,128)(2,1)}, bf16[512,1024]{1,0:T(8,128)(2,1)}, f32[6,1024,256]{2,1,0:T(8,128)}, f32[6,1024,256]{2,1,0:T(8,128)}, f32[1024,16]{1,0:T(8,128)}) custom-call(bf16[512,1024]{1,0:T(8,128)(2,1)} %collective-permute-done.6.refs_0_, bf16[512,1152]{1,0:T(8,128)(2,1)} %collective-permute-done.2.refs_1_, ...), custom_call_target="tpu_custom_call" | custom-call | flops 4831838208 | tf_op jit(solution)/shard_map/experts/pallas_call | solution.py:296
  117.8 26.4 %collective-permute-done.11.refs_0_ = bf16[512,1024]{1,0:T(8,128)(2,1)S(1)} collective-permute-done((bf16[512,1024]{1,0:T(8,128)(2,1)S(1)}, bf16[512,1024]{1,0:T(8,128)(2,1)S(1)}, u32[]{:S(2)}, u32[]{:S(2)}) %collective-permute-start.11) | collective-permute-done | bytes 1048608 | tf_op jit(solution)/shard_map/ppermute | solution.py:611
  145.5 20.5 %experts.11 = (bf16[512,1024]{1,0:T(8,128)(2,1)}, bf16[512,1024]{1,0:T(8,128)(2,1)}, bf16[6,1024,256]{2,1,0:T(8,128)(2,1)}, bf16[6,1024,256]{2,1,0:T(8,128)(2,1)}, f32[1024,16]{1,0:T(8,128)}) custom-call(bf16[512,1024]{1,0:T(8,128)(2,1)} %copy-done.45, bf16[512,1152]{1,0:T(8,128)(2,1)} %copy-done.38, bf16[128,16]{1,0:T(8,128)(2,1)} %get-tuple-element.375.refs_2_, ...), custom_call_target="tpu_custom_call" | custom-call | flops 4831838208 | tf_op jit(solution)/shard_map/experts/pallas_call | solution.py:296
  168.4 6.0 %collective-permute-done.10.refs_7_ = bf16[3,1024,256]{2,1,0:T(8,128)(2,1)} collective-permute-done((bf16[3,1024,256]{2,1,0:T(8,128)(2,1)}, bf16[3,1024,256]{2,1,0:T(8,128)(2,1)}, u32[]{:S(2)}, u32[]{:S(2)}) %collective-permute-start.10) | collective-permute-done | bytes 1572896 | tf_op jit(solution)/shard_map/ppermute | solution.py:591
  174.3 20.6 %experts.12 = (bf16[512,1024]{1,0:T(8,128)(2,1)}, bf16[512,1024]{1,0:T(8,128)(2,1)}, f32[6,1024,256]{2,1,0:T(8,128)}, f32[6,1024,256]{2,1,0:T(8,128)}, f32[1024,16]{1,0:T(8,128)}) custom-call(bf16[512,1024]{1,0:T(8,128)(2,1)} %copy-done.45, bf16[512,1152]{1,0:T(8,128)(2,1)} %copy-done.38, bf16[128,16]{1,0:T(8,128)(2,1)} %get-tuple-element.373.refs_2_, ...), custom_call_target="tpu_custom_call" | custom-call | flops 4831838208 | tf_op jit(solution)/shard_map/experts/pallas_call | solution.py:296
  199.6 22.1 %experts.13 = (bf16[512,1024]{1,0:T(8,128)(2,1)}, bf16[512,1024]{1,0:T(8,128)(2,1)}, f32[6,1024,256]{2,1,0:T(8,128)}, f32[6,1024,256]{2,1,0:T(8,128)}, f32[1024,16]{1,0:T(8,128)}) custom-call(bf16[512,1024]{1,0:T(8,128)(2,1)} %collective-permute-done.5.refs_0_, bf16[512,1152]{1,0:T(8,128)(2,1)} %collective-permute-done.1.refs_1_, ...), custom_call_target="tpu_custom_call" | custom-call | flops 4831838208 | tf_op jit(solution)/shard_map/experts/pallas_call | solution.py:296
  221.8 22.1 %experts.14 = (bf16[512,1024]{1,0:T(8,128)(2,1)}, bf16[512,1024]{1,0:T(8,128)(2,1)}, f32[6,1024,256]{2,1,0:T(8,128)}, f32[6,1024,256]{2,1,0:T(8,128)}, f32[1024,16]{1,0:T(8,128)}) custom-call(bf16[512,1024]{1,0:T(8,128)(2,1)} %collective-permute-done.6.refs_0_, bf16[512,1152]{1,0:T(8,128)(2,1)} %collective-permute-done.2.refs_1_, ...), custom_call_target="tpu_custom_call" | custom-call | flops 4831838208 | tf_op jit(solution)/shard_map/experts/pallas_call | solution.py:296
  246.0 21.9 %experts.15 = (bf16[512,1024]{1,0:T(8,128)(2,1)}, bf16[512,1024]{1,0:T(8,128)(2,1)}, bf16[6,1024,256]{2,1,0:T(8,128)(2,1)}, bf16[6,1024,256]{2,1,0:T(8,128)(2,1)}, f32[1024,16]{1,0:T(8,128)}) custom-call(bf16[512,1024]{1,0:T(8,128)(2,1)} %copy-done.27, bf16[512,1152]{1,0:T(8,128)(2,1)} %fusion.13.refs_1_, bf16[128,16]{1,0:T(8,128)(2,1)} %get-tuple-element.373.refs_2_, ...), custom_call_target="tpu_custom_call" | custom-call | flops 4831838208 | tf_op jit(solution)/shard_map/experts/pallas_call | solution.py:296
  272.9 5.1 fusion.31
  296.7 20.9 %attend_back.1 = (bf16[512,512]{1,0:T(8,128)(2,1)S(1)}, bf16[512,512]{1,0:T(8,128)(2,1)S(1)}, bf16[512,2560]{1,0:T(8,128)(2,1)}, bf16[512,256]{1,0:T(8,128)(2,1)S(1)}) custom-call(bf16[512,1024]{1,0:T(8,128)(2,1)S(1)} %get-tuple-element.218.refs_0_.middle_ref, bf16[2560,1024]{1,0:T(8,128)(2,1)} %output_weight.1, ...), custom_call_target="tpu_custom_call" | custom-call | flops 4026531840 | tf_op jit(solution)/shard_map/attend_back/pallas_call | solution.py:529
  329.0 8.1 %collective-permute-done.15 = bf16[512,1024]{1,0:T(8,128)(2,1)} collective-permute-done((bf16[512,1024]{1,0:T(8,128)(2,1)}, bf16[512,1024]{1,0:T(8,128)(2,1)}, u32[]{:S(2)}, u32[]{:S(2)}) %collective-permute-start.15) | collective-permute-done | bytes 1048608 | tf_op jit(solution)/shard_map/ppermute | solution.py:602
  346.6 13.0 %collective-permute-done.26 = bf16[8,80,1024]{2,1,0:T(8,128)(2,1)S(1)} collective-permute-done((bf16[8,80,1024]{2,1,0:T(8,128)(2,1)S(1)}, bf16[8,80,1024]{2,1,0:T(8,128)(2,1)S(1)}, u32[]{:S(2)}, u32[]{:S(2)}) %collective-permute-start.26) | collective-permute-done | bytes 1310752 | tf_op jit(solution)/shard_map/ppermute | solution.py:652
  369.1 5.1 add_add_fusion
  374.2 11.2 %collective-permute-done.27 = bf16[4,80,1024]{2,1,0:T(8,128)(2,1)S(1)} collective-permute-done((bf16[4,80,1024]{2,1,0:T(8,128)(2,1)}, bf16[4,80,1024]{2,1,0:T(8,128)(2,1)S(1)}, u32[]{:S(2)}, u32[]{:S(2)}) %collective-permute-start.27) | collective-permute-done | bytes 655392 | tf_op jit(solution)/shard_map/ppermute | solution.py:652
  393.3 5.4 collective-permute-done.29
  411.5 6.5 %collective-permute-done.33 = bf16[1,80,1024]{2,1,0:T(8,128)(2,1)S(1)} collective-permute-done((bf16[1,80,1024]{2,1,0:T(8,128)(2,1)S(1)}, bf16[1,80,1024]{2,1,0:T(8,128)(2,1)S(1)}, u32[]{:S(2)}, u32[]{:S(2)}) %collective-permute-start.33) | collective-permute-done | bytes 163872 | tf_op jit(solution)/shard_map/ppermute | solution.py:652
  420.4 8.6 %collective-permute-done.36 = f32[3,1024]{1,0:T(4,128)S(1)} collective-permute-done((f32[3,1024]{1,0:T(4,128)S(1)}, f32[3,1024]{1,0:T(4,128)S(1)}, u32[]{:S(2)}, u32[]{:S(2)}) %collective-permute-start.36) | collective-permute-done | bytes 12320 | tf_op jit(solution)/shard_map/ppermute | solution.py:849
  437.7 7.3 %collective-permute-done.50 = bf16[1,32,2560]{2,1,0:T(8,128)(2,1)S(1)} collective-permute-done((bf16[1,32,2560]{2,1,0:T(8,128)(2,1)S(1)}, bf16[1,32,2560]{2,1,0:T(8,128)(2,1)S(1)}, u32[]{:S(2)}, u32[]{:S(2)}) %collective-permute-start.50) | collective-permute-done | bytes 163872 | tf_op jit(solution)/shard_map/ppermute | solution.py:652
  448.0 7.3 %collective-permute-done.51 = bf16[1,32,2560]{2,1,0:T(8,128)(2,1)S(1)} collective-permute-done((bf16[1,32,2560]{2,1,0:T(8,128)(2,1)S(1)}, bf16[1,32,2560]{2,1,0:T(8,128)(2,1)S(1)}, u32[]{:S(2)}, u32[]{:S(2)}) %collective-permute-start.51) | collective-permute-done | bytes 163872 | tf_op jit(solution)/shard_map/ppermute | solution.py:652
  459.3 7.5 %collective-permute-done.52 = bf16[2,32,2560]{2,1,0:T(8,128)(2,1)S(1)} collective-permute-done((bf16[2,32,2560]{2,1,0:T(8,128)(2,1)S(1)}, bf16[2,32,2560]{2,1,0:T(8,128)(2,1)S(1)}, u32[]{:S(2)}, u32[]{:S(2)}) %collective-permute-start.52) | collective-permute-done | bytes 327712 | tf_op jit(solution)/shard_map/ppermute | solution.py:652
  468.6 12.3 %collective-permute-done.53 = bf16[4,32,2560]{2,1,0:T(8,128)(2,1)S(1)} collective-permute-done((bf16[4,32,2560]{2,1,0:T(8,128)(2,1)S(1)}, bf16[4,32,2560]{2,1,0:T(8,128)(2,1)S(1)}, u32[]{:S(2)}, u32[]{:S(2)}) %collective-permute-start.53) | collective-permute-done | bytes 655392 | tf_op jit(solution)/shard_map/ppermute | solution.py:652
  483.7 6.3 %collective-permute-done.43 = bf16[2,32,1408]{2,1,0:T(8,128)(2,1)S(1)} collective-permute-done((bf16[2,32,1408]{2,1,0:T(8,128)(2,1)S(1)}, bf16[2,32,1408]{2,1,0:T(8,128)(2,1)S(1)}, u32[]{:S(2)}, u32[]{:S(2)}) %collective-permute-start.43) | collective-permute-done | bytes 180256 | tf_op jit(solution)/shard_map/ppermute | solution.py:652
  495.8 5.6 collective-permute-done.44
  503.8 5.6 %assemble.4 = f32[32,80,1024]{2,1,0:T(8,128)} custom-call(s32[10]{0:T(128)S(1)} %stack.231.order_ref, bf16[8,80,1024]{2,1,0:T(8,128)(2,1)S(1)} %constant_dynamic-update-slice_fusion.2.refs_0_, bf16[8,80,1024]{2,1,0:T(8,128)(2,1)S(1)} %collective-permute-done.56.refs_1_, bf16[8,80,1024]{2,1,0:T(8,128)(2,1)S(1)} %collective-permute-done.57.refs_2_, ...), custom_call_target="tpu_custom_call" | custom-call | bytes 5242880 | tf_op jit(solution)/shard_map/assemble/pallas_call | solution.py:764
  512.0 16.8 %collective-permute-done.37 = f32[3,1024]{1,0:T(4,128)S(1)} collective-permute-done((f32[3,1024]{1,0:T(4,128)S(1)}, f32[3,1024]{1,0:T(4,128)S(1)}, u32[]{:S(2)}, u32[]{:S(2)}) %collective-permute-start.37) | collective-permute-done | bytes 12320 | tf_op jit(solution)/shard_map/ppermute | solution.py:849
  537.3 7.2 %assemble.3 = (f32[32,32,512]{2,1,0:T(8,128)}, f32[32,32,512]{2,1,0:T(8,128)}, f32[32,32,20]{2,1,0:T(8,128)S(1)}, f32[32,32,20]{2,1,0:T(8,128)S(1)}, f32[32,32,96]{2,1,0:T(8,128)S(1)}) custom-call(s32[10]{0:T(128)S(1)} %stack.231.order_ref, bf16[8,32,1408]{2,1,0:T(8,128)(2,1)S(1)} %pad_maximum_fusion.1.refs_0_, ...), custom_call_target="tpu_custom_call" | custom-call | bytes 2883584 | tf_op jit(solution)/shard_map/assemble/pallas_call | solution.py:764
  552.7 8.3 %assemble.5 = f32[32,32,2560]{2,1,0:T(8,128)} custom-call(s32[10]{0:T(128)S(1)} %stack.231.order_ref, bf16[8,32,2560]{2,1,0:T(8,128)(2,1)S(1)} %constant_dynamic-update-slice_fusion.refs_0_, bf16[8,32,2560]{2,1,0:T(8,128)(2,1)S(1)} %collective-permute-done.54.refs_1_, bf16[8,32,2560]{2,1,0:T(8,128)(2,1)} %collective-permute-done.59.refs_2_, ...), custom_call_target="tpu_custom_call" | custom-call | bytes 5242880 | tf_op jit(solution)/shard_map/assemble/pallas_call | solution.py:764
  (311 shorter events, 162.6 us)
Async XLA Ops:
  3.6 39.8 %collective-permute-start = (bf16[3,1024,256]{2,1,0:T(8,128)(2,1)}, bf16[3,1024,256]{2,1,0:T(8,128)(2,1)}, u32[]{:S(2)}, u32[]{:S(2)}) collective-permute-start(bf16[3,1024,256]{2,1,0:T(8,128)(2,1)} %pad_maximum_fusion.refs_4_), channel_id=1, source_target_pairs={{0,2},{1,3},{2,4},{3,5},{4,6},{5,7},{6,0},{7,1},{8,10},{9,11},{10,... | collective-permute-start | bytes 4718600 | tf_op jit(solution)/shard_map/ppermute | solution.py:595
  8.5 29.6 %collective-permute-start.1 = (bf16[512,1152]{1,0:T(8,128)(2,1)}, bf16[512,1152]{1,0:T(8,128)(2,1)}, u32[]{:S(2)}, u32[]{:S(2)}) collective-permute-start(bf16[512,1152]{1,0:T(8,128)(2,1)} %fusion.13.refs_1_), channel_id=1, source_target_pairs={{0,1},{1,0},{2,3},{3,2},{4,5},{5,4},{6,7},{7,6},{8,9},{9,8},{10,11... | collective-permute-start | bytes 3538952 | tf_op jit(solution)/shard_map/ppermute | solution.py:602
  10.0 28.1 %collective-permute-start.2 = (bf16[512,1152]{1,0:T(8,128)(2,1)}, bf16[512,1152]{1,0:T(8,128)(2,1)}, u32[]{:S(2)}, u32[]{:S(2)}) collective-permute-start(bf16[512,1152]{1,0:T(8,128)(2,1)} %fusion.13.refs_1_), channel_id=1, source_target_pairs={{0,16},{8,24},{16,0},{24,8},{1,17},{9,25},{17,1},{25,9},{2,18},{10... | collective-permute-start | bytes 3538952 | tf_op jit(solution)/shard_map/ppermute | solution.py:605
  11.5 36.9 %collective-permute-start.3 = (bf16[3,1024,256]{2,1,0:T(8,128)(2,1)}, bf16[3,1024,256]{2,1,0:T(8,128)(2,1)}, u32[]{:S(2)}, u32[]{:S(2)}) collective-permute-start(bf16[3,1024,256]{2,1,0:T(8,128)(2,1)} %pad_maximum_fusion.refs_4_), channel_id=1, source_target_pairs={{0,8},{8,0},{16,24},{24,16},{1,9},{9,1},{17,25},{25,17},{2,10},{10... | collective-permute-start | bytes 4718600 | tf_op jit(solution)/shard_map/ppermute | solution.py:591
  43.4 48.7 %collective-permute-start.7 = (bf16[3,1024,256]{2,1,0:T(8,128)(2,1)}, bf16[3,1024,256]{2,1,0:T(8,128)(2,1)}, u32[]{:S(2)}, u32[]{:S(2)}) collective-permute-start(bf16[3,1024,256]{2,1,0:T(8,128)(2,1)} %collective-permute-done.refs_6_), channel_id=1, source_target_pairs={{0,2},{1,3},{2,4},{3,5},{4,6},{5,7},{6,0},{7,1},{8,10},{9,11},{10,... | collective-permute-start | bytes 4718600 | tf_op jit(solution)/shard_map/ppermute | solution.py:595
  43.6 25.7 %collective-permute-start.5 = (bf16[512,1024]{1,0:T(8,128)(2,1)S(1)}, bf16[512,1024]{1,0:T(8,128)(2,1)}, u32[]{:S(2)}, u32[]{:S(2)}) collective-permute-start(bf16[512,1024]{1,0:T(8,128)(2,1)S(1)} %multiply_convert_fusion.refs_0_), channel_id=1, source_target_pairs={{0,1},{1,0},{2,3},{3,2},{4,5},{5,4},{6,7},{7,6},{8,9},{9,8},{10,11... | collective-permute-start | bytes 3145736 | tf_op jit(solution)/shard_map/ppermute | solution.py:602
  45.2 25.4 %collective-permute-start.6 = (bf16[512,1024]{1,0:T(8,128)(2,1)S(1)}, bf16[512,1024]{1,0:T(8,128)(2,1)}, u32[]{:S(2)}, u32[]{:S(2)}) collective-permute-start(bf16[512,1024]{1,0:T(8,128)(2,1)S(1)} %multiply_convert_fusion.refs_0_), channel_id=1, source_target_pairs={{0,16},{8,24},{16,0},{24,8},{1,17},{9,25},{17,1},{25,9},{2,18},{10... | collective-permute-start | bytes 3145736 | tf_op jit(solution)/shard_map/ppermute | solution.py:605
  92.1 25.6 %collective-permute-start.8 = (bf16[3,1024,256]{2,1,0:T(8,128)(2,1)}, bf16[3,1024,256]{2,1,0:T(8,128)(2,1)S(1)}, u32[]{:S(2)}, u32[]{:S(2)}) collective-permute-start(bf16[3,1024,256]{2,1,0:T(8,128)(2,1)} %collective-permute-done.7.refs_4_), channel_id=1, source_target_pairs={{0,8},{8,0},{16,24},{24,16},{1,9},{9,1},{17,25},{25,17},{2,10},{10... | collective-permute-start | bytes 4718600 | tf_op jit(solution)/shard_map/ppermute | solution.py:591
  92.2 52.0 %collective-permute-start.12 = (bf16[512,1152]{1,0:T(8,128)(2,1)}, bf16[512,1152]{1,0:T(8,128)(2,1)S(1)}, u32[]{:S(2)}, u32[]{:S(2)}) collective-permute-start(bf16[512,1152]{1,0:T(8,128)(2,1)} %fusion.13.refs_1_), channel_id=1, source_target_pairs={{0,17},{1,16},{2,19},{3,18},{4,21},{5,20},{6,23},{7,22},{8,25},{9,... | collective-permute-start | bytes 3538952 | tf_op jit(solution)/shard_map/ppermute | solution.py:611
  93.7 50.4 %collective-permute-start.11 = (bf16[512,1024]{1,0:T(8,128)(2,1)S(1)}, bf16[512,1024]{1,0:T(8,128)(2,1)S(1)}, u32[]{:S(2)}, u32[]{:S(2)}) collective-permute-start(bf16[512,1024]{1,0:T(8,128)(2,1)S(1)} %copy-done.28), channel_id=1, source_target_pairs={{0,17},{1,16},{2,19},{3,18},{4,21},{5,20},{6,23},{7,22},{8,25},{9,... | collective-permute-start | bytes 3145736 | tf_op jit(solution)/shard_map/ppermute | solution.py:611
  95.2 70.9 %collective-permute-start.9 = (bf16[3,1024,256]{2,1,0:T(8,128)(2,1)}, bf16[3,1024,256]{2,1,0:T(8,128)(2,1)}, u32[]{:S(2)}, u32[]{:S(2)}) collective-permute-start(bf16[3,1024,256]{2,1,0:T(8,128)(2,1)} %collective-permute-done.7.refs_4_), channel_id=1, source_target_pairs={{0,2},{1,3},{2,4},{3,5},{4,6},{5,7},{6,0},{7,1},{8,10},{9,11},{10,... | collective-permute-start | bytes 4718600 | tf_op jit(solution)/shard_map/ppermute | solution.py:595
  166.0 29.0 %collective-permute-start.13 = (bf16[6,1024,256]{2,1,0:T(8,128)(2,1)}, bf16[6,1024,256]{2,1,0:T(8,128)(2,1)}, u32[]{:S(2)}, u32[]{:S(2)}) collective-permute-start(bf16[6,1024,256]{2,1,0:T(8,128)(2,1)} %get-tuple-element.185), channel_id=1, source_target_pairs={{0,8},{8,0},{16,24},{24,16},{1,9},{9,1},{17,25},{25,17},{2,10},{10... | collective-permute-start | bytes 9437192 | tf_op jit(solution)/shard_map/ppermute | solution.py:591
  196.8 49.3 %collective-permute-start.14 = (bf16[3,1024,256]{2,1,0:T(8,128)(2,1)S(1)}, bf16[3,1024,256]{2,1,0:T(8,128)(2,1)S(1)}, u32[]{:S(2)}, u32[]{:S(2)}) collective-permute-start(bf16[3,1024,256]{2,1,0:T(8,128)(2,1)S(1)} %add_convert_fusion.2), channel_id=1, source_target_pairs={{0,2},{1,3},{2,4},{3,5},{4,6},{5,7},{6,0},{7,1},{8,10},{9,11},{10,... | collective-permute-start | bytes 4718600 | tf_op jit(solution)/shard_map/ppermute | solution.py:595
  198.2 70.1 %collective-permute-start.22 = (bf16[512,1024]{1,0:T(8,128)(2,1)}, bf16[512,1024]{1,0:T(8,128)(2,1)S(1)}, u32[]{:S(2)}, u32[]{:S(2)}) collective-permute-start(bf16[512,1024]{1,0:T(8,128)(2,1)} %get-tuple-element.213), channel_id=1, source_target_pairs={{0,17},{1,16},{2,19},{3,18},{4,21},{5,20},{6,23},{7,22},{8,25},{9,... | collective-permute-start | bytes 3145736 | tf_op jit(solution)/shard_map/ppermute | solution.py:611
  243.9 25.0 %collective-permute-start.21 = (bf16[512,1024]{1,0:T(8,128)(2,1)}, bf16[512,1024]{1,0:T(8,128)(2,1)}, u32[]{:S(2)}, u32[]{:S(2)}) collective-permute-start(bf16[512,1024]{1,0:T(8,128)(2,1)} %get-tuple-element.212), channel_id=1, source_target_pairs={{0,16},{8,24},{16,0},{24,8},{1,17},{9,25},{17,1},{25,9},{2,18},{10... | collective-permute-start | bytes 3145736 | tf_op jit(solution)/shard_map/ppermute | solution.py:605
  244.5 24.7 %collective-permute-start.20 = (bf16[512,1024]{1,0:T(8,128)(2,1)}, bf16[512,1024]{1,0:T(8,128)(2,1)}, u32[]{:S(2)}, u32[]{:S(2)}) collective-permute-start(bf16[512,1024]{1,0:T(8,128)(2,1)} %get-tuple-element.211), channel_id=1, source_target_pairs={{0,1},{1,0},{2,3},{3,2},{4,5},{5,4},{6,7},{7,6},{8,9},{9,8},{10,11... | collective-permute-start | bytes 3145736 | tf_op jit(solution)/shard_map/ppermute | solution.py:602
  283.1 34.6 %collective-permute-start.23 = (bf16[16,80,1024]{2,1,0:T(8,128)(2,1)}, bf16[16,80,1024]{2,1,0:T(8,128)(2,1)}, u32[]{:S(2)}, u32[]{:S(2)}) collective-permute-start(bf16[16,80,1024]{2,1,0:T(8,128)(2,1)} %get-tuple-element.217), channel_id=1, source_target_pairs={{0,8},{8,0},{16,24},{24,16},{1,9},{9,1},{17,25},{25,17},{2,10},{10... | collective-permute-start | bytes 7864328 | tf_op jit(solution)/shard_map/ppermute | solution.py:591
  287.2 38.1 %collective-permute-start.19 = (bf16[3,1024,256]{2,1,0:T(8,128)(2,1)}, bf16[3,1024,256]{2,1,0:T(8,128)(2,1)}, u32[]{:S(2)}, u32[]{:S(2)}) collective-permute-start(bf16[3,1024,256]{2,1,0:T(8,128)(2,1)} %add_convert_fusion.1), channel_id=1, source_target_pairs={{0,2},{1,3},{2,4},{3,5},{4,6},{5,7},{6,0},{7,1},{8,10},{9,11},{10,... | collective-permute-start | bytes 4718600 | tf_op jit(solution)/shard_map/ppermute | solution.py:595
  288.9 40.1 %collective-permute-start.17 = (bf16[512,1024]{1,0:T(8,128)(2,1)}, bf16[512,1024]{1,0:T(8,128)(2,1)S(1)}, u32[]{:S(2)}, u32[]{:S(2)}) collective-permute-start(bf16[512,1024]{1,0:T(8,128)(2,1)} %get-tuple-element.206), channel_id=1, source_target_pairs={{0,17},{1,16},{2,19},{3,18},{4,21},{5,20},{6,23},{7,22},{8,25},{9,... | collective-permute-start | bytes 3145736 | tf_op jit(solution)/shard_map/ppermute | solution.py:611
  291.4 45.7 %collective-permute-start.15 = (bf16[512,1024]{1,0:T(8,128)(2,1)}, bf16[512,1024]{1,0:T(8,128)(2,1)}, u32[]{:S(2)}, u32[]{:S(2)}) collective-permute-start(bf16[512,1024]{1,0:T(8,128)(2,1)} %get-tuple-element.202), channel_id=1, source_target_pairs={{0,1},{1,0},{2,3},{3,2},{4,5},{5,4},{6,7},{7,6},{8,9},{9,8},{10,11... | collective-permute-start | bytes 3145736 | tf_op jit(solution)/shard_map/ppermute | solution.py:602
  291.9 45.2 %collective-permute-start.16 = (bf16[512,1024]{1,0:T(8,128)(2,1)}, bf16[512,1024]{1,0:T(8,128)(2,1)}, u32[]{:S(2)}, u32[]{:S(2)}) collective-permute-start(bf16[512,1024]{1,0:T(8,128)(2,1)} %get-tuple-element.205), channel_id=1, source_target_pairs={{0,16},{8,24},{16,0},{24,8},{1,17},{9,25},{17,1},{25,9},{2,18},{10... | collective-permute-start | bytes 3145736 | tf_op jit(solution)/shard_map/ppermute | solution.py:605
  362.8 24.8 %collective-permute-start.25 = (bf16[8,32,2560]{2,1,0:T(8,128)(2,1)}, bf16[8,32,2560]{2,1,0:T(8,128)(2,1)S(1)}, u32[]{:S(2)}, u32[]{:S(2)}) collective-permute-start(bf16[8,32,2560]{2,1,0:T(8,128)(2,1)} %get-tuple-element.236), channel_id=1, source_target_pairs={{0,16},{1,17},{2,18},{3,19},{4,20},{5,21},{6,22},{7,23},{8,9},{9,8... | collective-permute-start | bytes 3932168 | tf_op jit(solution)/shard_map/ppermute | solution.py:652
  436.2 21.5 %collective-permute-start.55 = (bf16[4,80,1024]{2,1,0:T(8,128)(2,1)S(1)}, bf16[4,80,1024]{2,1,0:T(8,128)(2,1)S(1)}, u32[]{:S(2)}, u32[]{:S(2)}) collective-permute-start(bf16[4,80,1024]{2,1,0:T(8,128)(2,1)S(1)} %pad_maximum_fusion.2), channel_id=1, source_target_pairs={{0,1},{1,0},{2,3},{3,2},{4,5},{5,4},{6,7},{7,6},{8,24},{9,25},{10,... | collective-permute-start | bytes 1966088 | tf_op jit(solution)/shard_map/ppermute | solution.py:652
  457.8 24.7 %collective-permute-start.56 = (bf16[8,80,1024]{2,1,0:T(8,128)(2,1)S(1)}, bf16[8,80,1024]{2,1,0:T(8,128)(2,1)S(1)}, u32[]{:S(2)}, u32[]{:S(2)}) collective-permute-start(bf16[8,80,1024]{2,1,0:T(8,128)(2,1)S(1)} %constant_dynamic-update-slice_fusion.2.refs_0_), channel_id=1, source_target_pairs={{0,16},{1,17},{2,18},{3,19},{4,20},{5,21},{6,22},{7,23},{8,9},{9,8... | collective-permute-start | bytes 3932168 | tf_op jit(solution)/shard_map/ppermute | solution.py:652
  468.5 34.2 %collective-permute-start.57 = (bf16[8,80,1024]{2,1,0:T(8,128)(2,1)S(1)}, bf16[8,80,1024]{2,1,0:T(8,128)(2,1)S(1)}, u32[]{:S(2)}, u32[]{:S(2)}) collective-permute-start(bf16[8,80,1024]{2,1,0:T(8,128)(2,1)S(1)} %constant_dynamic-update-slice_fusion.2.refs_0_), channel_id=1, source_target_pairs={{0,8},{8,0},{16,24},{24,16},{1,9},{9,1},{17,25},{25,17},{2,10},{10... | collective-permute-start | bytes 3932168 | tf_op jit(solution)/shard_map/ppermute | solution.py:591
  480.9 28.5 %collective-permute-start.54 = (bf16[8,32,2560]{2,1,0:T(8,128)(2,1)S(1)}, bf16[8,32,2560]{2,1,0:T(8,128)(2,1)S(1)}, u32[]{:S(2)}, u32[]{:S(2)}) collective-permute-start(bf16[8,32,2560]{2,1,0:T(8,128)(2,1)S(1)} %constant_dynamic-update-slice_fusion.refs_0_), channel_id=1, source_target_pairs={{0,16},{1,17},{2,18},{3,19},{4,20},{5,21},{6,22},{7,23},{8,9},{9,8... | collective-permute-start | bytes 3932168 | tf_op jit(solution)/shard_map/ppermute | solution.py:652
  482.5 21.3 %collective-permute-start.58 = (bf16[8,80,1024]{2,1,0:T(8,128)(2,1)S(1)}, bf16[8,80,1024]{2,1,0:T(8,128)(2,1)S(1)}, u32[]{:S(2)}, u32[]{:S(2)}) collective-permute-start(bf16[8,80,1024]{2,1,0:T(8,128)(2,1)S(1)} %collective-permute-done.56.refs_1_), channel_id=1, source_target_pairs={{0,8},{8,0},{16,24},{24,16},{1,9},{9,1},{17,25},{25,17},{2,10},{10... | collective-permute-start | bytes 3932168 | tf_op jit(solution)/shard_map/ppermute | solution.py:591
  490.8 39.6 %collective-permute-start.61 = (bf16[3,1024,256]{2,1,0:T(8,128)(2,1)S(1)}, bf16[3,1024,256]{2,1,0:T(8,128)(2,1)S(1)}, u32[]{:S(2)}, u32[]{:S(2)}) collective-permute-start(bf16[3,1024,256]{2,1,0:T(8,128)(2,1)S(1)} %copy-done.35), channel_id=1, source_target_pairs={{0,2},{1,3},{2,4},{3,5},{4,6},{5,7},{6,0},{7,1},{8,10},{9,11},{10,... | collective-permute-start | bytes 4718600 | tf_op jit(solution)/shard_map/ppermute | solution.py:595
  501.4 27.3 %collective-permute-start.37 = (f32[3,1024]{1,0:T(4,128)S(1)}, f32[3,1024]{1,0:T(4,128)S(1)}, u32[]{:S(2)}, u32[]{:S(2)}) collective-permute-start(f32[3,1024]{1,0:T(4,128)S(1)} %add.546), channel_id=1, source_target_pairs={{0,4},{1,5},{2,6},{3,7},{4,0},{5,1},{6,2},{7,3},{8,12},{9,13},{10,... | collective-permute-start | bytes 36872 | tf_op jit(solution)/shard_map/ppermute | solution.py:849
  502.7 27.2 %collective-permute-start.45 = (bf16[8,32,1408]{2,1,0:T(8,128)(2,1)S(1)}, bf16[8,32,1408]{2,1,0:T(8,128)(2,1)}, u32[]{:S(2)}, u32[]{:S(2)}) collective-permute-start(bf16[8,32,1408]{2,1,0:T(8,128)(2,1)S(1)} %pad_maximum_fusion.1.refs_0_), channel_id=1, source_target_pairs={{0,16},{1,17},{2,18},{3,19},{4,20},{5,21},{6,22},{7,23},{8,9},{9,8... | collective-permute-start | bytes 2162696 | tf_op jit(solution)/shard_map/ppermute | solution.py:652
  509.5 43.2 %collective-permute-start.59 = (bf16[8,32,2560]{2,1,0:T(8,128)(2,1)S(1)}, bf16[8,32,2560]{2,1,0:T(8,128)(2,1)}, u32[]{:S(2)}, u32[]{:S(2)}) collective-permute-start(bf16[8,32,2560]{2,1,0:T(8,128)(2,1)S(1)} %constant_dynamic-update-slice_fusion.refs_0_), channel_id=1, source_target_pairs={{0,8},{8,0},{16,24},{24,16},{1,9},{9,1},{17,25},{25,17},{2,10},{10... | collective-permute-start | bytes 3932168 | tf_op jit(solution)/shard_map/ppermute | solution.py:591
  509.5 43.2 %collective-permute-start.60 = (bf16[8,32,2560]{2,1,0:T(8,128)(2,1)S(1)}, bf16[8,32,2560]{2,1,0:T(8,128)(2,1)}, u32[]{:S(2)}, u32[]{:S(2)}) collective-permute-start(bf16[8,32,2560]{2,1,0:T(8,128)(2,1)S(1)} %collective-permute-done.54.refs_1_), channel_id=1, source_target_pairs={{0,8},{8,0},{16,24},{24,16},{1,9},{9,1},{17,25},{25,17},{2,10},{10... | collective-permute-start | bytes 3932168 | tf_op jit(solution)/shard_map/ppermute | solution.py:591
  (89 other events, 932.1 us)

commit v4 on v3

--- a/solution.py
+++ b/solution.py
@@ -730,17 +730,30 @@
     )(order, *operands)
 
 
+def lanes_of(width):
+    return width + -width % 128
+
+
 def assemble_kernel(count, cuts, order_ref, *refs):
-    pieces, outs = refs[:4], refs[4:]
+    pieces, outs, buffers = refs[:4], refs[4 : 4 + len(cuts)], refs[4 + len(cuts) :]
     step = pl.program_id(0)
     for index, piece in enumerate(pieces):
 
         @pl.when(step // 2 == index)
         def _():
             low = order_ref[8 + index // 2]
+            rows = piece.shape[1]
             for r in range(count):
-                for out, (start, width) in zip(outs, cuts):
-                    out[lax.bitwise_xor(low, r)] = piece[r, :, start : start + width].astype(f32)
+                place = lax.bitwise_xor(low, r)
+                for out, buffer, (start, width) in zip(outs, buffers, cuts):
+                    if width % 128:
+                        block = piece[r, :, start : start + lanes_of(width)].astype(f32)
+                        buffer[pl.ds(pl.multiple_of(place * rows, rows), rows), :] = block
+                    else:
+                        out[place] = piece[r, :, start : start + width].astype(f32)
+            for out, buffer, (_, width) in zip(outs, buffers, cuts):
+                if width % 128:
+                    out[...] = buffer[...].T[:width]
 
 
 def assemble(cube, pieces, cuts):
@@ -768,16 +781,28 @@
             grid=(8,),
             in_specs=[piece(index) for index in range(4)],
             out_specs=[
-                pl.BlockSpec((count, rows, width), lambda i, o: (o[i], 0, 0))
+                pl.BlockSpec((width, count * rows), lambda i, o: (0, o[i]))
+                if width % 128
+                else pl.BlockSpec((count, rows, width), lambda i, o: (o[i], 0, 0))
+                for _, width in cuts
+            ],
+            scratch_shapes=[
+                pltpu.VMEM((count * rows, lanes_of(width)) if width % 128 else (8, 128), f32)
                 for _, width in cuts
             ],
         ),
-        out_shape=[jax.ShapeDtypeStruct((n, rows, width), f32) for _, width in cuts],
+        out_shape=[
+            jax.ShapeDtypeStruct((width, n * rows) if width % 128 else (n, rows, width), f32)
+            for _, width in cuts
+        ],
         compiler_params=pltpu.CompilerParams(vmem_limit_bytes=40 * 1024 * 1024),
         cost_estimate=small_cost(0, n * rows * columns * 2),
         name="assemble",
     )(order, *pieces)
-    return [out.reshape(n * rows, width) for out, (_, width) in zip(outs, cuts)]
+    return [
+        out.T if width % 128 else out.reshape(n * rows, width)
+        for out, (_, width) in zip(outs, cuts)
+    ]
 
 
 def add_halves(kept, got):
@@ -964,7 +989,7 @@
     phases = nh // 2
     chosen_by = [selection((2 * p, 2 * p + 1)) for p in range(phases)]
     held = None
-    sent_back, later = {}, []
+    sent_back, outputs_back, later = {}, [], []
     for phase in range(phases):
         last = phase == phases - 1
         if phase == 0:
@@ -982,8 +1007,12 @@
                 for s, value in zip(near, values[3:]):
                     xs[s] = value
                 for s in far:
+                    ums[s] = moves.over_plane(far_um, s)
+            if phase == 0 and turn == 1:
+                grads[0], far_x, *values = tie(grads[0], far_x, *[ums[s] for s in far])
+                for s, value in zip(far, values):
+                    ums[s] = value
                     xs[s] = moves.over_plane(far_x, s)
-                    ums[s] = moves.over_plane(far_um, s)
             if phase == 0 and turn == 1 and nh > 2:
                 grads[0], weights[2] = tie(grads[0], weights[2])
                 for s in range(3, nh):
@@ -1001,7 +1030,8 @@
                 if later:
                     grads[0], *late = tie(grads[0], *[sums[s][0] for s in later])
                     for s, value in zip(later, late):
-                        sent_back[s].append(moves.over_plane(value, s, back=True))
+                        if s in far:
+                            outputs_back.append(moves.over_plane(value, s, back=True))
                 later = [s for s in offsets if s != home]
                 for s in later:
                     sent_back[s] = [moves.over_plane(sums[s][1], s, back=True)]
@@ -1011,6 +1041,8 @@
             preferred_element_type=f32,
         )
         mine, got = grads[0], moves.over_core(grads[1])
+        if last and phase > 0:
+            continue
         for k in range(2):
             s = 2 * phase + k
             parts = [grad[k * local : (k + 1) * local] for grad in (mine, got)]
@@ -1032,6 +1064,10 @@
     cube = Cube(moves)
     out_sum = Sum(cube, grad_blocks(cube, spread_low, [middle_low]), [(0, D)])
     middle_sent = out_sum.tied(middle_low)
+    if phases > 1:
+        got, middle_sent = tie(got, middle_sent)
+        passed = moves.over_hi(add_low(mine[:local], got[:local], held))
+        held = add_low(mine[local:], got[local:], passed)
     out_sum.step()
     query_delta, key_delta, values_delta, select_delta = attend_back(
         middle_sent,
@@ -1045,13 +1081,14 @@
         head_chosen,
         segments,
     )
+    out_sum.step()
+    held, *outputs_back, values_delta = tie(held, *outputs_back, values_delta)
     values_delta = out_sum.tied(values_delta)
-    held, values_delta = tie(held, values_delta)
-    *outputs_back, values_delta = tie(*[sent_back[s][1] for s in moves.plane[1:]], values_delta)
     out_sum.step()
     value_sum = Sum(cube, grad_blocks(cube, normed_low, [values_delta]), [(0, H * NE * DH)])
     value_sum.step()
     query_delta = value_sum.tied(query_delta)
+    query_delta = out_sum.tied(query_delta)
     cuts = [(0, H * DH), (H * DH, H * DH)]
     start = 2 * H * DH
     cuts += [(start, H * NE), (start + narrow, H * NE), (start + 2 * narrow, experts)]
@@ -1075,25 +1112,30 @@
     grad_attention = jnp.sum(normed_delta * inputs * att_rms, axis=0)
     small = jnp.stack([grad_attention, grad_mixture, jnp.pad(local_counts, (0, D - experts))])
     for axis, span in small_steps(moves):
-        small = out_sum.tied(small)
+        small = rest_sum.tied(out_sum.tied(small))
         small = sum_step(moves, small, axis, span)
         for each in (out_sum, rest_sum, value_sum):
             if each.done < each.steps:
                 each.step()
-    while value_sum.done < 2 * cube.bits - 2:
+    small = out_sum.tied(small)
+    while rest_sum.done < 2 * cube.bits - 1:
         for each in (out_sum, rest_sum, value_sum):
             if each.done < each.steps:
                 each.step()
-    last_held = moves.over_hi(value_sum.tied(held))
+    last_held = moves.over_hi(rest_sum.tied(held))
     while value_sum.done < value_sum.steps - 1:
         for each in (out_sum, rest_sum, value_sum):
             if each.done < each.steps:
                 each.step()
     out_sum.out[0] = value_sum.tied(out_sum.out[0])
+    for s in near:
+        outputs_back.append(moves.over_plane(value_sum.tied(sums[s][0]), s, back=True))
+    last_held = value_sum.tied(last_held)
     for each in (out_sum, rest_sum, value_sum):
         each.run(each.steps - each.done)
     (grad_output,) = out_sum.out
     (grad_value,) = value_sum.out
+    *outputs_back, grad_value = tie(*outputs_back, grad_value)
     grad_query, grad_key, grad_vselect, grad_oselect, grad_router = rest_sum.out
     input_delta = middle_delta + norm_back(inputs, att_rms, attention_gain, normed_delta)
     output_rows = middle_rows + sums[home][0].astype(f32)

time: 568 us -> 502 us (0.88)
  waiting for transfers between devices: 176 us -> 124 us
  local copies, waits for them, and re-layouts: 26.2 us -> 18.7 us
    ppermute x5, waiting for transfers between devices: 31 us -> 5.92 us  [sum_step(): lax.ppermute(value, axis, [(i, i ^ span) for i in range(size)])]
    ppermute x4, waiting for transfers between devices: 26.4 us -> 7.89 us  [over_plane(): return lax.ppermute(value, ('dp', 'expert'), pairs)]
    ppermute x24, waiting for transfers between devices: 91.4 us -> 78.6 us  [exchange(): return lax.ppermute(value, ('dp', 'expert'), pairs)]
    unnamed x128 -> x118, local copies, waits for them, and re-layouts: 21.4 us -> 13.9 us
    ppermute x4, waiting for transfers between devices: 9.33 us -> 3.07 us  [over_plane(): return lax.ppermute(value, 'expert', [(i, i ^ b) for i in range(self.ex)])]
  transfers between devices with their start and end apart: 62 -> 62, of which waited for: 28 -> 36; matrix products, arithmetic and copies ran while one was open for 12% -> 11% of each run, Pallas kernels for 40% -> 47%
where the time goes in v4:
time: 502 us; the launch traced here: 495 us
  Pallas kernels  239 us (48%)
  waiting for transfers between devices  124 us (25%)
  starting transfers between devices  56.9 us (11%)
  other arithmetic  39.9 us (8%)
  local copies, waits for them, and re-layouts  18.7 us (4%)
  matrix products  13.4 us (3%)
    pallas_call x8, Pallas kernels, run_experts(): pl.pallas_call(functools.partial(experts_kernel, blocks, pairs, previous...  173 us
    ppermute x24, waiting for transfers between devices, exchange(): return lax.ppermute(value, ('dp', 'expert'), pairs)  78.6 us
    ppermute x24, starting transfers between devices, exchange(): return lax.ppermute(value, ('dp', 'expert'), pairs)  28.3 us
    pallas_call x1, Pallas kernels, attend_back(): pl.pallas_call(attend_back_kernel, grid=(H,), in_specs=[whole, pl.BlockSp...  20.9 us
    pallas_call x3, Pallas kernels, assemble(): pl.pallas_call(functools.partial(assemble_kernel, count, cuts), grid_spec...  19 us
    convert_element_type x18, other arithmetic, add_low(): return total.astype(bf16)  16.5 us
    ppermute x6, waiting for transfers between devices, over_hi(): return lax.ppermute(value, 'expert', pairs)  14 us
    unnamed x118, local copies, waits for them, and re-layouts  13.9 us
  transfers between devices with their start and end apart: 62, of which 36 were waited for; matrix products, arithmetic and copies ran while one was open for 11% of the time, Pallas kernels for 47%

profile of v4, /device:TPU:0, one launch (start us, length us, event | category | flops | bytes accessed | tf_op | source)
XLA Modules:
  0.0 494.5 jit_solution(8874375538959594875)
XLA Ops:
  15.5 13.8 %attend.1 = (bf16[512,512]{1,0:T(8,128)(2,1)S(1)}, bf16[512,512]{1,0:T(8,128)(2,1)S(1)}, f32[512,2560]{1,0:T(8,128)}, bf16[512,512]{1,0:T(8,128)(2,1)S(1)}, f32[...) custom-call(bf16[512,1024]{1,0:T(8,128)(2,1)S(1)} %fusion.3.normed_ref.left_a.left_b, ...), custom_call_target="tpu_custom_call" | custom-call | flops 4294967296 | tf_op jit(solution)/shard_map/attend/pallas_call | solution.py:423
  29.4 5.7 %multiply_reduce_fusion.2 = (f32[512]{0:T(512)S(1)}, f32[512,1024]{1,0:T(8,128)S(1)}) fusion(bf16[512,2560]{1,0:T(8,128)(2,1)} %get-tuple-element.181.left_a.left_b, bf16[2560,1024]{1,0:T(8,128)(2,1)S(1)} %bitcast.94, bf16[1,512,1024]{2,1,0:T(8,128)(2,1)S(1)} %copy-done.19), kind=kOutput, calls=%fused_computation.37 | convolution fusion | flops 2686451200 | bytes 11012096 | tf_op jit(solution)/shard_map/dot_general | solution.py:933
  37.5 5.9 %collective-permute-done.refs_6_ = bf16[3,1024,256]{2,1,0:T(8,128)(2,1)} collective-permute-done((bf16[3,1024,256]{2,1,0:T(8,128)(2,1)}, bf16[3,1024,256]{2,1,0:T(8,128)(2,1)}, u32[]{:S(2)}, u32[]{:S(2)}) %collective-permute-start) | collective-permute-done | bytes 1572896 | tf_op jit(solution)/shard_map/ppermute | solution.py:595
  48.4 20.4 %experts.8 = (bf16[512,1024]{1,0:T(8,128)(2,1)}, bf16[512,1024]{1,0:T(8,128)(2,1)}, f32[6,1024,256]{2,1,0:T(8,128)}, f32[6,1024,256]{2,1,0:T(8,128)}, f32[1024,16]{1,0:T(8,128)}) custom-call(bf16[512,1024]{1,0:T(8,128)(2,1)} %copy-done.27, bf16[512,1152]{1,0:T(8,128)(2,1)} %fusion.13.refs_1_, bf16[128,16]{1,0:T(8,128)(2,1)} %get-tuple-element.441.refs_2_, ...), custom_call_target="tpu_custom_call" | custom-call | flops 4831838208 | tf_op jit(solution)/shard_map/experts/pallas_call | solution.py:296
  71.8 21.9 %experts.9 = (bf16[512,1024]{1,0:T(8,128)(2,1)}, bf16[512,1024]{1,0:T(8,128)(2,1)}, f32[6,1024,256]{2,1,0:T(8,128)}, f32[6,1024,256]{2,1,0:T(8,128)}, f32[1024,16]{1,0:T(8,128)}) custom-call(bf16[512,1024]{1,0:T(8,128)(2,1)} %collective-permute-done.5.refs_0_, bf16[512,1152]{1,0:T(8,128)(2,1)} %collective-permute-done.1.refs_1_, ...), custom_call_target="tpu_custom_call" | custom-call | flops 4831838208 | tf_op jit(solution)/shard_map/experts/pallas_call | solution.py:296
  93.7 5.0 %collective-permute-done.7.refs_1_ = bf16[512,1152]{1,0:T(8,128)(2,1)S(1)} collective-permute-done((bf16[512,1152]{1,0:T(8,128)(2,1)}, bf16[512,1152]{1,0:T(8,128)(2,1)S(1)}, u32[]{:S(2)}, u32[]{:S(2)}) %collective-permute-start.7) | collective-permute-done | bytes 1179680 | tf_op jit(solution)/shard_map/ppermute | solution.py:611
  100.5 21.9 %experts.10 = (bf16[512,1024]{1,0:T(8,128)(2,1)}, bf16[512,1024]{1,0:T(8,128)(2,1)}, f32[6,1024,256]{2,1,0:T(8,128)}, f32[6,1024,256]{2,1,0:T(8,128)}, f32[1024,16]{1,0:T(8,128)}) custom-call(bf16[512,1024]{1,0:T(8,128)(2,1)} %collective-permute-done.6.refs_0_, bf16[512,1152]{1,0:T(8,128)(2,1)} %collective-permute-done.2.refs_1_, ...), custom_call_target="tpu_custom_call" | custom-call | flops 4831838208 | tf_op jit(solution)/shard_map/experts/pallas_call | solution.py:296
  125.3 21.1 %experts.11 = (bf16[512,1024]{1,0:T(8,128)(2,1)}, bf16[512,1024]{1,0:T(8,128)(2,1)}, bf16[6,1024,256]{2,1,0:T(8,128)(2,1)}, bf16[6,1024,256]{2,1,0:T(8,128)(2,1)}, f32[1024,16]{1,0:T(8,128)}) custom-call(bf16[512,1024]{1,0:T(8,128)(2,1)} %collective-permute-done.12.refs_0_, bf16[512,1152]{1,0:T(8,128)(2,1)} %copy-done.39, ...), custom_call_target="tpu_custom_call" | custom-call | flops 4831838208 | tf_op jit(solution)/shard_map/experts/pallas_call | solution.py:296
  148.8 6.0 %collective-permute-done.11.refs_7_ = bf16[3,1024,256]{2,1,0:T(8,128)(2,1)} collective-permute-done((bf16[3,1024,256]{2,1,0:T(8,128)(2,1)}, bf16[3,1024,256]{2,1,0:T(8,128)(2,1)}, u32[]{:S(2)}, u32[]{:S(2)}) %collective-permute-start.11) | collective-permute-done | bytes 1572896 | tf_op jit(solution)/shard_map/ppermute | solution.py:591
  154.7 21.2 %experts.12 = (bf16[512,1024]{1,0:T(8,128)(2,1)}, bf16[512,1024]{1,0:T(8,128)(2,1)}, f32[6,1024,256]{2,1,0:T(8,128)}, f32[6,1024,256]{2,1,0:T(8,128)}, f32[1024,16]{1,0:T(8,128)}) custom-call(bf16[512,1024]{1,0:T(8,128)(2,1)} %collective-permute-done.12.refs_0_, bf16[512,1152]{1,0:T(8,128)(2,1)} %copy-done.39, bf16[128,16]{1,0:T(8,128)(2,1)} %get-tuple-element.439.refs_2_, ...), custom_call_target="tpu_custom_call" | custom-call | flops 4831838208 | tf_op jit(solution)/shard_map/experts/pallas_call | solution.py:296
  180.9 22.5 %experts.13 = (bf16[512,1024]{1,0:T(8,128)(2,1)}, bf16[512,1024]{1,0:T(8,128)(2,1)}, f32[6,1024,256]{2,1,0:T(8,128)}, f32[6,1024,256]{2,1,0:T(8,128)}, f32[1024,16]{1,0:T(8,128)}) custom-call(bf16[512,1024]{1,0:T(8,128)(2,1)} %collective-permute-done.5.refs_0_, bf16[512,1152]{1,0:T(8,128)(2,1)} %collective-permute-done.1.refs_1_, ...), custom_call_target="tpu_custom_call" | custom-call | flops 4831838208 | tf_op jit(solution)/shard_map/experts/pallas_call | solution.py:296
  203.4 22.5 %experts.14 = (bf16[512,1024]{1,0:T(8,128)(2,1)}, bf16[512,1024]{1,0:T(8,128)(2,1)}, f32[6,1024,256]{2,1,0:T(8,128)}, f32[6,1024,256]{2,1,0:T(8,128)}, f32[1024,16]{1,0:T(8,128)}) custom-call(bf16[512,1024]{1,0:T(8,128)(2,1)} %collective-permute-done.6.refs_0_, bf16[512,1152]{1,0:T(8,128)(2,1)} %collective-permute-done.2.refs_1_, ...), custom_call_target="tpu_custom_call" | custom-call | flops 4831838208 | tf_op jit(solution)/shard_map/experts/pallas_call | solution.py:296
  228.1 22.1 %experts.15 = (bf16[512,1024]{1,0:T(8,128)(2,1)}, bf16[512,1024]{1,0:T(8,128)(2,1)}, bf16[6,1024,256]{2,1,0:T(8,128)(2,1)}, bf16[6,1024,256]{2,1,0:T(8,128)(2,1)}, f32[1024,16]{1,0:T(8,128)}) custom-call(bf16[512,1024]{1,0:T(8,128)(2,1)} %copy-done.27, bf16[512,1152]{1,0:T(8,128)(2,1)} %fusion.13.refs_1_, bf16[128,16]{1,0:T(8,128)(2,1)} %get-tuple-element.439.refs_2_, ...), custom_call_target="tpu_custom_call" | custom-call | flops 4831838208 | tf_op jit(solution)/shard_map/experts/pallas_call | solution.py:296
  254.6 4.5 fusion.28
  259.1 4.0 grad_blocks.3
  263.2 4.9 collective-permute-done.21
  272.4 4.3 add_convert_fusion.1
  283.9 20.9 %attend_back.1 = (bf16[512,512]{1,0:T(8,128)(2,1)S(1)}, bf16[512,512]{1,0:T(8,128)(2,1)S(1)}, bf16[512,2560]{1,0:T(8,128)(2,1)}, bf16[512,256]{1,0:T(8,128)(2,1)S(1)}) custom-call(bf16[512,1024]{1,0:T(8,128)(2,1)S(1)} %get-tuple-element.251.refs_0_.middle_ref, bf16[2560,1024]{1,0:T(8,128)(2,1)} %output_weight.1, ...), custom_call_target="tpu_custom_call" | custom-call | flops 4026531840 | tf_op jit(solution)/shard_map/attend_back/pallas_call | solution.py:529
  306.9 8.1 %collective-permute-done.19 = bf16[3,1024,256]{2,1,0:T(8,128)(2,1)} collective-permute-done((bf16[3,1024,256]{2,1,0:T(8,128)(2,1)}, bf16[3,1024,256]{2,1,0:T(8,128)(2,1)}, u32[]{:S(2)}, u32[]{:S(2)}) %collective-permute-start.19) | collective-permute-done | bytes 1572896 | tf_op jit(solution)/shard_map/ppermute | solution.py:595
  317.9 4.7 grad_blocks.4
  325.2 4.9 fusion.32
  341.5 6.2 %collective-permute-done.26 = bf16[2,80,1024]{2,1,0:T(8,128)(2,1)S(1)} collective-permute-done((bf16[2,80,1024]{2,1,0:T(8,128)(2,1)S(1)}, bf16[2,80,1024]{2,1,0:T(8,128)(2,1)S(1)}, u32[]{:S(2)}, u32[]{:S(2)}) %collective-permute-start.26) | collective-permute-done | bytes 327712 | tf_op jit(solution)/shard_map/ppermute | solution.py:652
  353.9 7.6 %collective-permute-done.35 = bf16[1,80,1024]{2,1,0:T(8,128)(2,1)S(1)} collective-permute-done((bf16[1,80,1024]{2,1,0:T(8,128)(2,1)S(1)}, bf16[1,80,1024]{2,1,0:T(8,128)(2,1)S(1)}, u32[]{:S(2)}, u32[]{:S(2)}) %collective-permute-start.35) | collective-permute-done | bytes 163872 | tf_op jit(solution)/shard_map/ppermute | solution.py:652
  380.6 5.6 %collective-permute-done.40 = bf16[2,80,1024]{2,1,0:T(8,128)(2,1)S(1)} collective-permute-done((bf16[2,80,1024]{2,1,0:T(8,128)(2,1)S(1)}, bf16[2,80,1024]{2,1,0:T(8,128)(2,1)S(1)}, u32[]{:S(2)}, u32[]{:S(2)}) %collective-permute-start.40) | collective-permute-done | bytes 327712 | tf_op jit(solution)/shard_map/ppermute | solution.py:652
  388.6 5.6 %collective-permute-done.44 = bf16[2,32,1408]{2,1,0:T(8,128)(2,1)S(1)} collective-permute-done((bf16[2,32,1408]{2,1,0:T(8,128)(2,1)S(1)}, bf16[2,32,1408]{2,1,0:T(8,128)(2,1)S(1)}, u32[]{:S(2)}, u32[]{:S(2)}) %collective-permute-start.44) | collective-permute-done | bytes 180256 | tf_op jit(solution)/shard_map/ppermute | solution.py:652
  401.0 4.0 collective-permute-done.43
  416.8 4.6 collective-permute-done.48
  429.6 4.0 collective-permute-done.46.refs_1_
  437.2 18.1 %collective-permute-done.59.refs_1_ = bf16[8,32,1408]{2,1,0:T(8,128)(2,1)S(1)} collective-permute-done((bf16[8,32,1408]{2,1,0:T(8,128)(2,1)S(1)}, bf16[8,32,1408]{2,1,0:T(8,128)(2,1)S(1)}, u32[]{:S(2)}, u32[]{:S(2)}) %collective-permute-start.59) | collective-permute-done | bytes 720928 | tf_op jit(solution)/shard_map/ppermute | solution.py:652
  455.9 5.6 %assemble.3 = f32[32,80,1024]{2,1,0:T(8,128)} custom-call(s32[10]{0:T(128)S(1)} %stack.231.order_ref, bf16[8,80,1024]{2,1,0:T(8,128)(2,1)S(1)} %pad_maximum_fusion.2.refs_0_, bf16[8,80,1024]{2,1,0:T(8,128)(2,1)S(1)} %collective-permute-done.46.refs_1_, bf16[8,80,1024]{2,1,0:T(8,128)(2,1)S(1)} %collective-permute-done.49.refs_2_, ...), custom_call_target="tpu_custom_call" | custom-call | bytes 5242880 | tf_op jit(solution)/shard_map/assemble/pallas_call | solution.py:777
  466.8 4.8 assemble.5
  478.5 8.6 %assemble.4 = f32[32,32,2560]{2,1,0:T(8,128)} custom-call(s32[10]{0:T(128)S(1)} %stack.231.order_ref, bf16[8,32,2560]{2,1,0:T(8,128)(2,1)S(1)} %pad_maximum_fusion.1.refs_0_, bf16[8,32,2560]{2,1,0:T(8,128)(2,1)S(1)} %collective-permute-done.34.refs_1_, bf16[8,32,2560]{2,1,0:T(8,128)(2,1)} %collective-permute-done.56.refs_2_, ...), custom_call_target="tpu_custom_call" | custom-call | bytes 5242880 | tf_op jit(solution)/shard_map/assemble/pallas_call | solution.py:777
  (301 shorter events, 151.9 us)
Async XLA Ops:
  3.6 39.8 %collective-permute-start = (bf16[3,1024,256]{2,1,0:T(8,128)(2,1)}, bf16[3,1024,256]{2,1,0:T(8,128)(2,1)}, u32[]{:S(2)}, u32[]{:S(2)}) collective-permute-start(bf16[3,1024,256]{2,1,0:T(8,128)(2,1)} %pad_maximum_fusion.refs_4_), channel_id=1, source_target_pairs={{0,2},{1,3},{2,4},{3,5},{4,6},{5,7},{6,0},{7,1},{8,10},{9,11},{10,... | collective-permute-start | bytes 4718600 | tf_op jit(solution)/shard_map/ppermute | solution.py:595
  8.5 28.3 %collective-permute-start.1 = (bf16[512,1152]{1,0:T(8,128)(2,1)}, bf16[512,1152]{1,0:T(8,128)(2,1)}, u32[]{:S(2)}, u32[]{:S(2)}) collective-permute-start(bf16[512,1152]{1,0:T(8,128)(2,1)} %fusion.13.refs_1_), channel_id=1, source_target_pairs={{0,1},{1,0},{2,3},{3,2},{4,5},{5,4},{6,7},{7,6},{8,9},{9,8},{10,11... | collective-permute-start | bytes 3538952 | tf_op jit(solution)/shard_map/ppermute | solution.py:602
  10.0 27.5 %collective-permute-start.2 = (bf16[512,1152]{1,0:T(8,128)(2,1)}, bf16[512,1152]{1,0:T(8,128)(2,1)}, u32[]{:S(2)}, u32[]{:S(2)}) collective-permute-start(bf16[512,1152]{1,0:T(8,128)(2,1)} %fusion.13.refs_1_), channel_id=1, source_target_pairs={{0,16},{8,24},{16,0},{24,8},{1,17},{9,25},{17,1},{25,9},{2,18},{10... | collective-permute-start | bytes 3538952 | tf_op jit(solution)/shard_map/ppermute | solution.py:605
  11.5 36.9 %collective-permute-start.3 = (bf16[3,1024,256]{2,1,0:T(8,128)(2,1)}, bf16[3,1024,256]{2,1,0:T(8,128)(2,1)}, u32[]{:S(2)}, u32[]{:S(2)}) collective-permute-start(bf16[3,1024,256]{2,1,0:T(8,128)(2,1)} %pad_maximum_fusion.refs_4_), channel_id=1, source_target_pairs={{0,8},{8,0},{16,24},{24,16},{1,9},{9,1},{17,25},{25,17},{2,10},{10... | collective-permute-start | bytes 4718600 | tf_op jit(solution)/shard_map/ppermute | solution.py:591
  43.4 25.7 %collective-permute-start.5 = (bf16[512,1024]{1,0:T(8,128)(2,1)S(1)}, bf16[512,1024]{1,0:T(8,128)(2,1)}, u32[]{:S(2)}, u32[]{:S(2)}) collective-permute-start(bf16[512,1024]{1,0:T(8,128)(2,1)S(1)} %multiply_convert_fusion.refs_0_), channel_id=1, source_target_pairs={{0,1},{1,0},{2,3},{3,2},{4,5},{5,4},{6,7},{7,6},{8,9},{9,8},{10,11... | collective-permute-start | bytes 3145736 | tf_op jit(solution)/shard_map/ppermute | solution.py:602
  44.9 25.4 %collective-permute-start.6 = (bf16[512,1024]{1,0:T(8,128)(2,1)S(1)}, bf16[512,1024]{1,0:T(8,128)(2,1)}, u32[]{:S(2)}, u32[]{:S(2)}) collective-permute-start(bf16[512,1024]{1,0:T(8,128)(2,1)S(1)} %multiply_convert_fusion.refs_0_), channel_id=1, source_target_pairs={{0,16},{8,24},{16,0},{24,8},{1,17},{9,25},{17,1},{25,9},{2,18},{10... | collective-permute-start | bytes 3145736 | tf_op jit(solution)/shard_map/ppermute | solution.py:605
  48.2 50.5 %collective-permute-start.8 = (bf16[3,1024,256]{2,1,0:T(8,128)(2,1)}, bf16[3,1024,256]{2,1,0:T(8,128)(2,1)S(1)}, u32[]{:S(2)}, u32[]{:S(2)}) collective-permute-start(bf16[3,1024,256]{2,1,0:T(8,128)(2,1)} %collective-permute-done.refs_6_), channel_id=1, source_target_pairs={{0,2},{1,3},{2,4},{3,5},{4,6},{5,7},{6,0},{7,1},{8,10},{9,11},{10,... | collective-permute-start | bytes 4718600 | tf_op jit(solution)/shard_map/ppermute | solution.py:595
  70.3 28.4 %collective-permute-start.7 = (bf16[512,1152]{1,0:T(8,128)(2,1)}, bf16[512,1152]{1,0:T(8,128)(2,1)S(1)}, u32[]{:S(2)}, u32[]{:S(2)}) collective-permute-start(bf16[512,1152]{1,0:T(8,128)(2,1)} %fusion.13.refs_1_), channel_id=1, source_target_pairs={{0,17},{1,16},{2,19},{3,18},{4,21},{5,20},{6,23},{7,22},{8,25},{9,... | collective-permute-start | bytes 3538952 | tf_op jit(solution)/shard_map/ppermute | solution.py:611
  98.7 23.7 %collective-permute-start.9 = (bf16[3,1024,256]{2,1,0:T(8,128)(2,1)S(1)}, bf16[3,1024,256]{2,1,0:T(8,128)(2,1)S(1)}, u32[]{:S(2)}, u32[]{:S(2)}) collective-permute-start(bf16[3,1024,256]{2,1,0:T(8,128)(2,1)S(1)} %collective-permute-done.8.refs_4_), channel_id=1, source_target_pairs={{0,8},{8,0},{16,24},{24,16},{1,9},{9,1},{17,25},{25,17},{2,10},{10... | collective-permute-start | bytes 4718600 | tf_op jit(solution)/shard_map/ppermute | solution.py:591
  98.8 26.6 %collective-permute-start.12 = (bf16[512,1024]{1,0:T(8,128)(2,1)S(1)}, bf16[512,1024]{1,0:T(8,128)(2,1)}, u32[]{:S(2)}, u32[]{:S(2)}) collective-permute-start(bf16[512,1024]{1,0:T(8,128)(2,1)S(1)} %copy-done.28), channel_id=1, source_target_pairs={{0,17},{1,16},{2,19},{3,18},{4,21},{5,20},{6,23},{7,22},{8,25},{9,... | collective-permute-start | bytes 3145736 | tf_op jit(solution)/shard_map/ppermute | solution.py:611
  100.3 46.2 %collective-permute-start.10 = (bf16[3,1024,256]{2,1,0:T(8,128)(2,1)S(1)}, bf16[3,1024,256]{2,1,0:T(8,128)(2,1)}, u32[]{:S(2)}, u32[]{:S(2)}) collective-permute-start(bf16[3,1024,256]{2,1,0:T(8,128)(2,1)S(1)} %collective-permute-done.8.refs_4_), channel_id=1, source_target_pairs={{0,2},{1,3},{2,4},{3,5},{4,6},{5,7},{6,0},{7,1},{8,10},{9,11},{10,... | collective-permute-start | bytes 4718600 | tf_op jit(solution)/shard_map/ppermute | solution.py:595
  146.4 29.5 %collective-permute-start.13 = (bf16[6,1024,256]{2,1,0:T(8,128)(2,1)}, bf16[6,1024,256]{2,1,0:T(8,128)(2,1)}, u32[]{:S(2)}, u32[]{:S(2)}) collective-permute-start(bf16[6,1024,256]{2,1,0:T(8,128)(2,1)} %get-tuple-element.220), channel_id=1, source_target_pairs={{0,8},{8,0},{16,24},{24,16},{1,9},{9,1},{17,25},{25,17},{2,10},{10... | collective-permute-start | bytes 9437192 | tf_op jit(solution)/shard_map/ppermute | solution.py:591
  178.9 49.2 %collective-permute-start.14 = (bf16[3,1024,256]{2,1,0:T(8,128)(2,1)}, bf16[3,1024,256]{2,1,0:T(8,128)(2,1)}, u32[]{:S(2)}, u32[]{:S(2)}) collective-permute-start(bf16[3,1024,256]{2,1,0:T(8,128)(2,1)} %add_convert_fusion.2), channel_id=1, source_target_pairs={{0,2},{1,3},{2,4},{3,5},{4,6},{5,7},{6,0},{7,1},{8,10},{9,11},{10,... | collective-permute-start | bytes 4718600 | tf_op jit(solution)/shard_map/ppermute | solution.py:595
  179.5 70.8 %collective-permute-start.18 = (bf16[512,1024]{1,0:T(8,128)(2,1)}, bf16[512,1024]{1,0:T(8,128)(2,1)S(1)}, u32[]{:S(2)}, u32[]{:S(2)}) collective-permute-start(bf16[512,1024]{1,0:T(8,128)(2,1)} %get-tuple-element.244), channel_id=1, source_target_pairs={{0,17},{1,16},{2,19},{3,18},{4,21},{5,20},{6,23},{7,22},{8,25},{9,... | collective-permute-start | bytes 3145736 | tf_op jit(solution)/shard_map/ppermute | solution.py:611
  225.9 25.3 %collective-permute-start.17 = (bf16[512,1024]{1,0:T(8,128)(2,1)}, bf16[512,1024]{1,0:T(8,128)(2,1)}, u32[]{:S(2)}, u32[]{:S(2)}) collective-permute-start(bf16[512,1024]{1,0:T(8,128)(2,1)} %get-tuple-element.243), channel_id=1, source_target_pairs={{0,16},{8,24},{16,0},{24,8},{1,17},{9,25},{17,1},{25,9},{2,18},{10... | collective-permute-start | bytes 3145736 | tf_op jit(solution)/shard_map/ppermute | solution.py:605
  226.5 24.9 %collective-permute-start.16 = (bf16[512,1024]{1,0:T(8,128)(2,1)}, bf16[512,1024]{1,0:T(8,128)(2,1)}, u32[]{:S(2)}, u32[]{:S(2)}) collective-permute-start(bf16[512,1024]{1,0:T(8,128)(2,1)} %get-tuple-element.242), channel_id=1, source_target_pairs={{0,1},{1,0},{2,3},{3,2},{4,5},{5,4},{6,7},{7,6},{8,9},{9,8},{10,11... | collective-permute-start | bytes 3145736 | tf_op jit(solution)/shard_map/ppermute | solution.py:602
  250.2 22.2 %collective-permute-start.15 = (bf16[6,1024,256]{2,1,0:T(8,128)(2,1)}, bf16[6,1024,256]{2,1,0:T(8,128)(2,1)S(1)}, u32[]{:S(2)}, u32[]{:S(2)}) collective-permute-start(bf16[6,1024,256]{2,1,0:T(8,128)(2,1)} %get-tuple-element.240), channel_id=1, source_target_pairs={{0,8},{8,0},{16,24},{24,16},{1,9},{9,1},{17,25},{25,17},{2,10},{10... | collective-permute-start | bytes 9437192 | tf_op jit(solution)/shard_map/ppermute | solution.py:591
  270.9 33.9 %collective-permute-start.22 = (bf16[8,80,1024]{2,1,0:T(8,128)(2,1)}, bf16[8,80,1024]{2,1,0:T(8,128)(2,1)}, u32[]{:S(2)}, u32[]{:S(2)}) collective-permute-start(bf16[8,80,1024]{2,1,0:T(8,128)(2,1)} %get-tuple-element.415), channel_id=1, source_target_pairs={{0,16},{1,17},{2,18},{3,19},{4,20},{5,21},{6,22},{7,23},{8,9},{9,8... | collective-permute-start | bytes 3932168 | tf_op jit(solution)/shard_map/ppermute | solution.py:652
  276.7 38.2 %collective-permute-start.19 = (bf16[3,1024,256]{2,1,0:T(8,128)(2,1)}, bf16[3,1024,256]{2,1,0:T(8,128)(2,1)}, u32[]{:S(2)}, u32[]{:S(2)}) collective-permute-start(bf16[3,1024,256]{2,1,0:T(8,128)(2,1)} %add_convert_fusion.1), channel_id=1, source_target_pairs={{0,2},{1,3},{2,4},{3,5},{4,6},{5,7},{6,0},{7,1},{8,10},{9,11},{10,... | collective-permute-start | bytes 4718600 | tf_op jit(solution)/shard_map/ppermute | solution.py:595
  277.7 39.2 %collective-permute-start.20 = (bf16[512,1024]{1,0:T(8,128)(2,1)}, bf16[512,1024]{1,0:T(8,128)(2,1)S(1)}, u32[]{:S(2)}, u32[]{:S(2)}) collective-permute-start(bf16[512,1024]{1,0:T(8,128)(2,1)} %get-tuple-element.250), channel_id=1, source_target_pairs={{0,17},{1,16},{2,19},{3,18},{4,21},{5,20},{6,23},{7,22},{8,25},{9,... | collective-permute-start | bytes 3145736 | tf_op jit(solution)/shard_map/ppermute | solution.py:611
  330.9 17.7 %collective-permute-start.24 = (bf16[8,32,2560]{2,1,0:T(8,128)(2,1)S(1)}, bf16[8,32,2560]{2,1,0:T(8,128)(2,1)S(1)}, u32[]{:S(2)}, u32[]{:S(2)}) collective-permute-start(bf16[8,32,2560]{2,1,0:T(8,128)(2,1)S(1)} %get-tuple-element.268), channel_id=1, source_target_pairs={{0,16},{1,17},{2,18},{3,19},{4,20},{5,21},{6,22},{7,23},{8,9},{9,8... | collective-permute-start | bytes 3932168 | tf_op jit(solution)/shard_map/ppermute | solution.py:652
  405.1 28.5 %collective-permute-start.46 = (bf16[8,80,1024]{2,1,0:T(8,128)(2,1)S(1)}, bf16[8,80,1024]{2,1,0:T(8,128)(2,1)S(1)}, u32[]{:S(2)}, u32[]{:S(2)}) collective-permute-start(bf16[8,80,1024]{2,1,0:T(8,128)(2,1)S(1)} %pad_maximum_fusion.2.refs_0_), channel_id=1, source_target_pairs={{0,16},{1,17},{2,18},{3,19},{4,20},{5,21},{6,22},{7,23},{8,9},{9,8... | collective-permute-start | bytes 3932168 | tf_op jit(solution)/shard_map/ppermute | solution.py:652
  411.2 18.1 %collective-permute-start.33 = (bf16[4,32,2560]{2,1,0:T(8,128)(2,1)S(1)}, bf16[4,32,2560]{2,1,0:T(8,128)(2,1)S(1)}, u32[]{:S(2)}, u32[]{:S(2)}) collective-permute-start(bf16[4,32,2560]{2,1,0:T(8,128)(2,1)S(1)} %pad_maximum_fusion.3), channel_id=1, source_target_pairs={{0,1},{1,0},{2,3},{3,2},{4,5},{5,4},{6,7},{7,6},{8,24},{9,25},{10,... | collective-permute-start | bytes 1966088 | tf_op jit(solution)/shard_map/ppermute | solution.py:652
  422.6 38.9 %collective-permute-start.55 = (bf16[3,1024,256]{2,1,0:T(8,128)(2,1)S(1)}, bf16[3,1024,256]{2,1,0:T(8,128)(2,1)S(1)}, u32[]{:S(2)}, u32[]{:S(2)}) collective-permute-start(bf16[3,1024,256]{2,1,0:T(8,128)(2,1)S(1)} %add_convert_fusion), channel_id=1, source_target_pairs={{0,2},{1,3},{2,4},{3,5},{4,6},{5,7},{6,0},{7,1},{8,10},{9,11},{10,... | collective-permute-start | bytes 4718600 | tf_op jit(solution)/shard_map/ppermute | solution.py:595
  429.4 32.1 %collective-permute-start.34 = (bf16[8,32,2560]{2,1,0:T(8,128)(2,1)S(1)}, bf16[8,32,2560]{2,1,0:T(8,128)(2,1)S(1)}, u32[]{:S(2)}, u32[]{:S(2)}) collective-permute-start(bf16[8,32,2560]{2,1,0:T(8,128)(2,1)S(1)} %pad_maximum_fusion.1.refs_0_), channel_id=1, source_target_pairs={{0,16},{1,17},{2,18},{3,19},{4,20},{5,21},{6,22},{7,23},{8,9},{9,8... | collective-permute-start | bytes 3932168 | tf_op jit(solution)/shard_map/ppermute | solution.py:652
  433.6 21.8 %collective-permute-start.49 = (bf16[8,80,1024]{2,1,0:T(8,128)(2,1)S(1)}, bf16[8,80,1024]{2,1,0:T(8,128)(2,1)S(1)}, u32[]{:S(2)}, u32[]{:S(2)}) collective-permute-start(bf16[8,80,1024]{2,1,0:T(8,128)(2,1)S(1)} %pad_maximum_fusion.2.refs_0_), channel_id=1, source_target_pairs={{0,8},{8,0},{16,24},{24,16},{1,9},{9,1},{17,25},{25,17},{2,10},{10... | collective-permute-start | bytes 3932168 | tf_op jit(solution)/shard_map/ppermute | solution.py:591
  433.6 22.3 %collective-permute-start.50 = (bf16[8,80,1024]{2,1,0:T(8,128)(2,1)S(1)}, bf16[8,80,1024]{2,1,0:T(8,128)(2,1)S(1)}, u32[]{:S(2)}, u32[]{:S(2)}) collective-permute-start(bf16[8,80,1024]{2,1,0:T(8,128)(2,1)S(1)} %collective-permute-done.46.refs_1_), channel_id=1, source_target_pairs={{0,8},{8,0},{16,24},{24,16},{1,9},{9,1},{17,25},{25,17},{2,10},{10... | collective-permute-start | bytes 3932168 | tf_op jit(solution)/shard_map/ppermute | solution.py:591
  437.1 18.3 %collective-permute-start.59 = (bf16[8,32,1408]{2,1,0:T(8,128)(2,1)S(1)}, bf16[8,32,1408]{2,1,0:T(8,128)(2,1)S(1)}, u32[]{:S(2)}, u32[]{:S(2)}) collective-permute-start(bf16[8,32,1408]{2,1,0:T(8,128)(2,1)S(1)} %constant_dynamic-update-slice_fusion.refs_0_), channel_id=1, source_target_pairs={{0,16},{1,17},{2,18},{3,19},{4,20},{5,21},{6,22},{7,23},{8,9},{9,8... | collective-permute-start | bytes 2162696 | tf_op jit(solution)/shard_map/ppermute | solution.py:652
  461.6 16.9 %collective-permute-start.56 = (bf16[8,32,2560]{2,1,0:T(8,128)(2,1)S(1)}, bf16[8,32,2560]{2,1,0:T(8,128)(2,1)}, u32[]{:S(2)}, u32[]{:S(2)}) collective-permute-start(bf16[8,32,2560]{2,1,0:T(8,128)(2,1)S(1)} %pad_maximum_fusion.1.refs_0_), channel_id=1, source_target_pairs={{0,8},{8,0},{16,24},{24,16},{1,9},{9,1},{17,25},{25,17},{2,10},{10... | collective-permute-start | bytes 3932168 | tf_op jit(solution)/shard_map/ppermute | solution.py:591
  461.6 16.9 %collective-permute-start.57 = (bf16[8,32,2560]{2,1,0:T(8,128)(2,1)S(1)}, bf16[8,32,2560]{2,1,0:T(8,128)(2,1)}, u32[]{:S(2)}, u32[]{:S(2)}) collective-permute-start(bf16[8,32,2560]{2,1,0:T(8,128)(2,1)S(1)} %collective-permute-done.34.refs_1_), channel_id=1, source_target_pairs={{0,8},{8,0},{16,24},{24,16},{1,9},{9,1},{17,25},{25,17},{2,10},{10... | collective-permute-start | bytes 3932168 | tf_op jit(solution)/shard_map/ppermute | solution.py:591
  464.1 25.5 %collective-permute-start.51 = (bf16[512,1024]{1,0:T(8,128)(2,1)}, bf16[512,1024]{1,0:T(8,128)(2,1)}, u32[]{:S(2)}, u32[]{:S(2)}) collective-permute-start(bf16[512,1024]{1,0:T(8,128)(2,1)} %get-tuple-element.324), channel_id=1, source_target_pairs={{0,1},{1,0},{2,3},{3,2},{4,5},{5,4},{6,7},{7,6},{8,9},{9,8},{10,11... | collective-permute-start | bytes 3145736 | tf_op jit(solution)/shard_map/ppermute | solution.py:602
  465.5 25.2 %collective-permute-start.52 = (bf16[512,1024]{1,0:T(8,128)(2,1)}, bf16[512,1024]{1,0:T(8,128)(2,1)}, u32[]{:S(2)}, u32[]{:S(2)}) collective-permute-start(bf16[512,1024]{1,0:T(8,128)(2,1)} %get-tuple-element.327), channel_id=1, source_target_pairs={{0,16},{8,24},{16,0},{24,8},{1,17},{9,25},{17,1},{25,9},{2,18},{10... | collective-permute-start | bytes 3145736 | tf_op jit(solution)/shard_map/ppermute | solution.py:605
  (86 other events, 786.7 us)

commit v5 on v4

--- a/solution.py
+++ b/solution.py
@@ -441,7 +441,7 @@
             jax.ShapeDtypeStruct((tokens, H * NE * DH), bf16),
             jax.ShapeDtypeStruct((tokens, 256), f32),
         ],
-        compiler_params=pltpu.CompilerParams(vmem_limit_bytes=48 * 1024 * 1024),
+        compiler_params=pltpu.CompilerParams(vmem_limit_bytes=32 * 1024 * 1024),
         cost_estimate=pl.CostEstimate(
             flops=2 * tokens * H * DH * (D * (NE + 2) + 2 * tokens),
             bytes_accessed=0,
@@ -552,7 +552,7 @@
             pltpu.VMEM((tokens, 128), f32),
             pltpu.VMEM((tokens, 128), f32),
         ],
-        compiler_params=pltpu.CompilerParams(vmem_limit_bytes=48 * 1024 * 1024),
+        compiler_params=pltpu.CompilerParams(vmem_limit_bytes=32 * 1024 * 1024),
         cost_estimate=pl.CostEstimate(
             flops=2 * tokens * H * DH * (D * NE + 5 * tokens), bytes_accessed=0, transcendentals=0
         ),
@@ -724,7 +724,7 @@
             out_specs=[pl.BlockSpec((group, rows, columns), lambda i, o: (i, 0, 0))] * 2,
         ),
         out_shape=[shape, shape],
-        compiler_params=pltpu.CompilerParams(vmem_limit_bytes=40 * 1024 * 1024),
+        compiler_params=pltpu.CompilerParams(vmem_limit_bytes=24 * 1024 * 1024),
         cost_estimate=small_cost(tokens * total * columns, total * columns * 2),
         name="grad_blocks",
     )(order, *operands)
@@ -795,7 +795,7 @@
             jax.ShapeDtypeStruct((width, n * rows) if width % 128 else (n, rows, width), f32)
             for _, width in cuts
         ],
-        compiler_params=pltpu.CompilerParams(vmem_limit_bytes=40 * 1024 * 1024),
+        compiler_params=pltpu.CompilerParams(vmem_limit_bytes=24 * 1024 * 1024),
         cost_estimate=small_cost(0, n * rows * columns * 2),
         name="assemble",
     )(order, *pieces)

time: 502 us -> 499 us (level)
  local copies, waits for them, and re-layouts: 18.7 us -> 30.4 us
  Pallas kernels: 239 us -> 232 us
    unnamed x118 -> x138, local copies, waits for them, and re-layouts: 13.9 us -> 25.6 us
    ppermute x24, waiting for transfers between devices: 78.6 us -> 84 us  [exchange(): return lax.ppermute(value, ('dp', 'expert'), pairs)]
  transfers between devices with their start and end apart: 62 -> 62, of which waited for: 36 -> 32; matrix products, arithmetic and copies ran while one was open for 11% -> 10% of each run, Pallas kernels for 47% -> 46%
where the time goes in v5:
time: 499 us; the launch traced here: 491 us
  Pallas kernels  232 us (46%)
  waiting for transfers between devices  124 us (25%)
  starting transfers between devices  53.8 us (11%)
  other arithmetic  39.9 us (8%)
  local copies, waits for them, and re-layouts  30.4 us (6%)
  matrix products  8.83 us (2%)
    pallas_call x8, Pallas kernels, run_experts(): pl.pallas_call(functools.partial(experts_kernel, blocks, pairs, previous...  170 us
    ppermute x24, waiting for transfers between devices, exchange(): return lax.ppermute(value, ('dp', 'expert'), pairs)  84 us
    unnamed x138, local copies, waits for them, and re-layouts  25.6 us
    ppermute x24, starting transfers between devices, exchange(): return lax.ppermute(value, ('dp', 'expert'), pairs)  23.7 us
    pallas_call x1, Pallas kernels, attend_back(): pl.pallas_call(attend_back_kernel, grid=(H,), in_specs=[whole, pl.BlockSp...  19.1 us
    pallas_call x3, Pallas kernels, assemble(): pl.pallas_call(functools.partial(assemble_kernel, count, cuts), grid_spec...  19 us
    convert_element_type x18, other arithmetic, add_low(): return total.astype(bf16)  16.6 us
    pallas_call x3, Pallas kernels, grad_blocks(): pl.pallas_call(functools.partial(grad_blocks_kernel, steps, group, rows,...  12.1 us
  transfers between devices with their start and end apart: 62, of which 32 were waited for; matrix products, arithmetic and copies ran while one was open for 10% of the time, Pallas kernels for 46%

profile of v5, /device:TPU:0, one launch (start us, length us, event | category | flops | bytes accessed | tf_op | source)
XLA Modules:
  0.0 491.4 jit_solution(4921273893507241523)
XLA Ops:
  20.7 12.1 %attend.1 = (bf16[512,512]{1,0:T(8,128)(2,1)S(1)}, bf16[512,512]{1,0:T(8,128)(2,1)S(1)}, f32[512,2560]{1,0:T(8,128)S(1)}, bf16[512,512]{1,0:T(8,128)(2,1)S(1)}, ...) custom-call(bf16[512,1024]{1,0:T(8,128)(2,1)S(1)} %fusion.3.normed_ref.left_a.left_b, ...), custom_call_target="tpu_custom_call" | custom-call | flops 4294967296 | tf_op jit(solution)/shard_map/attend/pallas_call | solution.py:423
  38.6 4.8 collective-permute-done.refs_6_
  48.4 19.9 %experts.8 = (bf16[512,1024]{1,0:T(8,128)(2,1)}, bf16[512,1024]{1,0:T(8,128)(2,1)}, f32[6,1024,256]{2,1,0:T(8,128)}, f32[6,1024,256]{2,1,0:T(8,128)}, f32[1024,16]{1,0:T(8,128)}) custom-call(bf16[512,1024]{1,0:T(8,128)(2,1)} %multiply_convert_fusion.refs_0_, bf16[512,1152]{1,0:T(8,128)(2,1)} %fusion.13.refs_1_, bf16[128,16]{1,0:T(8,128)(2,1)} %get-tuple-element.441.refs_2_, ...), custom_call_target="tpu_custom_call" | custom-call | flops 4831838208 | tf_op jit(solution)/shard_map/experts/pallas_call | solution.py:296
  72.0 21.4 %experts.9 = (bf16[512,1024]{1,0:T(8,128)(2,1)}, bf16[512,1024]{1,0:T(8,128)(2,1)}, f32[6,1024,256]{2,1,0:T(8,128)}, f32[6,1024,256]{2,1,0:T(8,128)}, f32[1024,16]{1,0:T(8,128)}) custom-call(bf16[512,1024]{1,0:T(8,128)(2,1)} %collective-permute-done.5.refs_0_, bf16[512,1152]{1,0:T(8,128)(2,1)} %collective-permute-done.1.refs_1_, ...), custom_call_target="tpu_custom_call" | custom-call | flops 4831838208 | tf_op jit(solution)/shard_map/experts/pallas_call | solution.py:296
  93.4 5.5 %collective-permute-done.7.refs_1_ = bf16[512,1152]{1,0:T(8,128)(2,1)S(1)} collective-permute-done((bf16[512,1152]{1,0:T(8,128)(2,1)}, bf16[512,1152]{1,0:T(8,128)(2,1)S(1)}, u32[]{:S(2)}, u32[]{:S(2)}) %collective-permute-start.7) | collective-permute-done | bytes 1179680 | tf_op jit(solution)/shard_map/ppermute | solution.py:611
  100.9 21.5 %experts.10 = (bf16[512,1024]{1,0:T(8,128)(2,1)}, bf16[512,1024]{1,0:T(8,128)(2,1)}, f32[6,1024,256]{2,1,0:T(8,128)}, f32[6,1024,256]{2,1,0:T(8,128)}, f32[1024,16]{1,0:T(8,128)}) custom-call(bf16[512,1024]{1,0:T(8,128)(2,1)} %collective-permute-done.6.refs_0_, bf16[512,1152]{1,0:T(8,128)(2,1)} %collective-permute-done.2.refs_1_, ...), custom_call_target="tpu_custom_call" | custom-call | flops 4831838208 | tf_op jit(solution)/shard_map/experts/pallas_call | solution.py:296
  125.7 20.6 %experts.11 = (bf16[512,1024]{1,0:T(8,128)(2,1)}, bf16[512,1024]{1,0:T(8,128)(2,1)}, bf16[6,1024,256]{2,1,0:T(8,128)(2,1)}, bf16[6,1024,256]{2,1,0:T(8,128)(2,1)}, f32[1024,16]{1,0:T(8,128)}) custom-call(bf16[512,1024]{1,0:T(8,128)(2,1)} %collective-permute-done.12.refs_0_, bf16[512,1152]{1,0:T(8,128)(2,1)} %copy-done.48, ...), custom_call_target="tpu_custom_call" | custom-call | flops 4831838208 | tf_op jit(solution)/shard_map/experts/pallas_call | solution.py:296
  148.7 6.0 %collective-permute-done.11.refs_7_ = bf16[3,1024,256]{2,1,0:T(8,128)(2,1)} collective-permute-done((bf16[3,1024,256]{2,1,0:T(8,128)(2,1)}, bf16[3,1024,256]{2,1,0:T(8,128)(2,1)}, u32[]{:S(2)}, u32[]{:S(2)}) %collective-permute-start.11) | collective-permute-done | bytes 1572896 | tf_op jit(solution)/shard_map/ppermute | solution.py:591
  154.7 20.6 %experts.12 = (bf16[512,1024]{1,0:T(8,128)(2,1)}, bf16[512,1024]{1,0:T(8,128)(2,1)}, f32[6,1024,256]{2,1,0:T(8,128)}, f32[6,1024,256]{2,1,0:T(8,128)}, f32[1024,16]{1,0:T(8,128)}) custom-call(bf16[512,1024]{1,0:T(8,128)(2,1)} %collective-permute-done.12.refs_0_, bf16[512,1152]{1,0:T(8,128)(2,1)} %copy-done.48, bf16[128,16]{1,0:T(8,128)(2,1)} %get-tuple-element.439.refs_2_, ...), custom_call_target="tpu_custom_call" | custom-call | flops 4831838208 | tf_op jit(solution)/shard_map/experts/pallas_call | solution.py:296
  180.0 22.1 %experts.13 = (bf16[512,1024]{1,0:T(8,128)(2,1)}, bf16[512,1024]{1,0:T(8,128)(2,1)}, f32[6,1024,256]{2,1,0:T(8,128)}, f32[6,1024,256]{2,1,0:T(8,128)}, f32[1024,16]{1,0:T(8,128)}) custom-call(bf16[512,1024]{1,0:T(8,128)(2,1)} %collective-permute-done.5.refs_0_, bf16[512,1152]{1,0:T(8,128)(2,1)} %collective-permute-done.1.refs_1_, ...), custom_call_target="tpu_custom_call" | custom-call | flops 4831838208 | tf_op jit(solution)/shard_map/experts/pallas_call | solution.py:296
  202.1 22.1 %experts.14 = (bf16[512,1024]{1,0:T(8,128)(2,1)}, bf16[512,1024]{1,0:T(8,128)(2,1)}, f32[6,1024,256]{2,1,0:T(8,128)}, f32[6,1024,256]{2,1,0:T(8,128)}, f32[1024,16]{1,0:T(8,128)}) custom-call(bf16[512,1024]{1,0:T(8,128)(2,1)} %collective-permute-done.6.refs_0_, bf16[512,1152]{1,0:T(8,128)(2,1)} %collective-permute-done.2.refs_1_, ...), custom_call_target="tpu_custom_call" | custom-call | flops 4831838208 | tf_op jit(solution)/shard_map/experts/pallas_call | solution.py:296
  226.4 21.8 %experts.15 = (bf16[512,1024]{1,0:T(8,128)(2,1)}, bf16[512,1024]{1,0:T(8,128)(2,1)}, bf16[6,1024,256]{2,1,0:T(8,128)(2,1)}, bf16[6,1024,256]{2,1,0:T(8,128)(2,1)}, f32[1024,16]{1,0:T(8,128)}) custom-call(bf16[512,1024]{1,0:T(8,128)(2,1)} %multiply_convert_fusion.refs_0_, bf16[512,1152]{1,0:T(8,128)(2,1)} %fusion.13.refs_1_, ...), custom_call_target="tpu_custom_call" | custom-call | flops 4831838208 | tf_op jit(solution)/shard_map/experts/pallas_call | solution.py:296
  253.1 4.4 fusion.28
  257.5 4.0 grad_blocks.3
  261.6 4.9 collective-permute-done.21
  270.9 4.3 add_convert_fusion.1
  288.1 19.1 %attend_back.1 = (bf16[512,512]{1,0:T(8,128)(2,1)S(1)}, bf16[512,512]{1,0:T(8,128)(2,1)S(1)}, bf16[512,2560]{1,0:T(8,128)(2,1)S(1)}, bf16[512,256]{1,0:T(8,128)(2,1)S(1)}) custom-call(bf16[512,1024]{1,0:T(8,128)(2,1)S(1)} %copy-done.5, bf16[2560,1024]{1,0:T(8,128)(2,1)S(1)} %copy-done.6, bf16[512,512]{1,0:T(8,128)(2,1)S(1)} %copy-done.18, ...), custom_call_target="tpu_custom_call" | custom-call | flops 4026531840 | tf_op jit(solution)/shard_map/attend_back/pallas_call | solution.py:529
  309.3 4.1 collective-permute-done.19
  315.5 4.7 grad_blocks.4
  328.3 7.7 %collective-permute-done.25 = bf16[4,80,1024]{2,1,0:T(8,128)(2,1)S(1)} collective-permute-done((bf16[4,80,1024]{2,1,0:T(8,128)(2,1)S(1)}, bf16[4,80,1024]{2,1,0:T(8,128)(2,1)S(1)}, u32[]{:S(2)}, u32[]{:S(2)}) %collective-permute-start.25) | collective-permute-done | bytes 655392 | tf_op jit(solution)/shard_map/ppermute | solution.py:652
  341.1 5.7 %collective-permute-done.26 = bf16[2,80,1024]{2,1,0:T(8,128)(2,1)S(1)} collective-permute-done((bf16[2,80,1024]{2,1,0:T(8,128)(2,1)S(1)}, bf16[2,80,1024]{2,1,0:T(8,128)(2,1)S(1)}, u32[]{:S(2)}, u32[]{:S(2)}) %collective-permute-start.26) | collective-permute-done | bytes 327712 | tf_op jit(solution)/shard_map/ppermute | solution.py:652
  351.9 7.5 %collective-permute-done.35 = bf16[1,80,1024]{2,1,0:T(8,128)(2,1)S(1)} collective-permute-done((bf16[1,80,1024]{2,1,0:T(8,128)(2,1)S(1)}, bf16[1,80,1024]{2,1,0:T(8,128)(2,1)S(1)}, u32[]{:S(2)}, u32[]{:S(2)}) %collective-permute-start.35) | collective-permute-done | bytes 163872 | tf_op jit(solution)/shard_map/ppermute | solution.py:652
  370.6 5.0 %collective-permute-done.29 = bf16[2,32,2560]{2,1,0:T(8,128)(2,1)S(1)} collective-permute-done((bf16[2,32,2560]{2,1,0:T(8,128)(2,1)S(1)}, bf16[2,32,2560]{2,1,0:T(8,128)(2,1)S(1)}, u32[]{:S(2)}, u32[]{:S(2)}) %collective-permute-start.29) | collective-permute-done | bytes 327712 | tf_op jit(solution)/shard_map/ppermute | solution.py:652
  378.1 5.5 %collective-permute-done.40 = bf16[2,80,1024]{2,1,0:T(8,128)(2,1)S(1)} collective-permute-done((bf16[2,80,1024]{2,1,0:T(8,128)(2,1)S(1)}, bf16[2,80,1024]{2,1,0:T(8,128)(2,1)S(1)}, u32[]{:S(2)}, u32[]{:S(2)}) %collective-permute-start.40) | collective-permute-done | bytes 327712 | tf_op jit(solution)/shard_map/ppermute | solution.py:652
  386.3 5.2 %collective-permute-done.44 = bf16[2,32,1408]{2,1,0:T(8,128)(2,1)S(1)} collective-permute-done((bf16[2,32,1408]{2,1,0:T(8,128)(2,1)S(1)}, bf16[2,32,1408]{2,1,0:T(8,128)(2,1)S(1)}, u32[]{:S(2)}, u32[]{:S(2)}) %collective-permute-start.44) | collective-permute-done | bytes 180256 | tf_op jit(solution)/shard_map/ppermute | solution.py:652
  398.0 4.3 collective-permute-done.43
  413.0 4.6 collective-permute-done.48
  425.1 5.9 %collective-permute-done.46.refs_1_ = bf16[8,80,1024]{2,1,0:T(8,128)(2,1)S(1)} collective-permute-done((bf16[8,80,1024]{2,1,0:T(8,128)(2,1)S(1)}, bf16[8,80,1024]{2,1,0:T(8,128)(2,1)S(1)}, u32[]{:S(2)}, u32[]{:S(2)}) %collective-permute-start.46) | collective-permute-done | bytes 1310752 | tf_op jit(solution)/shard_map/ppermute | solution.py:652
  433.1 19.6 %collective-permute-done.59.refs_1_ = bf16[8,32,1408]{2,1,0:T(8,128)(2,1)S(1)} collective-permute-done((bf16[8,32,1408]{2,1,0:T(8,128)(2,1)S(1)}, bf16[8,32,1408]{2,1,0:T(8,128)(2,1)S(1)}, u32[]{:S(2)}, u32[]{:S(2)}) %collective-permute-start.59) | collective-permute-done | bytes 720928 | tf_op jit(solution)/shard_map/ppermute | solution.py:652
  453.3 5.6 %assemble.3 = f32[32,80,1024]{2,1,0:T(8,128)} custom-call(s32[10]{0:T(128)S(1)} %stack.231.order_ref, bf16[8,80,1024]{2,1,0:T(8,128)(2,1)S(1)} %pad_maximum_fusion.2.refs_0_, bf16[8,80,1024]{2,1,0:T(8,128)(2,1)S(1)} %collective-permute-done.46.refs_1_, bf16[8,80,1024]{2,1,0:T(8,128)(2,1)S(1)} %collective-permute-done.49.refs_2_, ...), custom_call_target="tpu_custom_call" | custom-call | bytes 5242880 | tf_op jit(solution)/shard_map/assemble/pallas_call | solution.py:777
  465.1 4.8 assemble.5
  476.8 8.6 %assemble.4 = f32[32,32,2560]{2,1,0:T(8,128)} custom-call(s32[10]{0:T(128)S(1)} %stack.231.order_ref, bf16[8,32,2560]{2,1,0:T(8,128)(2,1)S(1)} %pad_maximum_fusion.1.refs_0_, bf16[8,32,2560]{2,1,0:T(8,128)(2,1)S(1)} %collective-permute-done.34.refs_1_, bf16[8,32,2560]{2,1,0:T(8,128)(2,1)} %collective-permute-done.56.refs_2_, ...), custom_call_target="tpu_custom_call" | custom-call | bytes 5242880 | tf_op jit(solution)/shard_map/assemble/pallas_call | solution.py:777
  (322 shorter events, 155.5 us)
Async XLA Ops:
  3.6 39.8 %collective-permute-start = (bf16[3,1024,256]{2,1,0:T(8,128)(2,1)}, bf16[3,1024,256]{2,1,0:T(8,128)(2,1)}, u32[]{:S(2)}, u32[]{:S(2)}) collective-permute-start(bf16[3,1024,256]{2,1,0:T(8,128)(2,1)} %pad_maximum_fusion.refs_4_), channel_id=1, source_target_pairs={{0,2},{1,3},{2,4},{3,5},{4,6},{5,7},{6,0},{7,1},{8,10},{9,11},{10,... | collective-permute-start | bytes 4718600 | tf_op jit(solution)/shard_map/ppermute | solution.py:595
  8.5 30.1 %collective-permute-start.1 = (bf16[512,1152]{1,0:T(8,128)(2,1)}, bf16[512,1152]{1,0:T(8,128)(2,1)}, u32[]{:S(2)}, u32[]{:S(2)}) collective-permute-start(bf16[512,1152]{1,0:T(8,128)(2,1)} %fusion.13.refs_1_), channel_id=1, source_target_pairs={{0,1},{1,0},{2,3},{3,2},{4,5},{5,4},{6,7},{7,6},{8,9},{9,8},{10,11... | collective-permute-start | bytes 3538952 | tf_op jit(solution)/shard_map/ppermute | solution.py:602
  10.0 28.6 %collective-permute-start.2 = (bf16[512,1152]{1,0:T(8,128)(2,1)}, bf16[512,1152]{1,0:T(8,128)(2,1)}, u32[]{:S(2)}, u32[]{:S(2)}) collective-permute-start(bf16[512,1152]{1,0:T(8,128)(2,1)} %fusion.13.refs_1_), channel_id=1, source_target_pairs={{0,16},{8,24},{16,0},{24,8},{1,17},{9,25},{17,1},{25,9},{2,18},{10... | collective-permute-start | bytes 3538952 | tf_op jit(solution)/shard_map/ppermute | solution.py:605
  11.5 36.9 %collective-permute-start.3 = (bf16[3,1024,256]{2,1,0:T(8,128)(2,1)}, bf16[3,1024,256]{2,1,0:T(8,128)(2,1)}, u32[]{:S(2)}, u32[]{:S(2)}) collective-permute-start(bf16[3,1024,256]{2,1,0:T(8,128)(2,1)} %pad_maximum_fusion.refs_4_), channel_id=1, source_target_pairs={{0,8},{8,0},{16,24},{24,16},{1,9},{9,1},{17,25},{25,17},{2,10},{10... | collective-permute-start | bytes 4718600 | tf_op jit(solution)/shard_map/ppermute | solution.py:591
  43.4 25.9 %collective-permute-start.5 = (bf16[512,1024]{1,0:T(8,128)(2,1)}, bf16[512,1024]{1,0:T(8,128)(2,1)}, u32[]{:S(2)}, u32[]{:S(2)}) collective-permute-start(bf16[512,1024]{1,0:T(8,128)(2,1)} %multiply_convert_fusion.refs_0_), channel_id=1, source_target_pairs={{0,1},{1,0},{2,3},{3,2},{4,5},{5,4},{6,7},{7,6},{8,9},{9,8},{10,11... | collective-permute-start | bytes 3145736 | tf_op jit(solution)/shard_map/ppermute | solution.py:602
  44.9 25.6 %collective-permute-start.6 = (bf16[512,1024]{1,0:T(8,128)(2,1)}, bf16[512,1024]{1,0:T(8,128)(2,1)}, u32[]{:S(2)}, u32[]{:S(2)}) collective-permute-start(bf16[512,1024]{1,0:T(8,128)(2,1)} %multiply_convert_fusion.refs_0_), channel_id=1, source_target_pairs={{0,16},{8,24},{16,0},{24,8},{1,17},{9,25},{17,1},{25,9},{2,18},{10... | collective-permute-start | bytes 3145736 | tf_op jit(solution)/shard_map/ppermute | solution.py:605
  48.2 50.7 %collective-permute-start.8 = (bf16[3,1024,256]{2,1,0:T(8,128)(2,1)}, bf16[3,1024,256]{2,1,0:T(8,128)(2,1)S(1)}, u32[]{:S(2)}, u32[]{:S(2)}) collective-permute-start(bf16[3,1024,256]{2,1,0:T(8,128)(2,1)} %collective-permute-done.refs_6_), channel_id=1, source_target_pairs={{0,2},{1,3},{2,4},{3,5},{4,6},{5,7},{6,0},{7,1},{8,10},{9,11},{10,... | collective-permute-start | bytes 4718600 | tf_op jit(solution)/shard_map/ppermute | solution.py:595
  70.5 28.4 %collective-permute-start.7 = (bf16[512,1152]{1,0:T(8,128)(2,1)}, bf16[512,1152]{1,0:T(8,128)(2,1)S(1)}, u32[]{:S(2)}, u32[]{:S(2)}) collective-permute-start(bf16[512,1152]{1,0:T(8,128)(2,1)} %fusion.13.refs_1_), channel_id=1, source_target_pairs={{0,17},{1,16},{2,19},{3,18},{4,21},{5,20},{6,23},{7,22},{8,25},{9,... | collective-permute-start | bytes 3538952 | tf_op jit(solution)/shard_map/ppermute | solution.py:611
  98.9 23.6 %collective-permute-start.9 = (bf16[3,1024,256]{2,1,0:T(8,128)(2,1)S(1)}, bf16[3,1024,256]{2,1,0:T(8,128)(2,1)S(1)}, u32[]{:S(2)}, u32[]{:S(2)}) collective-permute-start(bf16[3,1024,256]{2,1,0:T(8,128)(2,1)S(1)} %collective-permute-done.8.refs_4_), channel_id=1, source_target_pairs={{0,8},{8,0},{16,24},{24,16},{1,9},{9,1},{17,25},{25,17},{2,10},{10... | collective-permute-start | bytes 4718600 | tf_op jit(solution)/shard_map/ppermute | solution.py:591
  99.0 26.8 %collective-permute-start.12 = (bf16[512,1024]{1,0:T(8,128)(2,1)}, bf16[512,1024]{1,0:T(8,128)(2,1)}, u32[]{:S(2)}, u32[]{:S(2)}) collective-permute-start(bf16[512,1024]{1,0:T(8,128)(2,1)} %multiply_convert_fusion.refs_0_), channel_id=1, source_target_pairs={{0,17},{1,16},{2,19},{3,18},{4,21},{5,20},{6,23},{7,22},{8,25},{9,... | collective-permute-start | bytes 3145736 | tf_op jit(solution)/shard_map/ppermute | solution.py:611
  100.5 45.9 %collective-permute-start.10 = (bf16[3,1024,256]{2,1,0:T(8,128)(2,1)S(1)}, bf16[3,1024,256]{2,1,0:T(8,128)(2,1)}, u32[]{:S(2)}, u32[]{:S(2)}) collective-permute-start(bf16[3,1024,256]{2,1,0:T(8,128)(2,1)S(1)} %collective-permute-done.8.refs_4_), channel_id=1, source_target_pairs={{0,2},{1,3},{2,4},{3,5},{4,6},{5,7},{6,0},{7,1},{8,10},{9,11},{10,... | collective-permute-start | bytes 4718600 | tf_op jit(solution)/shard_map/ppermute | solution.py:595
  146.3 29.0 %collective-permute-start.13 = (bf16[6,1024,256]{2,1,0:T(8,128)(2,1)}, bf16[6,1024,256]{2,1,0:T(8,128)(2,1)}, u32[]{:S(2)}, u32[]{:S(2)}) collective-permute-start(bf16[6,1024,256]{2,1,0:T(8,128)(2,1)} %get-tuple-element.220), channel_id=1, source_target_pairs={{0,8},{8,0},{16,24},{24,16},{1,9},{9,1},{17,25},{25,17},{2,10},{10... | collective-permute-start | bytes 9437192 | tf_op jit(solution)/shard_map/ppermute | solution.py:591
  178.2 48.1 %collective-permute-start.14 = (bf16[3,1024,256]{2,1,0:T(8,128)(2,1)}, bf16[3,1024,256]{2,1,0:T(8,128)(2,1)}, u32[]{:S(2)}, u32[]{:S(2)}) collective-permute-start(bf16[3,1024,256]{2,1,0:T(8,128)(2,1)} %add_convert_fusion.2), channel_id=1, source_target_pairs={{0,2},{1,3},{2,4},{3,5},{4,6},{5,7},{6,0},{7,1},{8,10},{9,11},{10,... | collective-permute-start | bytes 4718600 | tf_op jit(solution)/shard_map/ppermute | solution.py:595
  178.4 69.8 %collective-permute-start.18 = (bf16[512,1024]{1,0:T(8,128)(2,1)}, bf16[512,1024]{1,0:T(8,128)(2,1)}, u32[]{:S(2)}, u32[]{:S(2)}) collective-permute-start(bf16[512,1024]{1,0:T(8,128)(2,1)} %get-tuple-element.244), channel_id=1, source_target_pairs={{0,17},{1,16},{2,19},{3,18},{4,21},{5,20},{6,23},{7,22},{8,25},{9,... | collective-permute-start | bytes 3145736 | tf_op jit(solution)/shard_map/ppermute | solution.py:611
  224.2 25.3 %collective-permute-start.17 = (bf16[512,1024]{1,0:T(8,128)(2,1)}, bf16[512,1024]{1,0:T(8,128)(2,1)}, u32[]{:S(2)}, u32[]{:S(2)}) collective-permute-start(bf16[512,1024]{1,0:T(8,128)(2,1)} %get-tuple-element.243), channel_id=1, source_target_pairs={{0,16},{8,24},{16,0},{24,8},{1,17},{9,25},{17,1},{25,9},{2,18},{10... | collective-permute-start | bytes 3145736 | tf_op jit(solution)/shard_map/ppermute | solution.py:605
  224.8 25.0 %collective-permute-start.16 = (bf16[512,1024]{1,0:T(8,128)(2,1)}, bf16[512,1024]{1,0:T(8,128)(2,1)}, u32[]{:S(2)}, u32[]{:S(2)}) collective-permute-start(bf16[512,1024]{1,0:T(8,128)(2,1)} %get-tuple-element.242), channel_id=1, source_target_pairs={{0,1},{1,0},{2,3},{3,2},{4,5},{5,4},{6,7},{7,6},{8,9},{9,8},{10,11... | collective-permute-start | bytes 3145736 | tf_op jit(solution)/shard_map/ppermute | solution.py:602
  248.2 22.7 %collective-permute-start.15 = (bf16[6,1024,256]{2,1,0:T(8,128)(2,1)}, bf16[6,1024,256]{2,1,0:T(8,128)(2,1)S(1)}, u32[]{:S(2)}, u32[]{:S(2)}) collective-permute-start(bf16[6,1024,256]{2,1,0:T(8,128)(2,1)} %get-tuple-element.240), channel_id=1, source_target_pairs={{0,8},{8,0},{16,24},{24,16},{1,9},{9,1},{17,25},{25,17},{2,10},{10... | collective-permute-start | bytes 9437192 | tf_op jit(solution)/shard_map/ppermute | solution.py:591
  269.3 37.9 %collective-permute-start.22 = (bf16[8,80,1024]{2,1,0:T(8,128)(2,1)}, bf16[8,80,1024]{2,1,0:T(8,128)(2,1)}, u32[]{:S(2)}, u32[]{:S(2)}) collective-permute-start(bf16[8,80,1024]{2,1,0:T(8,128)(2,1)} %get-tuple-element.415), channel_id=1, source_target_pairs={{0,16},{1,17},{2,18},{3,19},{4,20},{5,21},{6,22},{7,23},{8,9},{9,8... | collective-permute-start | bytes 3932168 | tf_op jit(solution)/shard_map/ppermute | solution.py:652
  275.2 38.2 %collective-permute-start.19 = (bf16[3,1024,256]{2,1,0:T(8,128)(2,1)}, bf16[3,1024,256]{2,1,0:T(8,128)(2,1)}, u32[]{:S(2)}, u32[]{:S(2)}) collective-permute-start(bf16[3,1024,256]{2,1,0:T(8,128)(2,1)} %add_convert_fusion.1), channel_id=1, source_target_pairs={{0,2},{1,3},{2,4},{3,5},{4,6},{5,7},{6,0},{7,1},{8,10},{9,11},{10,... | collective-permute-start | bytes 4718600 | tf_op jit(solution)/shard_map/ppermute | solution.py:595
  276.2 39.3 %collective-permute-start.20 = (bf16[512,1024]{1,0:T(8,128)(2,1)}, bf16[512,1024]{1,0:T(8,128)(2,1)S(1)}, u32[]{:S(2)}, u32[]{:S(2)}) collective-permute-start(bf16[512,1024]{1,0:T(8,128)(2,1)} %get-tuple-element.250), channel_id=1, source_target_pairs={{0,17},{1,16},{2,19},{3,18},{4,21},{5,20},{6,23},{7,22},{8,25},{9,... | collective-permute-start | bytes 3145736 | tf_op jit(solution)/shard_map/ppermute | solution.py:611
  326.7 20.1 %collective-permute-start.24 = (bf16[8,32,2560]{2,1,0:T(8,128)(2,1)S(1)}, bf16[8,32,2560]{2,1,0:T(8,128)(2,1)S(1)}, u32[]{:S(2)}, u32[]{:S(2)}) collective-permute-start(bf16[8,32,2560]{2,1,0:T(8,128)(2,1)S(1)} %get-tuple-element.268), channel_id=1, source_target_pairs={{0,16},{1,17},{2,18},{3,19},{4,20},{5,21},{6,22},{7,23},{8,9},{9,8... | collective-permute-start | bytes 3932168 | tf_op jit(solution)/shard_map/ppermute | solution.py:652
  402.4 28.6 %collective-permute-start.46 = (bf16[8,80,1024]{2,1,0:T(8,128)(2,1)S(1)}, bf16[8,80,1024]{2,1,0:T(8,128)(2,1)S(1)}, u32[]{:S(2)}, u32[]{:S(2)}) collective-permute-start(bf16[8,80,1024]{2,1,0:T(8,128)(2,1)S(1)} %pad_maximum_fusion.2.refs_0_), channel_id=1, source_target_pairs={{0,16},{1,17},{2,18},{3,19},{4,20},{5,21},{6,22},{7,23},{8,9},{9,8... | collective-permute-start | bytes 3932168 | tf_op jit(solution)/shard_map/ppermute | solution.py:652
  406.7 17.6 %collective-permute-start.33 = (bf16[4,32,2560]{2,1,0:T(8,128)(2,1)S(1)}, bf16[4,32,2560]{2,1,0:T(8,128)(2,1)S(1)}, u32[]{:S(2)}, u32[]{:S(2)}) collective-permute-start(bf16[4,32,2560]{2,1,0:T(8,128)(2,1)S(1)} %pad_maximum_fusion.3), channel_id=1, source_target_pairs={{0,1},{1,0},{2,3},{3,2},{4,5},{5,4},{6,7},{7,6},{8,24},{9,25},{10,... | collective-permute-start | bytes 1966088 | tf_op jit(solution)/shard_map/ppermute | solution.py:652
  417.7 41.3 %collective-permute-start.55 = (bf16[3,1024,256]{2,1,0:T(8,128)(2,1)S(1)}, bf16[3,1024,256]{2,1,0:T(8,128)(2,1)S(1)}, u32[]{:S(2)}, u32[]{:S(2)}) collective-permute-start(bf16[3,1024,256]{2,1,0:T(8,128)(2,1)S(1)} %add_convert_fusion), channel_id=1, source_target_pairs={{0,2},{1,3},{2,4},{3,5},{4,6},{5,7},{6,0},{7,1},{8,10},{9,11},{10,... | collective-permute-start | bytes 4718600 | tf_op jit(solution)/shard_map/ppermute | solution.py:595
  424.4 34.5 %collective-permute-start.34 = (bf16[8,32,2560]{2,1,0:T(8,128)(2,1)S(1)}, bf16[8,32,2560]{2,1,0:T(8,128)(2,1)S(1)}, u32[]{:S(2)}, u32[]{:S(2)}) collective-permute-start(bf16[8,32,2560]{2,1,0:T(8,128)(2,1)S(1)} %pad_maximum_fusion.1.refs_0_), channel_id=1, source_target_pairs={{0,16},{1,17},{2,18},{3,19},{4,20},{5,21},{6,22},{7,23},{8,9},{9,8... | collective-permute-start | bytes 3932168 | tf_op jit(solution)/shard_map/ppermute | solution.py:652
  431.0 21.8 %collective-permute-start.49 = (bf16[8,80,1024]{2,1,0:T(8,128)(2,1)S(1)}, bf16[8,80,1024]{2,1,0:T(8,128)(2,1)S(1)}, u32[]{:S(2)}, u32[]{:S(2)}) collective-permute-start(bf16[8,80,1024]{2,1,0:T(8,128)(2,1)S(1)} %pad_maximum_fusion.2.refs_0_), channel_id=1, source_target_pairs={{0,8},{8,0},{16,24},{24,16},{1,9},{9,1},{17,25},{25,17},{2,10},{10... | collective-permute-start | bytes 3932168 | tf_op jit(solution)/shard_map/ppermute | solution.py:591
  431.0 22.3 %collective-permute-start.50 = (bf16[8,80,1024]{2,1,0:T(8,128)(2,1)S(1)}, bf16[8,80,1024]{2,1,0:T(8,128)(2,1)S(1)}, u32[]{:S(2)}, u32[]{:S(2)}) collective-permute-start(bf16[8,80,1024]{2,1,0:T(8,128)(2,1)S(1)} %collective-permute-done.46.refs_1_), channel_id=1, source_target_pairs={{0,8},{8,0},{16,24},{24,16},{1,9},{9,1},{17,25},{25,17},{2,10},{10... | collective-permute-start | bytes 3932168 | tf_op jit(solution)/shard_map/ppermute | solution.py:591
  432.1 20.7 %collective-permute-start.59 = (bf16[8,32,1408]{2,1,0:T(8,128)(2,1)S(1)}, bf16[8,32,1408]{2,1,0:T(8,128)(2,1)S(1)}, u32[]{:S(2)}, u32[]{:S(2)}) collective-permute-start(bf16[8,32,1408]{2,1,0:T(8,128)(2,1)S(1)} %constant_dynamic-update-slice_fusion.refs_0_), channel_id=1, source_target_pairs={{0,16},{1,17},{2,18},{3,19},{4,20},{5,21},{6,22},{7,23},{8,9},{9,8... | collective-permute-start | bytes 2162696 | tf_op jit(solution)/shard_map/ppermute | solution.py:652
  459.0 17.8 %collective-permute-start.56 = (bf16[8,32,2560]{2,1,0:T(8,128)(2,1)S(1)}, bf16[8,32,2560]{2,1,0:T(8,128)(2,1)}, u32[]{:S(2)}, u32[]{:S(2)}) collective-permute-start(bf16[8,32,2560]{2,1,0:T(8,128)(2,1)S(1)} %pad_maximum_fusion.1.refs_0_), channel_id=1, source_target_pairs={{0,8},{8,0},{16,24},{24,16},{1,9},{9,1},{17,25},{25,17},{2,10},{10... | collective-permute-start | bytes 3932168 | tf_op jit(solution)/shard_map/ppermute | solution.py:591
  459.0 17.8 %collective-permute-start.57 = (bf16[8,32,2560]{2,1,0:T(8,128)(2,1)S(1)}, bf16[8,32,2560]{2,1,0:T(8,128)(2,1)}, u32[]{:S(2)}, u32[]{:S(2)}) collective-permute-start(bf16[8,32,2560]{2,1,0:T(8,128)(2,1)S(1)} %collective-permute-done.34.refs_1_), channel_id=1, source_target_pairs={{0,8},{8,0},{16,24},{24,16},{1,9},{9,1},{17,25},{25,17},{2,10},{10... | collective-permute-start | bytes 3932168 | tf_op jit(solution)/shard_map/ppermute | solution.py:591
  461.5 25.5 %collective-permute-start.51 = (bf16[512,1024]{1,0:T(8,128)(2,1)}, bf16[512,1024]{1,0:T(8,128)(2,1)}, u32[]{:S(2)}, u32[]{:S(2)}) collective-permute-start(bf16[512,1024]{1,0:T(8,128)(2,1)} %get-tuple-element.324), channel_id=1, source_target_pairs={{0,1},{1,0},{2,3},{3,2},{4,5},{5,4},{6,7},{7,6},{8,9},{9,8},{10,11... | collective-permute-start | bytes 3145736 | tf_op jit(solution)/shard_map/ppermute | solution.py:602
  462.4 25.2 %collective-permute-start.52 = (bf16[512,1024]{1,0:T(8,128)(2,1)}, bf16[512,1024]{1,0:T(8,128)(2,1)}, u32[]{:S(2)}, u32[]{:S(2)}) collective-permute-start(bf16[512,1024]{1,0:T(8,128)(2,1)} %get-tuple-element.327), channel_id=1, source_target_pairs={{0,16},{8,24},{16,0},{24,8},{1,17},{9,25},{17,1},{25,9},{2,18},{10... | collective-permute-start | bytes 3145736 | tf_op jit(solution)/shard_map/ppermute | solution.py:605
  (96 other events, 811.5 us)
